TPU v7x, 32 devices: a whole 2x2x4 slice. The times are simulated.
32 devices in a mesh: groups: 2 (over x), blocks: 16 (over z, y, core).
Axes of the slice: x: 2, y: 2, z: 4, core: 2. Of those that a mesh axis runs over, the one named last changes fastest.
Arguments:
- activations: float32 [2048, 2048], P('blocks', 'groups'), parts along dimension 1, may hold values from -180 to 180
- cotangent: float32 [2048, 2048], P('blocks', 'groups'), parts along dimension 1, may hold values from -6 to 6
- gain: float32 [2048], P('blocks'), may hold values from 0.5 to 1.5
- left_one: float32 [16, 128, 128], P('blocks'), may hold values from -0.5 to 0.5
- right_one: float32 [128, 16, 16], P('blocks'), may hold values from -1.5 to 1.5
- left_two: float32 [16, 128, 128], P('blocks'), may hold values from -0.5 to 0.5
- right_two: float32 [128, 16, 16], P('blocks'), may hold values from -1.5 to 1.5
Outputs:
- output: float32 [2048, 2048], P('blocks', 'groups'), parts along dimension 1
- input_gradient: float32 [2048, 2048], P('blocks', 'groups'), parts along dimension 1
- gain_gradient: float32 [4096], P(('groups', 'blocks')), parts along dimension 0
- grad_left_one: float32 [32, 128, 128], P(('groups', 'blocks')), parts along dimension 0
- grad_right_one: float32 [256, 16, 16], P(('groups', 'blocks')), parts along dimension 0
- grad_left_two: float32 [32, 128, 128], P(('groups', 'blocks')), parts along dimension 0
- grad_right_two: float32 [256, 16, 16], P(('groups', 'blocks')), parts along dimension 0
There are 2 independent parts, one for each index of `groups`. A program takes and returns all parts, laid end to end along the dimension named above; an argument that names none is the same for every part. Nothing has to cross between parts.
All inputs are finite; a program needn't handle non-finite values.
Results may differ from a plain program's by a relative error of at most 0.0001.
Values sent between devices are 32-bit elements; how exact they have to be, the bound alone decides.
No kernel may reach another device: no remote copies, remote signals or barrier semaphores. Data moves between devices by JAX's collectives and lax.ppermute only.
A program may use at most 64 MiB of HBM per device.

v0:
```python
import functools
import math

import jax
import jax.numpy as jnp
from jax import lax
from jax.experimental import pallas as pl
from jax.experimental.pallas import tpu as pltpu
from jax.sharding import PartitionSpec as P


COEFF = math.sqrt(2.0 / math.pi)
CUBIC = 0.044715
EPSILON = 1e-05
HIGH = lax.Precision.HIGHEST
SUB = 8
LANE = 128
KERNEL_VMEM = 16 << 20
LOADING_VMEM = 60 << 20


def gelu_value(values):
    return 0.5 * values * (1.0 + jnp.tanh(COEFF * (values + CUBIC * values * values * values)))


def gelu_slope(values):
    tangent = jnp.tanh(COEFF * (values + CUBIC * values * values * values))
    return 0.5 * (1.0 + tangent) + 0.5 * values * (1.0 - tangent * tangent) * COEFF * (
        1.0 + 3.0 * CUBIC * values * values
    )


def monarch_forward(stacked, left, right):
    first = jnp.einsum("bij,bit->bjt", left, stacked, precision=HIGH)
    regrouped = lax.all_to_all(first, "blocks", split_axis=1, concat_axis=0, tiled=True)
    second = jnp.einsum("jbk,bjt->jkt", right, regrouped, precision=HIGH)
    return (second, regrouped)


def monarch_backward(grad_out, stacked, left, right, regrouped, factor_matrix):
    grad_right = jnp.einsum("bjt,jkt->jbk", regrouped, grad_out, precision=HIGH) * factor_matrix
    grad_mid = jnp.einsum("jbk,jkt->bjt", right, grad_out, precision=HIGH)
    piece = lax.all_to_all(grad_mid, "blocks", split_axis=0, concat_axis=1, tiled=True)
    grad_stacked = jnp.einsum("bij,bjt->bit", left, piece, precision=HIGH)
    grad_left = jnp.einsum("bit,bjt->bij", stacked, piece, precision=HIGH) * factor_matrix
    return (grad_stacked, grad_left, grad_right)


def local_plain(activations, cotangent, gain, left_one, right_one, left_two, right_two):
    features, tokens = activations.shape
    blocks_here, block_order = left_one.shape[:2]
    outer_here, block_count = right_one.shape[:2]
    feature_width = features * lax.axis_size("blocks")
    factor_matrix = tokens ** (-0.5)
    squares = lax.psum(jnp.sum(activations * activations, axis=0), "blocks")
    inverse_root = lax.rsqrt(squares / feature_width + EPSILON)[None, :]
    centered_input = activations * inverse_root
    normed_rows = centered_input * gain[:, None]
    normed_stacked = normed_rows.reshape(blocks_here, block_order, tokens)
    second_one, regrouped_one = monarch_forward(normed_stacked, left_one, right_one)
    pre = second_one.reshape(features, tokens)
    acted_stacked = gelu_value(pre).reshape(blocks_here, block_order, tokens)
    second_two, regrouped_two = monarch_forward(acted_stacked, left_two, right_two)
    output = activations + second_two.reshape(features, tokens)
    grad_acted, grad_left_two, grad_right_two = monarch_backward(
        cotangent.reshape(outer_here, block_count, tokens),
        acted_stacked, left_two, right_two, regrouped_two, factor_matrix,
    )
    grad_pre = grad_acted.reshape(features, tokens) * gelu_slope(pre)
    inner = lax.psum(jnp.sum(grad_pre * pre, axis=0), "blocks")
    normalized_gradient, grad_left_one, grad_right_one = monarch_backward(
        grad_pre.reshape(outer_here, block_count, tokens),
        normed_stacked, left_one, right_one, regrouped_one, factor_matrix,
    )
    normalized_gradient = normalized_gradient.reshape(features, tokens)
    input_gradient = cotangent + inverse_root * (
        gain[:, None] * normalized_gradient - centered_input * (inner / feature_width)[None, :]
    )
    gain_gradient = jnp.sum(normalized_gradient * centered_input, axis=1) * factor_matrix
    return (output, input_gradient, gain_gradient, grad_left_one, grad_right_one, grad_left_two, grad_right_two)


def parts_of(values, count=2):
    parts = []
    for _ in range(count):
        parts.append(values.astype(jnp.bfloat16))
        values = values - parts[-1].astype(jnp.float32)
    return parts


def dot(a, b, dim_b):
    return lax.dot_general(a, b, (((1,), (dim_b,)), ((), ())), preferred_element_type=jnp.float32)


def matmul(a, b):
    (a_high, a_low), (b_high, b_low) = parts_of(a), parts_of(b)
    return dot(jnp.concatenate([a_high, a_high, a_low], axis=1), jnp.concatenate([b_high, b_low, b_high], axis=0), 0)


def matmul_nt(a, b):
    (a_high, a_low), (b_high, b_low) = parts_of(a), parts_of(b)
    both = dot(a_high, jnp.concatenate([b_high, b_low], axis=0), 1)
    return both[:, : b.shape[0]] + both[:, b.shape[0] :] + dot(a_low, b_high, 1)


def pick_rows(chosen, values):
    ones = chosen.astype(jnp.bfloat16)
    return sum(dot(ones, part, 0) for part in reversed(parts_of(values, 3)))


def pick_columns(values, chosen):
    ones = chosen.astype(jnp.bfloat16)
    return sum(dot(part, ones, 0) for part in reversed(parts_of(values, 3)))


def iota(shape, dim):
    return lax.broadcasted_iota(jnp.int32, shape, dim)


def stages(count):
    inner = 1 << (count.bit_length() // 2)
    return inner, count // inner


def send_order(count):
    return [*range(count // 2, count), *range(1, count // 2)]


def early_keys(count):
    keys = [0, *send_order(count)]
    return keys[: count // 2], keys[count // 2 :]


class Plan:
    def __init__(self, count, features, tokens):
        self.count, self.features, self.tokens = count, features, tokens
        self.inner, self.outer = stages(count)
        self.early, self.late = early_keys(self.outer)
        self.far, self.near = range(self.outer // 2, self.outer), range(self.outer // 2)
        self.rows = features // count
        self.chunks = tokens // LANE
        self.block_tiles = self.rows // SUB * self.chunks
        self.sum_tiles = self.chunks // SUB
        self.factor = tokens ** (-0.5)
        self.width = features * count

    def fits(self):
        whole = self.count & (self.count - 1) == 0 and self.count > 2
        return whole and self.rows % SUB == 0 and self.rows > 0 and self.tokens % (SUB * LANE) == 0

    def message(self, blocks, sums):
        return jax.ShapeDtypeStruct((blocks * self.block_tiles + (self.sum_tiles if sums else 0), SUB, LANE), jnp.float32)

    def tiles(self):
        for r in range(self.rows // SUB):
            for c in range(self.chunks):
                yield r * self.chunks + c, r * SUB, c * LANE

    def put_block(self, source, block, message, slot):
        start = pl.multiple_of(block * self.rows, SUB)
        for i, r, c in self.tiles():
            message[slot * self.block_tiles + i] = source[pl.ds(start + r, SUB), c : c + LANE]

    def take_block(self, message, slot, target, block, scale=None):
        start = pl.multiple_of(block * self.rows, SUB)
        for i, r, c in self.tiles():
            tile = message[slot * self.block_tiles + i]
            target[pl.ds(start + r, SUB), c : c + LANE] = tile if scale is None else tile * scale[:, c : c + LANE]

    def move_block(self, message, slot, target, place):
        size = self.block_tiles
        target[place * size : (place + 1) * size] = message[slot * size : (slot + 1) * size]

    def put_sums(self, row, message, blocks):
        for s in range(self.sum_tiles):
            pieces = [row[:, (s * SUB + c) * LANE : (s * SUB + c + 1) * LANE] for c in range(SUB)]
            message[blocks * self.block_tiles + s] = jnp.concatenate(pieces, axis=0)

    def has_sums(self, message):
        return message.shape[0] % self.block_tiles != 0

    def add_sums(self, messages):
        return sum(message[message.shape[0] - self.sum_tiles :] for message in messages if self.has_sums(message))

    def sums_row(self, tiles):
        return jnp.concatenate([tiles[c // SUB, c % SUB : c % SUB + 1, :] for c in range(self.chunks)], axis=1)

    def call(self, kernel, outs, me, *args, scratch=(), flops=0, loads=False, stores=0, **fixed):
        outs = tuple(o if isinstance(o, jax.ShapeDtypeStruct) else jax.ShapeDtypeStruct(o, jnp.float32) for o in outs)
        moved = 4 * sum(math.prod(a.shape) for a in (*args, *outs))
        vmem = pl.BlockSpec(memory_space=pltpu.VMEM)
        return pl.pallas_call(
            functools.partial(kernel, self, len(args), len(outs), **fixed),
            out_shape=outs,
            in_specs=[pl.BlockSpec(memory_space=pltpu.SMEM)]
            + [pl.BlockSpec(memory_space=pltpu.HBM) if loads else vmem] * len(args),
            out_specs=(pl.BlockSpec(memory_space=pl.ANY),) * stores + (vmem,) * (len(outs) - stores),
            scratch_shapes=[pltpu.VMEM(s, jnp.float32) for s in scratch]
            + ([pltpu.VMEM(a.shape, a.dtype) for a in args] + [pltpu.SemaphoreType.DMA((len(args),))] if loads else [])
            + ([pltpu.SemaphoreType.DMA((stores,))] if stores else []),
            cost_estimate=pl.CostEstimate(flops=flops, bytes_accessed=moved, transcendentals=0),
            compiler_params=pltpu.CompilerParams(vmem_limit_bytes=LOADING_VMEM if loads else KERNEL_VMEM),
        )(me, *args)


def split_refs(n_in, n_out, refs):
    return refs[0], refs[1 : 1 + n_in], refs[1 + n_in : 1 + n_in + n_out], refs[1 + n_in + n_out :]


def first_one(plan, n_in, n_out, *refs):
    me, sources, outs, (held, x, left, gain, arrived) = split_refs(n_in, n_out, refs)
    z, p = me[0] // plan.inner, me[0] % plan.inner
    loads = [pltpu.make_async_copy(s, t, arrived.at[i]) for i, (s, t) in enumerate(zip(sources, (x, left, gain)))]
    for load in loads:
        load.start()
    for load in loads:
        load.wait()
    values = x[...]
    held[...] = matmul(left[...].T * gain[...], values)
    squares = jnp.sum(values * values, axis=0, keepdims=True)
    for k in range(plan.outer):
        for m in range(plan.inner):
            plan.put_block(held, (z ^ k) * plan.inner + (p ^ m), outs[k], m)
        plan.put_sums(squares, outs[k], plan.inner)


def widen(plan, right):
    rows, count, full = plan.rows, plan.count, plan.features
    spread = (iota((count, full), 1) % count == iota((count, full), 0)).astype(jnp.float32)
    same = iota((full, full), 0) // count == iota((full, full), 1) // count
    tall = jnp.where(same, pick_columns(right, spread), 0.0)
    i, o = iota((full, full), 1), iota((full, full), 0)
    swap = (i == (o % rows) * count + o // rows).astype(jnp.float32)
    return pick_rows(swap, tall)


def narrow(plan, product):
    rows, count, full = plan.rows, plan.count, plan.features
    same = iota((full, full), 0) % rows == iota((full, full), 1) // count
    kept = jnp.where(same, product, 0.0)
    o, i = iota((full, full), 0), iota((full, full), 1)
    swap = (i == (o % count) * rows + o // count).astype(jnp.float32)
    gather = (iota((full, count), 0) % count == iota((full, count), 1)).astype(jnp.float32)
    return pick_columns(pick_rows(swap, kept), gather)


def back_two(plan, n_in, n_out, *refs):
    me, (cotangent, right_two), outs, (held,) = split_refs(n_in, n_out, refs)
    z, p = me[0] // plan.inner, me[0] % plan.inner
    wide_two = widen(plan, right_two[...])
    held[...] = matmul(wide_two, cotangent[...])
    for m in range(plan.inner):
        for k in range(plan.outer):
            plan.put_block(held, (z ^ k) * plan.inner + (p ^ m), outs[m], k)
    outs[-1][...] = wide_two


def widen_one(plan, n_in, n_out, *refs):
    _, (right, left, gain), (wide, turned, scaled, gain_kept), _ = split_refs(n_in, n_out, refs)
    wide[...] = widen(plan, right[...])
    turned[...] = left[...].T
    scaled[...] = (left[...].T * gain[...]).T
    gain_kept[...] = gain[...]


def regroup(plan, n_in, n_out, *refs, data):
    _, ins, outs, _ = split_refs(n_in, n_out, refs)
    sums = plan.has_sums(outs[0])
    total = plan.add_sums(ins) if sums else None
    for o in range(n_out):
        for i in range(data):
            plan.move_block(ins[i], o, outs[o], i)
        if sums:
            outs[o][data * plan.block_tiles :] = total


def middle(plan, n_in, n_out, *refs):
    me, ins, outs, (y1, held) = split_refs(n_in, n_out, refs)
    z, p = me[0] // plan.inner, me[0] % plan.inner
    parts, (wide_one, left_two) = ins[: 2 * plan.inner], ins[2 * plan.inner :]
    squares = plan.add_sums(parts)
    inverse_root = plan.sums_row(lax.rsqrt(squares / plan.width + EPSILON))
    for m in range(plan.inner):
        for message, keys in ((parts[m], plan.early), (parts[plan.inner + m], plan.late)):
            for slot, k in enumerate(keys):
                plan.take_block(message, slot, y1, (z ^ k) * plan.inner + (p ^ m), inverse_root)
    first = y1[...]
    pre = matmul(wide_one[...].T, first)
    tangent = jnp.tanh(COEFF * (pre + CUBIC * pre * pre * pre))
    half = 0.5 * (1.0 + tangent)
    act = half * pre
    slope = half + 0.5 * pre * (1.0 - tangent * tangent) * COEFF * (1.0 + 3.0 * CUBIC * pre * pre)
    held[...] = matmul(left_two[...].T, act)
    for k in range(plan.outer):
        for m in range(plan.inner):
            plan.put_block(held, (z ^ k) * plan.inner + (p ^ m), outs[k], m)
    for ref, value in zip(outs[plan.outer :], (first, pre, act, slope, inverse_root)):
        ref[...] = value


def back_one(plan, n_in, n_out, *refs):
    me, ins, outs, (dy2, held) = split_refs(n_in, n_out, refs)
    z, p = me[0] // plan.inner, me[0] % plan.inner
    parts, (left_two, wide_one, pre, slope) = ins[: plan.outer], ins[plan.outer :]
    for k in range(plan.outer):
        for m in range(plan.inner):
            plan.take_block(parts[k], m, dy2, (z ^ k) * plan.inner + (p ^ m))
    back = dy2[...]
    dpre = matmul(left_two[...], back) * slope[...]
    inner = jnp.sum(dpre * pre[...], axis=0, keepdims=True)
    held[...] = matmul(wide_one[...], dpre)
    for m in range(plan.inner):
        for message, keys in ((outs[m], plan.far), (outs[plan.inner + m], plan.near)):
            for slot, k in enumerate(keys):
                plan.put_block(held, (z ^ k) * plan.inner + (p ^ m), message, slot)
        plan.put_sums(inner, outs[m], len(plan.far))
    outs[-2][...] = back
    outs[-1][...] = dpre


def grads_middle(plan, n_in, n_out, *refs):
    _, (y1, dpre, act, dy2), (grad_right_one, grad_left_two), _ = split_refs(n_in, n_out, refs)
    grad_right_one[...] = narrow(plan, matmul_nt(y1[...], dpre[...])) * plan.factor
    grad_left_two[...] = matmul_nt(act[...], dy2[...]) * plan.factor


def finish_output(plan, n_in, n_out, *refs):
    me, ins, (output, grad_right_two), (y2,) = split_refs(n_in, n_out, refs)
    z, p = me[0] // plan.inner, me[0] % plan.inner
    parts, (x, cotangent, wide_two) = ins[: plan.inner], ins[plan.inner :]
    for m in range(plan.inner):
        for k in range(plan.outer):
            plan.take_block(parts[m], k, y2, (z ^ k) * plan.inner + (p ^ m))
    second = y2[...]
    output[...] = x[...] + matmul(wide_two[...].T, second)
    grad_right_two[...] = narrow(plan, matmul_nt(second, cotangent[...])) * plan.factor


def finish_input(plan, n_in, n_out, *refs):
    me, ins, (input_gradient, gain_gradient, grad_left_one), (dy1, result, done) = split_refs(n_in, n_out, refs)
    z, p = me[0] // plan.inner, me[0] % plan.inner
    parts, (x, cotangent, gain, turned, scaled, inverse_root) = ins[: plan.outer], ins[plan.outer :]
    inner = plan.sums_row(plan.add_sums(parts)) / plan.width
    for k in range(plan.outer):
        for m in range(plan.inner):
            plan.take_block(parts[k], m, dy1, (z ^ k) * plan.inner + (p ^ m))
    back = dy1[...]
    root = inverse_root[...]
    xhat = x[...] * root
    result[...] = cotangent[...] + root * (matmul(scaled[...], back) - xhat * inner)
    store = pltpu.make_async_copy(result, input_gradient, done.at[0])
    store.start()
    product = matmul_nt(back, xhat)
    gain_gradient[...] = jnp.sum(turned[...] * product, axis=0, keepdims=True) * plan.factor
    grad_left_one[...] = (product * gain[...] * plan.factor).T
    store.wait()


def local_tiled(plan, activations, cotangent, gain, left_one, right_one, left_two, right_two):
    features, tokens, count = plan.features, plan.tokens, plan.count
    inner, outer = plan.inner, plan.outer
    me = lax.axis_index("blocks").astype(jnp.int32).reshape(1)
    full, square = (features, tokens), (features, features)
    cost = 12 * features * features * tokens

    def across(messages, step):
        moved = dict(messages)
        for i in messages:
            if i:
                moved[i] = lax.ppermute(messages[i], "blocks", [(s, s ^ (i * step)) for s in range(count)])
        return moved

    def over_outer(keys, messages):
        return across(dict(zip(keys, messages, strict=True)), inner)

    def over_inner(messages):
        return [*across(dict(enumerate(messages)), 1).values()]

    def call(kernel, outs, *args, **options):
        return plan.call(kernel, outs, me, *args, **options)

    gain_row = gain.reshape(1, features)
    one, two = left_one.reshape(square), left_two.reshape(square)
    flat_one, flat_two = right_one.reshape(features, count), right_two.reshape(features, count)

    message, line = plan.message, range(outer)
    early, late, far, near = plan.early, plan.late, plan.far, plan.near

    sent = call(
        first_one, [message(inner, True)] * outer, activations, one, gain_row, scratch=[full], flops=cost, loads=True
    )
    first = over_outer(line, sent)
    *sent, wide_two = call(
        back_two, [message(outer, False)] * inner + [square], cotangent, flat_two, scratch=[full], flops=cost
    )
    dy2_half = over_inner(sent)
    wide_one, turned_one, scaled_one, gain_kept = call(
        widen_one, [square] * 3 + [(1, features)], flat_one, one, gain_row, flops=cost // 8
    )
    sent = call(regroup, [message(len(early), False)] * inner, *(first[k] for k in early), data=len(early))
    first_early = over_inner(sent)
    sent = call(regroup, [message(inner, False)] * outer, *dy2_half, data=inner)
    dy2_parts = over_outer(line, sent)
    sent = call(regroup, [message(len(late), True)] * inner, *(first[k] for k in (*late, *early)), data=len(late))
    first_late = over_inner(sent)
    *sent, y1, pre, act, slope, inverse_root = call(
        middle, [message(inner, False)] * outer + [full] * 4 + [(1, tokens)], *first_early, *first_late, wide_one, two,
        scratch=[full] * 2, flops=2 * cost,
    )
    second_half = over_outer(line, sent)
    *sent, dy2, dpre = call(
        back_one, [message(len(far), True)] * inner + [message(len(near), False)] * inner + [full] * 2,
        *(dy2_parts[k] for k in line), two, wide_one, pre, slope, scratch=[full] * 2, flops=2 * cost,
    )
    dy1_far, dy1_near = over_inner(sent[:inner]), over_inner(sent[inner:])
    sent = call(regroup, [message(inner, True)] * len(far), *dy1_far, data=inner)
    dy1_parts = over_outer(far, sent)
    sent = call(regroup, [message(inner, True)] * len(near), *dy1_near, *dy1_far, data=inner)
    dy1_parts |= over_outer(near, sent)
    sent = call(regroup, [message(outer, False)] * inner, *(second_half[k] for k in line), data=outer)
    second_parts = over_inner(sent)
    grad_right_one, grad_left_two = call(grads_middle, [(features, count), square], y1, dpre, act, dy2, flops=2 * cost)
    output, grad_right_two = call(
        finish_output, [full, (features, count)], *second_parts, activations, cotangent, wide_two,
        scratch=[full], flops=2 * cost,
    )
    input_gradient, gain_gradient, grad_left_one = call(
        finish_input, [full, (1, features), square], *(dy1_parts[k] for k in line), activations, cotangent,
        gain_kept, turned_one, scaled_one, inverse_root, scratch=[full] * 2, flops=2 * cost, stores=1,
    )
    return (
        output,
        input_gradient,
        gain_gradient.reshape(features),
        grad_left_one.reshape(left_one.shape),
        grad_right_one.reshape(right_one.shape),
        grad_left_two.reshape(left_two.shape),
        grad_right_two.reshape(right_two.shape),
    )


def local(activations, *rest):
    plan = Plan(lax.axis_size("blocks"), *activations.shape)
    if plan.fits() and rest[2].shape[0] == 1:
        return local_tiled(plan, activations, *rest)
    return local_plain(activations, *rest)


def solution(mesh):
    split = P("blocks", "groups")
    kept, laid = P("blocks", None, None), P(("groups", "blocks"), None, None)
    return jax.shard_map(
        local,
        mesh=mesh,
        in_specs=(split, split, P("blocks"), kept, kept, kept, kept),
        out_specs=(split, split, P(("groups", "blocks")), laid, laid, laid, laid),
        check_vma=False,
    )
```

profile of v0, /device:TPU:0, one launch (start us, length us, event | category | flops | bytes accessed | tf_op | source)
XLA Modules:
  0.0 76.5 jit_solution(16517670737899653947)
XLA Ops:
  0.7 2.3 %shard_map.126 = (f32[33,8,128]{2,1,0:T(8,128)}, f32[33,8,128]{2,1,0:T(8,128)}, f32[33,8,128]{2,1,0:T(8,128)}, f32[33,8,128]{2,1,0:T(8,128)}) custom-call(s32[1]{0:T(128)} %bitcast.refs_0_, f32[128,1024]{1,0:T(8,128)} %refs_5_.3, f32[128,128]{1,0:T(8,128)} %bitcast.13, f32[1,128]{1,0:T(1,128)} %bitcast.16), custom_call_target="tpu_custom_call" | custom-call | flops 201326592 | bytes 1131008 | tf_op jit(solution)/shard_map/pallas_call | solution.py:192
  2.9 4.1 %collective-permute-start = (f32[33,8,128]{2,1,0:T(8,128)}, f32[33,8,128]{2,1,0:T(8,128)S(1)}, u32[]{:S(2)}, u32[]{:S(2)}) collective-permute-start(f32[33,8,128]{2,1,0:T(8,128)} %get-tuple-element.67), channel_id=1, source_target_pairs={{0,8},{1,9},{2,10},{3,11},{4,12},{5,13},{6,14},{7,15},{8,0},{9,1},... | collective-permute-start | bytes 405512 | tf_op jit(solution)/shard_map/ppermute | solution.py:370
  7.1 0.0 copy-start.2
  7.1 0.6 shard_map.132
  7.8 0.1 collective-permute-start.15
  7.8 1.6 %collective-permute-start.16 = (f32[32,8,128]{2,1,0:T(8,128)S(1)}, f32[32,8,128]{2,1,0:T(8,128)S(1)}, u32[]{:S(2)}, u32[]{:S(2)}) collective-permute-start(f32[32,8,128]{2,1,0:T(8,128)S(1)} %get-tuple-element.91), channel_id=1, source_target_pairs={{0,2},{1,3},{2,0},{3,1},{4,6},{5,7},{6,4},{7,5},{8,10},{9,11},{10,... | collective-permute-start | bytes 393224 | tf_op jit(solution)/shard_map/ppermute | solution.py:370
  9.4 0.2 collective-permute-start.17
  9.7 1.4 %collective-permute-start.4 = (f32[33,8,128]{2,1,0:T(8,128)S(1)}, f32[33,8,128]{2,1,0:T(8,128)S(1)}, u32[]{:S(2)}, u32[]{:S(2)}) collective-permute-start(f32[33,8,128]{2,1,0:T(8,128)S(1)} %copy-done.9), channel_id=1, source_target_pairs={{0,12},{1,13},{2,14},{3,15},{4,8},{5,9},{6,10},{7,11},{8,4},{9,5},... | collective-permute-start | bytes 405512 | tf_op jit(solution)/shard_map/ppermute | solution.py:370
  11.0 2.8 %collective-permute-done.refs_2_.refs_4_ = f32[33,8,128]{2,1,0:T(8,128)S(1)} collective-permute-done((f32[33,8,128]{2,1,0:T(8,128)}, f32[33,8,128]{2,1,0:T(8,128)S(1)}, u32[]{:S(2)}, u32[]{:S(2)}) %collective-permute-start) | collective-permute-done | bytes 135200 | tf_op jit(solution)/shard_map/ppermute | solution.py:370
  13.9 3.7 %collective-permute-start.5 = (f32[33,8,128]{2,1,0:T(8,128)S(1)}, f32[33,8,128]{2,1,0:T(8,128)S(1)}, u32[]{:S(2)}, u32[]{:S(2)}) collective-permute-start(f32[33,8,128]{2,1,0:T(8,128)S(1)} %copy-done.8), channel_id=1, source_target_pairs={{0,4},{1,5},{2,6},{3,7},{4,0},{5,1},{6,2},{7,3},{8,12},{9,13},{10,... | collective-permute-start | bytes 405512 | tf_op jit(solution)/shard_map/ppermute | solution.py:370
  17.6 0.0 collective-permute-done.15.refs_2_
  17.6 0.1 collective-permute-start.1
  17.7 0.0 collective-permute-done.16.refs_3_
  17.7 1.6 %collective-permute-start.2 = (f32[16,8,128]{2,1,0:T(8,128)S(1)}, f32[16,8,128]{2,1,0:T(8,128)S(1)}, u32[]{:S(2)}, u32[]{:S(2)}) collective-permute-start(f32[16,8,128]{2,1,0:T(8,128)S(1)} %get-tuple-element.70), channel_id=1, source_target_pairs={{0,2},{1,3},{2,0},{3,1},{4,6},{5,7},{6,4},{7,5},{8,10},{9,11},{10,... | collective-permute-start | bytes 196616 | tf_op jit(solution)/shard_map/ppermute | solution.py:370
  19.3 0.0 collective-permute-done.17.refs_4_
  19.3 0.0 copy-start.4
  19.3 0.0 copy-start.5
  19.4 0.1 collective-permute-start.18
  19.4 1.8 %collective-permute-done.5.refs_2_ = f32[33,8,128]{2,1,0:T(8,128)S(1)} collective-permute-done((f32[33,8,128]{2,1,0:T(8,128)S(1)}, f32[33,8,128]{2,1,0:T(8,128)S(1)}, u32[]{:S(2)}, u32[]{:S(2)}) %collective-permute-start.5) | collective-permute-done | bytes 135200 | tf_op jit(solution)/shard_map/ppermute | solution.py:370
  21.3 0.1 collective-permute-start.6
  21.4 1.9 %collective-permute-start.3 = (f32[16,8,128]{2,1,0:T(8,128)S(1)}, f32[16,8,128]{2,1,0:T(8,128)S(1)}, u32[]{:S(2)}, u32[]{:S(2)}) collective-permute-start(f32[16,8,128]{2,1,0:T(8,128)S(1)} %get-tuple-element.71), channel_id=1, source_target_pairs={{0,3},{1,2},{2,1},{3,0},{4,7},{5,6},{6,5},{7,4},{8,11},{9,10},{10,... | collective-permute-start | bytes 196616 | tf_op jit(solution)/shard_map/ppermute | solution.py:370
  23.3 0.0 collective-permute-done.1.refs_2_
  23.3 0.2 collective-permute-start.7
  23.5 1.2 %collective-permute-start.8 = (f32[17,8,128]{2,1,0:T(8,128)S(1)}, f32[17,8,128]{2,1,0:T(8,128)S(1)}, u32[]{:S(2)}, u32[]{:S(2)}) collective-permute-start(f32[17,8,128]{2,1,0:T(8,128)S(1)} %get-tuple-element.77), channel_id=1, source_target_pairs={{0,3},{1,2},{2,1},{3,0},{4,7},{5,6},{6,5},{7,4},{8,11},{9,10},{10,... | collective-permute-start | bytes 208904 | tf_op jit(solution)/shard_map/ppermute | solution.py:370
  24.7 1.0 %collective-permute-done.3.refs_4_ = f32[16,8,128]{2,1,0:T(8,128)S(1)} collective-permute-done((f32[16,8,128]{2,1,0:T(8,128)S(1)}, f32[16,8,128]{2,1,0:T(8,128)S(1)}, u32[]{:S(2)}, u32[]{:S(2)}) %collective-permute-start.3) | collective-permute-done | bytes 65568 | tf_op jit(solution)/shard_map/ppermute | solution.py:370
  25.8 3.3 %collective-permute-start.19 = (f32[32,8,128]{2,1,0:T(8,128)S(1)}, f32[32,8,128]{2,1,0:T(8,128)S(1)}, u32[]{:S(2)}, u32[]{:S(2)}) collective-permute-start(f32[32,8,128]{2,1,0:T(8,128)S(1)} %get-tuple-element.95), channel_id=1, source_target_pairs={{0,8},{1,9},{2,10},{3,11},{4,12},{5,13},{6,14},{7,15},{8,0},{9,1},... | collective-permute-start | bytes 393224 | tf_op jit(solution)/shard_map/ppermute | solution.py:370
  29.0 0.0 collective-permute-done.6.refs_6_
  29.1 2.0 %collective-permute-start.20 = (f32[32,8,128]{2,1,0:T(8,128)S(1)}, f32[32,8,128]{2,1,0:T(8,128)S(1)}, u32[]{:S(2)}, u32[]{:S(2)}) collective-permute-start(f32[32,8,128]{2,1,0:T(8,128)S(1)} %get-tuple-element.96), channel_id=1, source_target_pairs={{0,12},{1,13},{2,14},{3,15},{4,8},{5,9},{6,10},{7,11},{8,4},{9,5},... | collective-permute-start | bytes 393224 | tf_op jit(solution)/shard_map/ppermute | solution.py:370
  31.0 0.3 shard_map.129
  31.4 0.0 collective-permute-done.7.refs_7_
  31.4 0.0 collective-permute-done.8.refs_8_
  31.4 0.5 copy-done.3
  31.9 1.0 %shard_map.130 = (f32[32,8,128]{2,1,0:T(8,128)S(1)}, f32[32,8,128]{2,1,0:T(8,128)S(1)}, f32[32,8,128]{2,1,0:T(8,128)S(1)}, f32[32,8,128]{2,1,0:T(8,128)S(1)}, f3...) custom-call(s32[1]{0:T(128)} %bitcast.refs_0_, ...), custom_call_target="tpu_custom_call" | custom-call | flops 402653184 | bytes 3297280 | tf_op jit(solution)/shard_map/pallas_call | solution.py:192
  32.9 1.2 %collective-permute-start.9 = (f32[32,8,128]{2,1,0:T(8,128)S(1)}, f32[32,8,128]{2,1,0:T(8,128)S(1)}, u32[]{:S(2)}, u32[]{:S(2)}) collective-permute-start(f32[32,8,128]{2,1,0:T(8,128)S(1)} %get-tuple-element.80), channel_id=1, source_target_pairs={{0,4},{1,5},{2,6},{3,7},{4,0},{5,1},{6,2},{7,3},{8,12},{9,13},{10,... | collective-permute-start | bytes 393224 | tf_op jit(solution)/shard_map/ppermute | solution.py:370
  34.1 1.3 %collective-permute-start.10 = (f32[32,8,128]{2,1,0:T(8,128)S(1)}, f32[32,8,128]{2,1,0:T(8,128)S(1)}, u32[]{:S(2)}, u32[]{:S(2)}) collective-permute-start(f32[32,8,128]{2,1,0:T(8,128)S(1)} %get-tuple-element.81), channel_id=1, source_target_pairs={{0,8},{1,9},{2,10},{3,11},{4,12},{5,13},{6,14},{7,15},{8,0},{9,1},... | collective-permute-start | bytes 393224 | tf_op jit(solution)/shard_map/ppermute | solution.py:370
  35.3 2.0 %collective-permute-start.11 = (f32[32,8,128]{2,1,0:T(8,128)S(1)}, f32[32,8,128]{2,1,0:T(8,128)S(1)}, u32[]{:S(2)}, u32[]{:S(2)}) collective-permute-start(f32[32,8,128]{2,1,0:T(8,128)S(1)} %get-tuple-element.82), channel_id=1, source_target_pairs={{0,12},{1,13},{2,14},{3,15},{4,8},{5,9},{6,10},{7,11},{8,4},{9,5},... | collective-permute-start | bytes 393224 | tf_op jit(solution)/shard_map/ppermute | solution.py:370
  37.3 1.7 %collective-permute-done.19.refs_3_ = f32[32,8,128]{2,1,0:T(8,128)S(1)} collective-permute-done((f32[32,8,128]{2,1,0:T(8,128)S(1)}, f32[32,8,128]{2,1,0:T(8,128)S(1)}, u32[]{:S(2)}, u32[]{:S(2)}) %collective-permute-start.19) | collective-permute-done | bytes 131104 | tf_op jit(solution)/shard_map/ppermute | solution.py:370
  39.1 0.7 shard_map.135
  39.7 0.1 collective-permute-start.21
  39.8 1.4 %collective-permute-start.22 = (f32[16,8,128]{2,1,0:T(8,128)S(1)}, f32[16,8,128]{2,1,0:T(8,128)S(1)}, u32[]{:S(2)}, u32[]{:S(2)}) collective-permute-start(f32[16,8,128]{2,1,0:T(8,128)S(1)} %get-tuple-element.101), channel_id=1, source_target_pairs={{0,2},{1,3},{2,0},{3,1},{4,6},{5,7},{6,4},{7,5},{8,10},{9,11},{10,... | collective-permute-start | bytes 196616 | tf_op jit(solution)/shard_map/ppermute | solution.py:370
  41.2 0.0 collective-permute-done.9.refs_2_
  41.2 9.1 %collective-permute-done.10.refs_3_ = f32[32,8,128]{2,1,0:T(8,128)S(1)} collective-permute-done((f32[32,8,128]{2,1,0:T(8,128)S(1)}, f32[32,8,128]{2,1,0:T(8,128)S(1)}, u32[]{:S(2)}, u32[]{:S(2)}) %collective-permute-start.10) | collective-permute-done | bytes 131104 | tf_op jit(solution)/shard_map/ppermute | solution.py:370
  50.3 0.0 collective-permute-done.11.refs_4_
  50.3 0.1 collective-permute-start.12
  50.4 0.5 collective-permute-start.24
  50.9 1.0 %collective-permute-start.23 = (f32[16,8,128]{2,1,0:T(8,128)S(1)}, f32[16,8,128]{2,1,0:T(8,128)S(1)}, u32[]{:S(2)}, u32[]{:S(2)}) collective-permute-start(f32[16,8,128]{2,1,0:T(8,128)S(1)} %get-tuple-element.102), channel_id=1, source_target_pairs={{0,3},{1,2},{2,1},{3,0},{4,7},{5,6},{6,5},{7,4},{8,11},{9,10},{10,... | collective-permute-start | bytes 196616 | tf_op jit(solution)/shard_map/ppermute | solution.py:370
  51.9 0.0 collective-permute-done.21.refs_2_
  51.9 0.7 collective-permute-start.25
  52.6 0.0 collective-permute-done.22.refs_3_
  52.6 0.8 collective-permute-start.26
  53.4 1.7 %collective-permute-done.23.refs_4_ = f32[16,8,128]{2,1,0:T(8,128)S(1)} collective-permute-done((f32[16,8,128]{2,1,0:T(8,128)S(1)}, f32[16,8,128]{2,1,0:T(8,128)S(1)}, u32[]{:S(2)}, u32[]{:S(2)}) %collective-permute-start.23) | collective-permute-done | bytes 65568 | tf_op jit(solution)/shard_map/ppermute | solution.py:370
  55.0 0.6 collective-permute-start.13
  55.7 1.0 %collective-permute-start.14 = (f32[32,8,128]{2,1,0:T(8,128)S(1)}, f32[32,8,128]{2,1,0:T(8,128)S(1)}, u32[]{:S(2)}, u32[]{:S(2)}) collective-permute-start(f32[32,8,128]{2,1,0:T(8,128)S(1)} %get-tuple-element.86), channel_id=1, source_target_pairs={{0,3},{1,2},{2,1},{3,0},{4,7},{5,6},{6,5},{7,4},{8,11},{9,10},{10,... | collective-permute-start | bytes 393224 | tf_op jit(solution)/shard_map/ppermute | solution.py:370
  56.7 0.3 collective-permute-done.25.refs_7_.refs_3_
  57.1 1.0 %collective-permute-done.26.refs_8_.refs_4_ = f32[17,8,128]{2,1,0:T(8,128)S(1)} collective-permute-done((f32[17,8,128]{2,1,0:T(8,128)S(1)}, f32[17,8,128]{2,1,0:T(8,128)S(1)}, u32[]{:S(2)}, u32[]{:S(2)}) %collective-permute-start.26) | collective-permute-done | bytes 69664 | tf_op jit(solution)/shard_map/ppermute | solution.py:370
  58.0 3.2 %collective-permute-start.27 = (f32[33,8,128]{2,1,0:T(8,128)S(1)}, f32[33,8,128]{2,1,0:T(8,128)S(1)}, u32[]{:S(2)}, u32[]{:S(2)}) collective-permute-start(f32[33,8,128]{2,1,0:T(8,128)S(1)} %get-tuple-element.108), channel_id=1, source_target_pairs={{0,4},{1,5},{2,6},{3,7},{4,0},{5,1},{6,2},{7,3},{8,12},{9,13},{10,... | collective-permute-start | bytes 405512 | tf_op jit(solution)/shard_map/ppermute | solution.py:370
  61.2 2.0 %collective-permute-start.28 = (f32[33,8,128]{2,1,0:T(8,128)S(1)}, f32[33,8,128]{2,1,0:T(8,128)S(1)}, u32[]{:S(2)}, u32[]{:S(2)}) collective-permute-start(f32[33,8,128]{2,1,0:T(8,128)S(1)} %get-tuple-element.109), channel_id=1, source_target_pairs={{0,8},{1,9},{2,10},{3,11},{4,12},{5,13},{6,14},{7,15},{8,0},{9,1},... | collective-permute-start | bytes 405512 | tf_op jit(solution)/shard_map/ppermute | solution.py:370
  63.3 1.5 %collective-permute-start.29 = (f32[33,8,128]{2,1,0:T(8,128)S(1)}, f32[33,8,128]{2,1,0:T(8,128)S(1)}, u32[]{:S(2)}, u32[]{:S(2)}) collective-permute-start(f32[33,8,128]{2,1,0:T(8,128)S(1)} %get-tuple-element.110), channel_id=1, source_target_pairs={{0,12},{1,13},{2,14},{3,15},{4,8},{5,9},{6,10},{7,11},{8,4},{9,5},... | collective-permute-start | bytes 405512 | tf_op jit(solution)/shard_map/ppermute | solution.py:370
  64.8 1.7 %shard_map.139 = (f32[128,16]{1,0:T(8,128)}, f32[128,128]{1,0:T(8,128)}) custom-call(s32[1]{0:T(128)} %bitcast.refs_0_, f32[128,1024]{1,0:T(8,128)S(1)} %get-tuple-element.118.refs_1_, f32[128,1024]{1,0:T(8,128)S(1)} %get-tuple-element.119.refs_2_, f32[128,1024]{1,0:T(8,128)S(1)} %get-tuple-element.120.refs_3_, f32[128,1024]{1,0:T(8,128)S(1)} %get-tuple-element.121.refs_4_), custom_call_target="tpu_custom_call" | custom-call | flops 402653184 | bytes 2170880 | tf_op jit(solution)/shard_map/pallas_call | solution.py:192
  66.5 1.6 %shard_map.133 = (f32[128,1024]{1,0:T(8,128)}, f32[128,16]{1,0:T(8,128)}) custom-call(s32[1]{0:T(128)} %bitcast.refs_0_, f32[32,8,128]{2,1,0:T(8,128)S(1)} %get-tuple-element.83.refs_1_, f32[32,8,128]{2,1,0:T(8,128)S(1)} %collective-permute-done.12.refs_2_, f32[32,8,128]{2,1,0:T(8,128)S(1)} %collective-permute-done.13.refs_3_, ...), custom_call_target="tpu_custom_call" | custom-call | flops 402653184 | bytes 2170880 | tf_op jit(solution)/shard_map/pallas_call | solution.py:192
  68.1 0.3 collective-permute-done.27.refs_2_
  68.4 0.6 collective-permute-done.28.refs_3_
  68.9 5.7 %collective-permute-done.29.refs_4_ = f32[33,8,128]{2,1,0:T(8,128)S(1)} collective-permute-done((f32[33,8,128]{2,1,0:T(8,128)S(1)}, f32[33,8,128]{2,1,0:T(8,128)S(1)}, u32[]{:S(2)}, u32[]{:S(2)}) %collective-permute-start.29) | collective-permute-done | bytes 135200 | tf_op jit(solution)/shard_map/ppermute | solution.py:370
  74.7 1.8 %shard_map.138 = (f32[128,1024]{1,0:T(8,128)}, f32[1,128]{1,0:T(1,128)}, f32[128,128]{1,0:T(8,128)}) custom-call(s32[1]{0:T(128)} %bitcast.refs_0_, f32[33,8,128]{2,1,0:T(8,128)S(1)} %get-tuple-element.107.refs_1_, f32[33,8,128]{2,1,0:T(8,128)S(1)} %collective-permute-done.27.refs_2_, f32[33,8,128]{2,1,0:T(8,128)S(1)} %collective-permute-done.28.refs_3_, ...), custom_call_target="tpu_custom_call" | custom-call | flops 402653184 | bytes 2315264 | tf_op jit(solution)/shard_map/pallas_call | solution.py:192
  (30 shorter events, 0.2 us)
Async XLA Ops:
  0.6 6.4 %copy-start.1 = (f32[128,1024]{1,0:T(8,128)S(1)}, f32[128,1024]{1,0:T(8,128)}, u32[]{:S(2)}) copy-start(f32[128,1024]{1,0:T(8,128)} %refs_6_.3) | copy-start | bytes 1572868
  0.6 6.4 %copy-start.7 = (f32[8,16,16]{2,1,0:T(8,128)S(1)}, f32[8,16,16]{2,1,0:T(8,128)}, u32[]{:S(2)}) copy-start(f32[8,16,16]{2,1,0:T(8,128)} %param.13) | copy-start | bytes 24580
  2.9 10.9 %collective-permute-start = (f32[33,8,128]{2,1,0:T(8,128)}, f32[33,8,128]{2,1,0:T(8,128)S(1)}, u32[]{:S(2)}, u32[]{:S(2)}) collective-permute-start(f32[33,8,128]{2,1,0:T(8,128)} %get-tuple-element.67), channel_id=1, source_target_pairs={{0,8},{1,9},{2,10},{3,11},{4,12},{5,13},{6,14},{7,15},{8,0},{9,1},... | collective-permute-start | bytes 405512 | tf_op jit(solution)/shard_map/ppermute | solution.py:370
  7.1 2.6 %copy-start.9 = (f32[33,8,128]{2,1,0:T(8,128)S(1)}, f32[33,8,128]{2,1,0:T(8,128)}, u32[]{:S(2)}) copy-start(f32[33,8,128]{2,1,0:T(8,128)} %get-tuple-element.72) | copy-start | bytes 405508
  7.1 6.8 %copy-start.8 = (f32[33,8,128]{2,1,0:T(8,128)S(1)}, f32[33,8,128]{2,1,0:T(8,128)}, u32[]{:S(2)}) copy-start(f32[33,8,128]{2,1,0:T(8,128)} %get-tuple-element.73) | copy-start | bytes 405508
  7.1 10.5 %copy-start.2 = (f32[33,8,128]{2,1,0:T(8,128)S(1)}, f32[33,8,128]{2,1,0:T(8,128)}, u32[]{:S(2)}) copy-start(f32[33,8,128]{2,1,0:T(8,128)} %get-tuple-element.66.refs_1_.refs_3_) | copy-start | bytes 405508
  7.8 9.9 %collective-permute-start.15 = (f32[32,8,128]{2,1,0:T(8,128)S(1)}, f32[32,8,128]{2,1,0:T(8,128)S(1)}, u32[]{:S(2)}, u32[]{:S(2)}) collective-permute-start(f32[32,8,128]{2,1,0:T(8,128)S(1)} %get-tuple-element.90), channel_id=1, source_target_pairs={{0,1},{1,0},{2,3},{3,2},{4,5},{5,4},{6,7},{7,6},{8,9},{9,8},{10,11... | collective-permute-start | bytes 393224 | tf_op jit(solution)/shard_map/ppermute | solution.py:370
  7.8 9.9 %collective-permute-start.16 = (f32[32,8,128]{2,1,0:T(8,128)S(1)}, f32[32,8,128]{2,1,0:T(8,128)S(1)}, u32[]{:S(2)}, u32[]{:S(2)}) collective-permute-start(f32[32,8,128]{2,1,0:T(8,128)S(1)} %get-tuple-element.91), channel_id=1, source_target_pairs={{0,2},{1,3},{2,0},{3,1},{4,6},{5,7},{6,4},{7,5},{8,10},{9,11},{10,... | collective-permute-start | bytes 393224 | tf_op jit(solution)/shard_map/ppermute | solution.py:370
  9.4 9.9 %collective-permute-start.17 = (f32[32,8,128]{2,1,0:T(8,128)S(1)}, f32[32,8,128]{2,1,0:T(8,128)S(1)}, u32[]{:S(2)}, u32[]{:S(2)}) collective-permute-start(f32[32,8,128]{2,1,0:T(8,128)S(1)} %get-tuple-element.92), channel_id=1, source_target_pairs={{0,3},{1,2},{2,1},{3,0},{4,7},{5,6},{6,5},{7,4},{8,11},{9,10},{10,... | collective-permute-start | bytes 393224 | tf_op jit(solution)/shard_map/ppermute | solution.py:370
  9.7 9.8 %collective-permute-start.4 = (f32[33,8,128]{2,1,0:T(8,128)S(1)}, f32[33,8,128]{2,1,0:T(8,128)S(1)}, u32[]{:S(2)}, u32[]{:S(2)}) collective-permute-start(f32[33,8,128]{2,1,0:T(8,128)S(1)} %copy-done.9), channel_id=1, source_target_pairs={{0,12},{1,13},{2,14},{3,15},{4,8},{5,9},{6,10},{7,11},{8,4},{9,5},... | collective-permute-start | bytes 405512 | tf_op jit(solution)/shard_map/ppermute | solution.py:370
  13.9 7.4 %collective-permute-start.5 = (f32[33,8,128]{2,1,0:T(8,128)S(1)}, f32[33,8,128]{2,1,0:T(8,128)S(1)}, u32[]{:S(2)}, u32[]{:S(2)}) collective-permute-start(f32[33,8,128]{2,1,0:T(8,128)S(1)} %copy-done.8), channel_id=1, source_target_pairs={{0,4},{1,5},{2,6},{3,7},{4,0},{5,1},{6,2},{7,3},{8,12},{9,13},{10,... | collective-permute-start | bytes 405512 | tf_op jit(solution)/shard_map/ppermute | solution.py:370
  17.6 5.7 %collective-permute-start.1 = (f32[16,8,128]{2,1,0:T(8,128)S(1)}, f32[16,8,128]{2,1,0:T(8,128)S(1)}, u32[]{:S(2)}, u32[]{:S(2)}) collective-permute-start(f32[16,8,128]{2,1,0:T(8,128)S(1)} %get-tuple-element.69), channel_id=1, source_target_pairs={{0,1},{1,0},{2,3},{3,2},{4,5},{5,4},{6,7},{7,6},{8,9},{9,8},{10,11... | collective-permute-start | bytes 196616 | tf_op jit(solution)/shard_map/ppermute | solution.py:370
  17.7 5.8 %collective-permute-start.2 = (f32[16,8,128]{2,1,0:T(8,128)S(1)}, f32[16,8,128]{2,1,0:T(8,128)S(1)}, u32[]{:S(2)}, u32[]{:S(2)}) collective-permute-start(f32[16,8,128]{2,1,0:T(8,128)S(1)} %get-tuple-element.70), channel_id=1, source_target_pairs={{0,2},{1,3},{2,0},{3,1},{4,6},{5,7},{6,4},{7,5},{8,10},{9,11},{10,... | collective-permute-start | bytes 196616 | tf_op jit(solution)/shard_map/ppermute | solution.py:370
  19.3 11.7 %copy-start.4 = (f32[1,128,128]{2,1,0:T(8,128)S(1)}, f32[1,128,128]{2,1,0:T(8,128)}, u32[]{:S(2)}) copy-start(f32[1,128,128]{2,1,0:T(8,128)} %param.10) | copy-start | bytes 196612
  19.3 11.7 %copy-start.5 = (f32[8,16,16]{2,1,0:T(8,128)S(1)}, f32[8,16,16]{2,1,0:T(8,128)}, u32[]{:S(2)}) copy-start(f32[8,16,16]{2,1,0:T(8,128)} %param.11) | copy-start | bytes 24580
  19.4 16.0 %collective-permute-start.18 = (f32[32,8,128]{2,1,0:T(8,128)S(1)}, f32[32,8,128]{2,1,0:T(8,128)S(1)}, u32[]{:S(2)}, u32[]{:S(2)}) collective-permute-start(f32[32,8,128]{2,1,0:T(8,128)S(1)} %get-tuple-element.94), channel_id=1, source_target_pairs={{0,4},{1,5},{2,6},{3,7},{4,0},{5,1},{6,2},{7,3},{8,12},{9,13},{10,... | collective-permute-start | bytes 393224 | tf_op jit(solution)/shard_map/ppermute | solution.py:370
  21.3 7.8 %collective-permute-start.6 = (f32[17,8,128]{2,1,0:T(8,128)S(1)}, f32[17,8,128]{2,1,0:T(8,128)S(1)}, u32[]{:S(2)}, u32[]{:S(2)}) collective-permute-start(f32[17,8,128]{2,1,0:T(8,128)S(1)} %get-tuple-element.75), channel_id=1, source_target_pairs={{0,1},{1,0},{2,3},{3,2},{4,5},{5,4},{6,7},{7,6},{8,9},{9,8},{10,11... | collective-permute-start | bytes 208904 | tf_op jit(solution)/shard_map/ppermute | solution.py:370
  21.4 4.4 %collective-permute-start.3 = (f32[16,8,128]{2,1,0:T(8,128)S(1)}, f32[16,8,128]{2,1,0:T(8,128)S(1)}, u32[]{:S(2)}, u32[]{:S(2)}) collective-permute-start(f32[16,8,128]{2,1,0:T(8,128)S(1)} %get-tuple-element.71), channel_id=1, source_target_pairs={{0,3},{1,2},{2,1},{3,0},{4,7},{5,6},{6,5},{7,4},{8,11},{9,10},{10,... | collective-permute-start | bytes 196616 | tf_op jit(solution)/shard_map/ppermute | solution.py:370
  23.3 8.1 %collective-permute-start.7 = (f32[17,8,128]{2,1,0:T(8,128)S(1)}, f32[17,8,128]{2,1,0:T(8,128)S(1)}, u32[]{:S(2)}, u32[]{:S(2)}) collective-permute-start(f32[17,8,128]{2,1,0:T(8,128)S(1)} %get-tuple-element.76), channel_id=1, source_target_pairs={{0,2},{1,3},{2,0},{3,1},{4,6},{5,7},{6,4},{7,5},{8,10},{9,11},{10,... | collective-permute-start | bytes 208904 | tf_op jit(solution)/shard_map/ppermute | solution.py:370
  23.5 7.9 %collective-permute-start.8 = (f32[17,8,128]{2,1,0:T(8,128)S(1)}, f32[17,8,128]{2,1,0:T(8,128)S(1)}, u32[]{:S(2)}, u32[]{:S(2)}) collective-permute-start(f32[17,8,128]{2,1,0:T(8,128)S(1)} %get-tuple-element.77), channel_id=1, source_target_pairs={{0,3},{1,2},{2,1},{3,0},{4,7},{5,6},{6,5},{7,4},{8,11},{9,10},{10,... | collective-permute-start | bytes 208904 | tf_op jit(solution)/shard_map/ppermute | solution.py:370
  25.8 13.3 %collective-permute-start.19 = (f32[32,8,128]{2,1,0:T(8,128)S(1)}, f32[32,8,128]{2,1,0:T(8,128)S(1)}, u32[]{:S(2)}, u32[]{:S(2)}) collective-permute-start(f32[32,8,128]{2,1,0:T(8,128)S(1)} %get-tuple-element.95), channel_id=1, source_target_pairs={{0,8},{1,9},{2,10},{3,11},{4,12},{5,13},{6,14},{7,15},{8,0},{9,1},... | collective-permute-start | bytes 393224 | tf_op jit(solution)/shard_map/ppermute | solution.py:370
  29.0 2.0 %copy-start.6 = (f32[128]{0:T(128)S(1)}, f32[128]{0:T(128)}, u32[]{:S(2)}) copy-start(f32[128]{0:T(128)} %param.9) | copy-start | bytes 1540
  29.1 10.0 %collective-permute-start.20 = (f32[32,8,128]{2,1,0:T(8,128)S(1)}, f32[32,8,128]{2,1,0:T(8,128)S(1)}, u32[]{:S(2)}, u32[]{:S(2)}) collective-permute-start(f32[32,8,128]{2,1,0:T(8,128)S(1)} %get-tuple-element.96), channel_id=1, source_target_pairs={{0,12},{1,13},{2,14},{3,15},{4,8},{5,9},{6,10},{7,11},{8,4},{9,5},... | collective-permute-start | bytes 393224 | tf_op jit(solution)/shard_map/ppermute | solution.py:370
  31.0 0.8 %copy-start.3 = (f32[1,128,128]{2,1,0:T(8,128)S(1)}, f32[1,128,128]{2,1,0:T(8,128)}, u32[]{:S(2)}) copy-start(f32[1,128,128]{2,1,0:T(8,128)} %param.12) | copy-start | bytes 196612
  32.9 8.4 %collective-permute-start.9 = (f32[32,8,128]{2,1,0:T(8,128)S(1)}, f32[32,8,128]{2,1,0:T(8,128)S(1)}, u32[]{:S(2)}, u32[]{:S(2)}) collective-permute-start(f32[32,8,128]{2,1,0:T(8,128)S(1)} %get-tuple-element.80), channel_id=1, source_target_pairs={{0,4},{1,5},{2,6},{3,7},{4,0},{5,1},{6,2},{7,3},{8,12},{9,13},{10,... | collective-permute-start | bytes 393224 | tf_op jit(solution)/shard_map/ppermute | solution.py:370
  34.1 16.2 %collective-permute-start.10 = (f32[32,8,128]{2,1,0:T(8,128)S(1)}, f32[32,8,128]{2,1,0:T(8,128)S(1)}, u32[]{:S(2)}, u32[]{:S(2)}) collective-permute-start(f32[32,8,128]{2,1,0:T(8,128)S(1)} %get-tuple-element.81), channel_id=1, source_target_pairs={{0,8},{1,9},{2,10},{3,11},{4,12},{5,13},{6,14},{7,15},{8,0},{9,1},... | collective-permute-start | bytes 393224 | tf_op jit(solution)/shard_map/ppermute | solution.py:370
  35.3 15.0 %collective-permute-start.11 = (f32[32,8,128]{2,1,0:T(8,128)S(1)}, f32[32,8,128]{2,1,0:T(8,128)S(1)}, u32[]{:S(2)}, u32[]{:S(2)}) collective-permute-start(f32[32,8,128]{2,1,0:T(8,128)S(1)} %get-tuple-element.82), channel_id=1, source_target_pairs={{0,12},{1,13},{2,14},{3,15},{4,8},{5,9},{6,10},{7,11},{8,4},{9,5},... | collective-permute-start | bytes 393224 | tf_op jit(solution)/shard_map/ppermute | solution.py:370
  39.7 12.2 %collective-permute-start.21 = (f32[16,8,128]{2,1,0:T(8,128)S(1)}, f32[16,8,128]{2,1,0:T(8,128)S(1)}, u32[]{:S(2)}, u32[]{:S(2)}) collective-permute-start(f32[16,8,128]{2,1,0:T(8,128)S(1)} %get-tuple-element.100), channel_id=1, source_target_pairs={{0,1},{1,0},{2,3},{3,2},{4,5},{5,4},{6,7},{7,6},{8,9},{9,8},{10,11... | collective-permute-start | bytes 196616 | tf_op jit(solution)/shard_map/ppermute | solution.py:370
  39.8 12.8 %collective-permute-start.22 = (f32[16,8,128]{2,1,0:T(8,128)S(1)}, f32[16,8,128]{2,1,0:T(8,128)S(1)}, u32[]{:S(2)}, u32[]{:S(2)}) collective-permute-start(f32[16,8,128]{2,1,0:T(8,128)S(1)} %get-tuple-element.101), channel_id=1, source_target_pairs={{0,2},{1,3},{2,0},{3,1},{4,6},{5,7},{6,4},{7,5},{8,10},{9,11},{10,... | collective-permute-start | bytes 196616 | tf_op jit(solution)/shard_map/ppermute | solution.py:370
  50.3 12.9 %collective-permute-start.12 = (f32[32,8,128]{2,1,0:T(8,128)S(1)}, f32[32,8,128]{2,1,0:T(8,128)S(1)}, u32[]{:S(2)}, u32[]{:S(2)}) collective-permute-start(f32[32,8,128]{2,1,0:T(8,128)S(1)} %get-tuple-element.84), channel_id=1, source_target_pairs={{0,1},{1,0},{2,3},{3,2},{4,5},{5,4},{6,7},{7,6},{8,9},{9,8},{10,11... | collective-permute-start | bytes 393224 | tf_op jit(solution)/shard_map/ppermute | solution.py:370
  50.4 5.3 %collective-permute-start.24 = (f32[17,8,128]{2,1,0:T(8,128)S(1)}, f32[17,8,128]{2,1,0:T(8,128)S(1)}, u32[]{:S(2)}, u32[]{:S(2)}) collective-permute-start(f32[17,8,128]{2,1,0:T(8,128)S(1)} %get-tuple-element.104), channel_id=1, source_target_pairs={{0,1},{1,0},{2,3},{3,2},{4,5},{5,4},{6,7},{7,6},{8,9},{9,8},{10,11... | collective-permute-start | bytes 208904 | tf_op jit(solution)/shard_map/ppermute | solution.py:370
  50.9 4.1 %collective-permute-start.23 = (f32[16,8,128]{2,1,0:T(8,128)S(1)}, f32[16,8,128]{2,1,0:T(8,128)S(1)}, u32[]{:S(2)}, u32[]{:S(2)}) collective-permute-start(f32[16,8,128]{2,1,0:T(8,128)S(1)} %get-tuple-element.102), channel_id=1, source_target_pairs={{0,3},{1,2},{2,1},{3,0},{4,7},{5,6},{6,5},{7,4},{8,11},{9,10},{10,... | collective-permute-start | bytes 196616 | tf_op jit(solution)/shard_map/ppermute | solution.py:370
  51.9 5.1 %collective-permute-start.25 = (f32[17,8,128]{2,1,0:T(8,128)S(1)}, f32[17,8,128]{2,1,0:T(8,128)S(1)}, u32[]{:S(2)}, u32[]{:S(2)}) collective-permute-start(f32[17,8,128]{2,1,0:T(8,128)S(1)} %get-tuple-element.105), channel_id=1, source_target_pairs={{0,2},{1,3},{2,0},{3,1},{4,6},{5,7},{6,4},{7,5},{8,10},{9,11},{10,... | collective-permute-start | bytes 208904 | tf_op jit(solution)/shard_map/ppermute | solution.py:370
  52.6 5.4 %collective-permute-start.26 = (f32[17,8,128]{2,1,0:T(8,128)S(1)}, f32[17,8,128]{2,1,0:T(8,128)S(1)}, u32[]{:S(2)}, u32[]{:S(2)}) collective-permute-start(f32[17,8,128]{2,1,0:T(8,128)S(1)} %get-tuple-element.106), channel_id=1, source_target_pairs={{0,3},{1,2},{2,1},{3,0},{4,7},{5,6},{6,5},{7,4},{8,11},{9,10},{10,... | collective-permute-start | bytes 208904 | tf_op jit(solution)/shard_map/ppermute | solution.py:370
  55.0 11.4 %collective-permute-start.13 = (f32[32,8,128]{2,1,0:T(8,128)S(1)}, f32[32,8,128]{2,1,0:T(8,128)S(1)}, u32[]{:S(2)}, u32[]{:S(2)}) collective-permute-start(f32[32,8,128]{2,1,0:T(8,128)S(1)} %get-tuple-element.85), channel_id=1, source_target_pairs={{0,2},{1,3},{2,0},{3,1},{4,6},{5,7},{6,4},{7,5},{8,10},{9,11},{10,... | collective-permute-start | bytes 393224 | tf_op jit(solution)/shard_map/ppermute | solution.py:370
  55.7 10.8 %collective-permute-start.14 = (f32[32,8,128]{2,1,0:T(8,128)S(1)}, f32[32,8,128]{2,1,0:T(8,128)S(1)}, u32[]{:S(2)}, u32[]{:S(2)}) collective-permute-start(f32[32,8,128]{2,1,0:T(8,128)S(1)} %get-tuple-element.86), channel_id=1, source_target_pairs={{0,3},{1,2},{2,1},{3,0},{4,7},{5,6},{6,5},{7,4},{8,11},{9,10},{10,... | collective-permute-start | bytes 393224 | tf_op jit(solution)/shard_map/ppermute | solution.py:370
  58.0 10.3 %collective-permute-start.27 = (f32[33,8,128]{2,1,0:T(8,128)S(1)}, f32[33,8,128]{2,1,0:T(8,128)S(1)}, u32[]{:S(2)}, u32[]{:S(2)}) collective-permute-start(f32[33,8,128]{2,1,0:T(8,128)S(1)} %get-tuple-element.108), channel_id=1, source_target_pairs={{0,4},{1,5},{2,6},{3,7},{4,0},{5,1},{6,2},{7,3},{8,12},{9,13},{10,... | collective-permute-start | bytes 405512 | tf_op jit(solution)/shard_map/ppermute | solution.py:370
  61.2 7.7 %collective-permute-start.28 = (f32[33,8,128]{2,1,0:T(8,128)S(1)}, f32[33,8,128]{2,1,0:T(8,128)S(1)}, u32[]{:S(2)}, u32[]{:S(2)}) collective-permute-start(f32[33,8,128]{2,1,0:T(8,128)S(1)} %get-tuple-element.109), channel_id=1, source_target_pairs={{0,8},{1,9},{2,10},{3,11},{4,12},{5,13},{6,14},{7,15},{8,0},{9,1},... | collective-permute-start | bytes 405512 | tf_op jit(solution)/shard_map/ppermute | solution.py:370
  63.3 11.4 %collective-permute-start.29 = (f32[33,8,128]{2,1,0:T(8,128)S(1)}, f32[33,8,128]{2,1,0:T(8,128)S(1)}, u32[]{:S(2)}, u32[]{:S(2)}) collective-permute-start(f32[33,8,128]{2,1,0:T(8,128)S(1)} %get-tuple-element.110), channel_id=1, source_target_pairs={{0,12},{1,13},{2,14},{3,15},{4,8},{5,9},{6,10},{7,11},{8,4},{9,5},... | collective-permute-start | bytes 405512 | tf_op jit(solution)/shard_map/ppermute | solution.py:370
  64.8 1.7 %copy-start = (f32[128,1024]{1,0:T(8,128)S(1)}, f32[128,1024]{1,0:T(8,128)}, u32[]{:S(2)}) copy-start(f32[128,1024]{1,0:T(8,128)} %refs_5_.3) | copy-start | bytes 1572868
where the time goes:
time: 77.3 us; the launch traced here: 76.5 us
  starting transfers between devices  38.9 us (50%)
  waiting for transfers between devices  26.1 us (34%)
  Pallas kernels  10.1 us (13%)
  between operations  0.87 us (1%)
    ppermute x30, starting transfers between devices, across(): lax.ppermute(messages[i], 'blocks', [(s, s ^ i * step) for s in range(cou...  38.9 us
    ppermute x30, waiting for transfers between devices, across(): lax.ppermute(messages[i], 'blocks', [(s, s ^ i * step) for s in range(cou...  26.1 us
    pallas_call x14, Pallas kernels, call(): pl.pallas_call(functools.partial(kernel, self, len(args), len(outs), **fi...  10.1 us
  transfers between devices with their start and end apart: 30, of which 11 were waited for; matrix products, arithmetic and copies ran while one was open for 0% of the time, Pallas kernels for 8%

commit v1 on v0

--- a/solution.py
+++ b/solution.py
@@ -16,7 +16,6 @@
 SUB = 8
 LANE = 128
 KERNEL_VMEM = 16 << 20
-LOADING_VMEM = 60 << 20
 
 
 def gelu_value(values):
@@ -103,6 +102,27 @@
     return both[:, : b.shape[0]] + both[:, b.shape[0] :] + dot(a_low, b_high, 1)
 
 
+def pair_of(values):
+    return jnp.concatenate(parts_of(values), axis=0)
+
+
+def stacked_left(rows):
+    high, low = (part.astype(jnp.float32) for part in parts_of(rows))
+    return jnp.concatenate([high, high, low, low], axis=0).T.astype(jnp.bfloat16)
+
+
+def matmul_stacked(left, b):
+    high, low = parts_of(b)
+    return dot(left, jnp.concatenate([high, low, high, low], axis=0), 0)
+
+
+def matmul_nt_pair(a, pair):
+    both = dot(pair_of(a), pair, 1)
+    rows, columns = a.shape[0], pair.shape[0] // 2
+    both = both[:rows] + both[rows:]
+    return both[:, :columns] + both[:, columns:]
+
+
 def pick_rows(chosen, values):
     ones = chosen.astype(jnp.bfloat16)
     return sum(dot(ones, part, 0) for part in reversed(parts_of(values, 3)))
@@ -167,6 +187,34 @@
             tile = message[slot * self.block_tiles + i]
             target[pl.ds(start + r, SUB), c : c + LANE] = tile if scale is None else tile * scale[:, c : c + LANE]
 
+    def take_halves(self, parts, target, z, p, scale=None):
+        for m in range(self.inner):
+            for message, keys in ((parts[m], self.early), (parts[self.inner + m], self.late)):
+                for slot, k in enumerate(keys):
+                    self.take_block(message, slot, target, (z ^ k) * self.inner + (p ^ m), scale)
+
+    def plane_spans(self, keys):
+        return [(m, slot, k, m) for m in range(self.inner) for slot, k in enumerate(keys)]
+
+    def line_spans(self, keys):
+        return [(i, m, k, m) for i, k in enumerate(keys) for m in range(self.inner)]
+
+    def line_up(self, parts, spans, target):
+        for place, (i, slot, _, _) in enumerate(spans):
+            for t, r, c in self.tiles():
+                start = place * self.rows + r
+                target[start : start + SUB, c : c + LANE] = parts[i][slot * self.block_tiles + t]
+
+    def start_of(self, span, z, p):
+        return pl.multiple_of(((z ^ span[2]) * self.inner + (p ^ span[3])) * self.rows, SUB)
+
+    def gather_rows(self, table, spans, z, p):
+        return jnp.concatenate([table[pl.ds(self.start_of(span, z, p), self.rows), :] for span in spans], axis=0)
+
+    def scatter_rows(self, values, spans, target, z, p):
+        for place, span in enumerate(spans):
+            target[pl.ds(self.start_of(span, z, p), self.rows), :] = values[place * self.rows : (place + 1) * self.rows]
+
     def move_block(self, message, slot, target, place):
         size = self.block_tiles
         target[place * size : (place + 1) * size] = message[slot * size : (slot + 1) * size]
@@ -187,6 +235,8 @@
 
     def call(self, kernel, outs, me, *args, scratch=(), flops=0, loads=False, stores=0, **fixed):
         outs = tuple(o if isinstance(o, jax.ShapeDtypeStruct) else jax.ShapeDtypeStruct(o, jnp.float32) for o in outs)
+        if loads:
+            args = [pltpu.with_memory_space_constraint(a, pltpu.HBM) for a in args]
         moved = 4 * sum(math.prod(a.shape) for a in (*args, *outs))
         vmem = pl.BlockSpec(memory_space=pltpu.VMEM)
         return pl.pallas_call(
@@ -199,7 +249,7 @@
             + ([pltpu.VMEM(a.shape, a.dtype) for a in args] + [pltpu.SemaphoreType.DMA((len(args),))] if loads else [])
             + ([pltpu.SemaphoreType.DMA((stores,))] if stores else []),
             cost_estimate=pl.CostEstimate(flops=flops, bytes_accessed=moved, transcendentals=0),
-            compiler_params=pltpu.CompilerParams(vmem_limit_bytes=LOADING_VMEM if loads else KERNEL_VMEM),
+            compiler_params=pltpu.CompilerParams(vmem_limit_bytes=KERNEL_VMEM),
         )(me, *args)
 
 
@@ -255,12 +305,20 @@
     outs[-1][...] = wide_two
 
 
-def widen_one(plan, n_in, n_out, *refs):
-    _, (right, left, gain), (wide, turned, scaled, gain_kept), _ = split_refs(n_in, n_out, refs)
+def prepare(plan, n_in, n_out, *refs):
+    me, (right, left, gain, wide_two, x, cotangent), outs, (table,) = split_refs(n_in, n_out, refs)
+    z, p = me[0] // plan.inner, me[0] % plan.inner
+    wide, turned, gain_kept, scaled_early, scaled_late, wide_early, wide_late, x_pair, cotangent_pair = outs
     wide[...] = widen(plan, right[...])
     turned[...] = left[...].T
-    scaled[...] = (left[...].T * gain[...]).T
     gain_kept[...] = gain[...]
+    table[...] = left[...].T * gain[...]
+    scaled_early[...] = stacked_left(plan.gather_rows(table, plan.line_spans(plan.early), z, p))
+    scaled_late[...] = stacked_left(plan.gather_rows(table, plan.line_spans(plan.late), z, p))
+    wide_early[...] = stacked_left(plan.gather_rows(wide_two, plan.plane_spans(plan.early), z, p))
+    wide_late[...] = stacked_left(plan.gather_rows(wide_two, plan.plane_spans(plan.late), z, p))
+    x_pair[...] = pair_of(x[...])
+    cotangent_pair[...] = pair_of(cotangent[...])
 
 
 def regroup(plan, n_in, n_out, *refs, data):
@@ -280,10 +338,7 @@
     parts, (wide_one, left_two) = ins[: 2 * plan.inner], ins[2 * plan.inner :]
     squares = plan.add_sums(parts)
     inverse_root = plan.sums_row(lax.rsqrt(squares / plan.width + EPSILON))
-    for m in range(plan.inner):
-        for message, keys in ((parts[m], plan.early), (parts[plan.inner + m], plan.late)):
-            for slot, k in enumerate(keys):
-                plan.take_block(message, slot, y1, (z ^ k) * plan.inner + (p ^ m), inverse_root)
+    plan.take_halves(parts, y1, z, p, inverse_root)
     first = y1[...]
     pre = matmul(wide_one[...].T, first)
     tangent = jnp.tanh(COEFF * (pre + CUBIC * pre * pre * pre))
@@ -324,36 +379,62 @@
     grad_left_two[...] = matmul_nt(act[...], dy2[...]) * plan.factor
 
 
+def early_output(plan, n_in, n_out, *refs):
+    _, ins, (partial, product), (y2,) = split_refs(n_in, n_out, refs)
+    parts, (x, wide, cotangent_pair) = ins[: plan.inner], ins[plan.inner :]
+    plan.line_up(parts, plan.plane_spans(plan.early), y2)
+    second = y2[...]
+    partial[...] = x[...] + matmul_stacked(wide[...], second)
+    product[...] = matmul_nt_pair(second, cotangent_pair[...])
+
+
 def finish_output(plan, n_in, n_out, *refs):
-    me, ins, (output, grad_right_two), (y2,) = split_refs(n_in, n_out, refs)
-    z, p = me[0] // plan.inner, me[0] % plan.inner
-    parts, (x, cotangent, wide_two) = ins[: plan.inner], ins[plan.inner :]
-    for m in range(plan.inner):
-        for k in range(plan.outer):
-            plan.take_block(parts[m], k, y2, (z ^ k) * plan.inner + (p ^ m))
+    me, ins, (output, grad_right_two), (y2, whole) = split_refs(n_in, n_out, refs)
+    z, p = me[0] // plan.inner, me[0] % plan.inner
+    parts, (partial, product, wide, cotangent_pair) = ins[: plan.inner], ins[plan.inner :]
+    spans = plan.plane_spans(plan.late)
+    plan.line_up(parts, spans, y2)
     second = y2[...]
-    output[...] = x[...] + matmul(wide_two[...].T, second)
-    grad_right_two[...] = narrow(plan, matmul_nt(second, cotangent[...])) * plan.factor
+    output[...] = partial[...] + matmul_stacked(wide[...], second)
+    plan.scatter_rows(product[...], plan.plane_spans(plan.early), whole, z, p)
+    plan.scatter_rows(matmul_nt_pair(second, cotangent_pair[...]), spans, whole, z, p)
+    grad_right_two[...] = narrow(plan, whole[...]) * plan.factor
+
+
+def early_input(plan, n_in, n_out, *refs):
+    _, ins, (partial, product), (dy1,) = split_refs(n_in, n_out, refs)
+    parts, (cotangent, scaled, x_pair, inverse_root) = ins[: len(plan.early)], ins[len(plan.early) :]
+    plan.line_up(parts, plan.line_spans(plan.early), dy1)
+    back = dy1[...] * inverse_root[...]
+    partial[...] = cotangent[...] + matmul_stacked(scaled[...], back)
+    product[...] = matmul_nt_pair(back, x_pair[...])
 
 
 def finish_input(plan, n_in, n_out, *refs):
-    me, ins, (input_gradient, gain_gradient, grad_left_one), (dy1, result, done) = split_refs(n_in, n_out, refs)
-    z, p = me[0] // plan.inner, me[0] % plan.inner
-    parts, (x, cotangent, gain, turned, scaled, inverse_root) = ins[: plan.outer], ins[plan.outer :]
+    me, ins, outs, (dy1, whole, *made, done) = split_refs(n_in, n_out, refs)
+    z, p = me[0] // plan.inner, me[0] % plan.inner
+    ready, parts, rest = ins[: n_out - len(made)], ins[n_out - len(made) :][: plan.outer], ins[n_out - len(made) + plan.outer :]
+    x, x_pair, gain, turned, scaled, inverse_root, partial, product = rest
+    stores = [pltpu.make_async_copy(s, t, done.at[i]) for i, (s, t) in enumerate(zip((*ready, *made), outs, strict=True))]
+    for store in stores[: len(ready)]:
+        store.start()
+    input_gradient, gain_gradient, grad_left_one = made
+    root = inverse_root[...]
     inner = plan.sums_row(plan.add_sums(parts)) / plan.width
-    for k in range(plan.outer):
-        for m in range(plan.inner):
-            plan.take_block(parts[k], m, dy1, (z ^ k) * plan.inner + (p ^ m))
-    back = dy1[...]
-    root = inverse_root[...]
-    xhat = x[...] * root
-    result[...] = cotangent[...] + root * (matmul(scaled[...], back) - xhat * inner)
-    store = pltpu.make_async_copy(result, input_gradient, done.at[0])
-    store.start()
-    product = matmul_nt(back, xhat)
-    gain_gradient[...] = jnp.sum(turned[...] * product, axis=0, keepdims=True) * plan.factor
-    grad_left_one[...] = (product * gain[...] * plan.factor).T
-    store.wait()
+    spans = plan.line_spans(plan.late)
+    plan.line_up(parts[: len(plan.late)], spans, dy1)
+    back = dy1[...] * root
+    input_gradient[...] = partial[...] + matmul_stacked(scaled[...], back) - x[...] * (root * root * inner)
+    stores[len(ready)].start()
+    plan.scatter_rows(product[...], plan.line_spans(plan.early), whole, z, p)
+    plan.scatter_rows(matmul_nt_pair(back, x_pair[...]), spans, whole, z, p)
+    total = whole[...]
+    gain_gradient[...] = jnp.sum(turned[...] * total, axis=0, keepdims=True) * plan.factor
+    stores[len(ready) + 1].start()
+    grad_left_one[...] = (total * gain[...] * plan.factor).T
+    stores[len(ready) + 2].start()
+    for store in stores:
+        store.wait()
 
 
 def local_tiled(plan, activations, cotangent, gain, left_one, right_one, left_two, right_two):
@@ -394,8 +475,11 @@
         back_two, [message(outer, False)] * inner + [square], cotangent, flat_two, scratch=[full], flops=cost
     )
     dy2_half = over_inner(sent)
-    wide_one, turned_one, scaled_one, gain_kept = call(
-        widen_one, [square] * 3 + [(1, features)], flat_one, one, gain_row, flops=cost // 8
+    half, stacked = (features // 2, tokens), jax.ShapeDtypeStruct((features, 2 * features), jnp.bfloat16)
+    pair = jax.ShapeDtypeStruct((2 * features, tokens), jnp.bfloat16)
+    wide_one, turned_one, gain_kept, scaled_early, scaled_late, wide_early, wide_late, x_pair, cotangent_pair = call(
+        prepare, [square] * 2 + [(1, features)] + [stacked] * 4 + [pair] * 2,
+        flat_one, one, gain_row, wide_two, activations, cotangent, scratch=[square], flops=cost // 8,
     )
     sent = call(regroup, [message(len(early), False)] * inner, *(first[k] for k in early), data=len(early))
     first_early = over_inner(sent)
@@ -417,16 +501,28 @@
     dy1_parts = over_outer(far, sent)
     sent = call(regroup, [message(inner, True)] * len(near), *dy1_near, *dy1_far, data=inner)
     dy1_parts |= over_outer(near, sent)
-    sent = call(regroup, [message(outer, False)] * inner, *(second_half[k] for k in line), data=outer)
-    second_parts = over_inner(sent)
+    sent = call(regroup, [message(len(early), False)] * inner, *(second_half[k] for k in early), data=len(early))
+    second_early = over_inner(sent)
+    sent = call(regroup, [message(len(late), False)] * inner, *(second_half[k] for k in late), data=len(late))
+    second_late = over_inner(sent)
     grad_right_one, grad_left_two = call(grads_middle, [(features, count), square], y1, dpre, act, dy2, flops=2 * cost)
+    partial_output, product_two = call(
+        early_output, [full, (features // 2, features)], *second_early, activations, wide_early, cotangent_pair,
+        scratch=[half], flops=cost,
+    )
+    partial_input, product_one = call(
+        early_input, [full, (features // 2, features)], *(dy1_parts[k] for k in early), cotangent, scaled_early,
+        x_pair, inverse_root, scratch=[half], flops=cost,
+    )
     output, grad_right_two = call(
-        finish_output, [full, (features, count)], *second_parts, activations, cotangent, wide_two,
-        scratch=[full], flops=2 * cost,
-    )
-    input_gradient, gain_gradient, grad_left_one = call(
-        finish_input, [full, (1, features), square], *(dy1_parts[k] for k in line), activations, cotangent,
-        gain_kept, turned_one, scaled_one, inverse_root, scratch=[full] * 2, flops=2 * cost, stores=1,
+        finish_output, [full, (features, count)], *second_late, partial_output, product_two, wide_late,
+        cotangent_pair, scratch=[half, square], flops=cost,
+    )
+    ready, made = [full, (features, count), square, (features, count)], [full, (1, features), square]
+    output, grad_right_one, grad_left_two, grad_right_two, input_gradient, gain_gradient, grad_left_one = call(
+        finish_input, ready + made, output, grad_right_one, grad_left_two, grad_right_two,
+        *(dy1_parts[k] for k in (*late, *early)), activations, x_pair, gain_kept, turned_one, scaled_late, inverse_root,
+        partial_input, product_one, scratch=[half, square, *made], flops=cost, stores=len(ready + made),
     )
     return (
         output,

time: 77.3 us -> 68.7 us (0.89)
  starting transfers between devices: 38.9 us -> 34.5 us
  waiting for transfers between devices: 26.1 us -> 23.8 us
  Pallas kernels: 10.1 us -> 8.7 us
    ppermute x30 -> x33, starting transfers between devices: 38.9 us -> 34.5 us  [across(): lax.ppermute(messages[i], 'blocks', [(s, s ^ i * step) for s in range(cou...]
    ppermute x30 -> x33, waiting for transfers between devices: 26.1 us -> 23.8 us  [across(): lax.ppermute(messages[i], 'blocks', [(s, s ^ i * step) for s in range(cou...]
    pallas_call x14 -> x17, Pallas kernels: 10.1 us -> 8.7 us  [call(): pl.pallas_call(functools.partial(kernel, self, len(args), len(outs), **fi...]
  transfers between devices with their start and end apart: 30 -> 33, of which waited for: 11 -> 12; matrix products, arithmetic and copies ran while one was open for 0% -> 0% of each run, Pallas kernels for 8% -> 8%
where the time goes in v1:
time: 68.7 us; the launch traced here: 68.6 us
  starting transfers between devices  34.5 us (50%)
  waiting for transfers between devices  23.8 us (35%)
  Pallas kernels  8.7 us (13%)
  between operations  0.88 us (1%)
    ppermute x33, starting transfers between devices, across(): lax.ppermute(messages[i], 'blocks', [(s, s ^ i * step) for s in range(cou...  34.5 us
    ppermute x33, waiting for transfers between devices, across(): lax.ppermute(messages[i], 'blocks', [(s, s ^ i * step) for s in range(cou...  23.8 us
    pallas_call x17, Pallas kernels, call(): pl.pallas_call(functools.partial(kernel, self, len(args), len(outs), **fi...  8.7 us
  transfers between devices with their start and end apart: 33, of which 12 were waited for; matrix products, arithmetic and copies ran while one was open for 0% of the time, Pallas kernels for 8%

profile of v1, /device:TPU:0, one launch (start us, length us, event | category | flops | bytes accessed | tf_op | source)
XLA Modules:
  0.0 68.6 jit_solution(661218535384760261)
XLA Ops:
  0.7 1.5 %shard_map.126 = (f32[33,8,128]{2,1,0:T(8,128)S(1)}, f32[33,8,128]{2,1,0:T(8,128)S(1)}, f32[33,8,128]{2,1,0:T(8,128)S(1)}, f32[33,8,128]{2,1,0:T(8,128)S(1)}) custom-call(s32[1]{0:T(128)} %bitcast.refs_0_, f32[128,1024]{1,0:T(8,128)} %refs_9_.1, f32[128,128]{1,0:T(8,128)} %bitcast.11, f32[1,128]{1,0:T(1,128)} %bitcast.16), custom_call_target="tpu_custom_call" | custom-call | flops 201326592 | bytes 1131008 | tf_op jit(solution)/shard_map/pallas_call | solution.py:242
  2.2 4.1 %collective-permute-start = (f32[33,8,128]{2,1,0:T(8,128)S(1)}, f32[33,8,128]{2,1,0:T(8,128)S(1)}, u32[]{:S(2)}, u32[]{:S(2)}) collective-permute-start(f32[33,8,128]{2,1,0:T(8,128)S(1)} %get-tuple-element.84), channel_id=1, source_target_pairs={{0,8},{1,9},{2,10},{3,11},{4,12},{5,13},{6,14},{7,15},{8,0},{9,1},... | collective-permute-start | bytes 405512 | tf_op jit(solution)/shard_map/ppermute | solution.py:451
  6.3 1.3 %collective-permute-start.4 = (f32[33,8,128]{2,1,0:T(8,128)S(1)}, f32[33,8,128]{2,1,0:T(8,128)S(1)}, u32[]{:S(2)}, u32[]{:S(2)}) collective-permute-start(f32[33,8,128]{2,1,0:T(8,128)S(1)} %get-tuple-element.89), channel_id=1, source_target_pairs={{0,12},{1,13},{2,14},{3,15},{4,8},{5,9},{6,10},{7,11},{8,4},{9,5},... | collective-permute-start | bytes 405512 | tf_op jit(solution)/shard_map/ppermute | solution.py:451
  7.7 0.2 collective-permute-start.5
  7.9 0.6 shard_map.129
  8.6 0.1 collective-permute-start.18
  8.6 1.6 %collective-permute-start.19 = (f32[32,8,128]{2,1,0:T(8,128)S(1)}, f32[32,8,128]{2,1,0:T(8,128)S(1)}, u32[]{:S(2)}, u32[]{:S(2)}) collective-permute-start(f32[32,8,128]{2,1,0:T(8,128)S(1)} %get-tuple-element.118), channel_id=1, source_target_pairs={{0,2},{1,3},{2,0},{3,1},{4,6},{5,7},{6,4},{7,5},{8,10},{9,11},{10,... | collective-permute-start | bytes 393224 | tf_op jit(solution)/shard_map/ppermute | solution.py:451
  10.2 6.4 %collective-permute-done.refs_2_.refs_4_ = f32[33,8,128]{2,1,0:T(8,128)S(1)} collective-permute-done((f32[33,8,128]{2,1,0:T(8,128)S(1)}, f32[33,8,128]{2,1,0:T(8,128)S(1)}, u32[]{:S(2)}, u32[]{:S(2)}) %collective-permute-start) | collective-permute-done | bytes 135200 | tf_op jit(solution)/shard_map/ppermute | solution.py:451
  16.6 0.0 collective-permute-start.20
  16.6 2.0 %collective-permute-start.1 = (f32[16,8,128]{2,1,0:T(8,128)S(1)}, f32[16,8,128]{2,1,0:T(8,128)S(1)}, u32[]{:S(2)}, u32[]{:S(2)}) collective-permute-start(f32[16,8,128]{2,1,0:T(8,128)S(1)} %get-tuple-element.86), channel_id=1, source_target_pairs={{0,1},{1,0},{2,3},{3,2},{4,5},{5,4},{6,7},{7,6},{8,9},{9,8},{10,11... | collective-permute-start | bytes 196616 | tf_op jit(solution)/shard_map/ppermute | solution.py:451
  18.6 0.2 collective-permute-start.2
  18.9 0.1 collective-permute-start.6
  19.0 0.0 collective-permute-done.19.refs_3_
  19.0 1.9 %collective-permute-start.3 = (f32[16,8,128]{2,1,0:T(8,128)S(1)}, f32[16,8,128]{2,1,0:T(8,128)S(1)}, u32[]{:S(2)}, u32[]{:S(2)}) collective-permute-start(f32[16,8,128]{2,1,0:T(8,128)S(1)} %get-tuple-element.88), channel_id=1, source_target_pairs={{0,3},{1,2},{2,1},{3,0},{4,7},{5,6},{6,5},{7,4},{8,11},{9,10},{10,... | collective-permute-start | bytes 196616 | tf_op jit(solution)/shard_map/ppermute | solution.py:451
  20.9 1.1 %collective-permute-done.20.refs_4_ = f32[32,8,128]{2,1,0:T(8,128)S(1)} collective-permute-done((f32[32,8,128]{2,1,0:T(8,128)S(1)}, f32[32,8,128]{2,1,0:T(8,128)S(1)}, u32[]{:S(2)}, u32[]{:S(2)}) %collective-permute-start.20) | collective-permute-done | bytes 131104 | tf_op jit(solution)/shard_map/ppermute | solution.py:451
  22.0 0.3 collective-permute-start.21
  22.4 0.0 collective-permute-done.1.refs_2_
  22.4 3.4 %collective-permute-start.22 = (f32[32,8,128]{2,1,0:T(8,128)S(1)}, f32[32,8,128]{2,1,0:T(8,128)S(1)}, u32[]{:S(2)}, u32[]{:S(2)}) collective-permute-start(f32[32,8,128]{2,1,0:T(8,128)S(1)} %get-tuple-element.122), channel_id=1, source_target_pairs={{0,8},{1,9},{2,10},{3,11},{4,12},{5,13},{6,14},{7,15},{8,0},{9,1},... | collective-permute-start | bytes 393224 | tf_op jit(solution)/shard_map/ppermute | solution.py:451
  25.7 0.9 %collective-permute-start.23 = (f32[32,8,128]{2,1,0:T(8,128)S(1)}, f32[32,8,128]{2,1,0:T(8,128)S(1)}, u32[]{:S(2)}, u32[]{:S(2)}) collective-permute-start(f32[32,8,128]{2,1,0:T(8,128)S(1)} %get-tuple-element.123), channel_id=1, source_target_pairs={{0,12},{1,13},{2,14},{3,15},{4,8},{5,9},{6,10},{7,11},{8,4},{9,5},... | collective-permute-start | bytes 393224 | tf_op jit(solution)/shard_map/ppermute | solution.py:451
  26.7 1.5 %collective-permute-start.7 = (f32[17,8,128]{2,1,0:T(8,128)S(1)}, f32[17,8,128]{2,1,0:T(8,128)S(1)}, u32[]{:S(2)}, u32[]{:S(2)}) collective-permute-start(f32[17,8,128]{2,1,0:T(8,128)S(1)} %get-tuple-element.93), channel_id=1, source_target_pairs={{0,2},{1,3},{2,0},{3,1},{4,6},{5,7},{6,4},{7,5},{8,10},{9,11},{10,... | collective-permute-start | bytes 208904 | tf_op jit(solution)/shard_map/ppermute | solution.py:451
  28.2 0.0 collective-permute-done.6.refs_6_
  28.2 0.6 copy-done.5
  28.9 0.5 shard_map.130
  29.4 1.6 %collective-permute-done.7.refs_7_ = f32[17,8,128]{2,1,0:T(8,128)S(1)} collective-permute-done((f32[17,8,128]{2,1,0:T(8,128)S(1)}, f32[17,8,128]{2,1,0:T(8,128)S(1)}, u32[]{:S(2)}, u32[]{:S(2)}) %collective-permute-start.7) | collective-permute-done | bytes 69664 | tf_op jit(solution)/shard_map/ppermute | solution.py:451
  31.0 1.5 %collective-permute-done.8.refs_8_ = f32[17,8,128]{2,1,0:T(8,128)S(1)} collective-permute-done((f32[17,8,128]{2,1,0:T(8,128)S(1)}, f32[17,8,128]{2,1,0:T(8,128)S(1)}, u32[]{:S(2)}, u32[]{:S(2)}) %collective-permute-start.8) | collective-permute-done | bytes 69664 | tf_op jit(solution)/shard_map/ppermute | solution.py:451
  32.5 1.0 %shard_map.131 = (f32[32,8,128]{2,1,0:T(8,128)S(1)}, f32[32,8,128]{2,1,0:T(8,128)S(1)}, f32[32,8,128]{2,1,0:T(8,128)S(1)}, f32[32,8,128]{2,1,0:T(8,128)S(1)}, f3...) custom-call(s32[1]{0:T(128)} %bitcast.refs_0_, ...), custom_call_target="tpu_custom_call" | custom-call | flops 402653184 | bytes 3297280 | tf_op jit(solution)/shard_map/pallas_call | solution.py:242
  33.5 3.0 %collective-permute-start.9 = (f32[32,8,128]{2,1,0:T(8,128)S(1)}, f32[32,8,128]{2,1,0:T(8,128)S(1)}, u32[]{:S(2)}, u32[]{:S(2)}) collective-permute-start(f32[32,8,128]{2,1,0:T(8,128)S(1)} %get-tuple-element.97), channel_id=1, source_target_pairs={{0,12},{1,13},{2,14},{3,15},{4,8},{5,9},{6,10},{7,11},{8,4},{9,5},... | collective-permute-start | bytes 393224 | tf_op jit(solution)/shard_map/ppermute | solution.py:451
  36.4 0.0 collective-permute-done.21.refs_2_
  36.4 1.5 %collective-permute-start.14 = (f32[32,8,128]{2,1,0:T(8,128)S(1)}, f32[32,8,128]{2,1,0:T(8,128)S(1)}, u32[]{:S(2)}, u32[]{:S(2)}) collective-permute-start(f32[32,8,128]{2,1,0:T(8,128)S(1)} %get-tuple-element.104), channel_id=1, source_target_pairs={{0,8},{1,9},{2,10},{3,11},{4,12},{5,13},{6,14},{7,15},{8,0},{9,1},... | collective-permute-start | bytes 393224 | tf_op jit(solution)/shard_map/ppermute | solution.py:451
  37.9 0.0 collective-permute-done.22.refs_3_
  37.9 0.0 collective-permute-done.23.refs_4_
  37.9 0.7 shard_map.137
  38.6 0.1 collective-permute-start.28
  38.7 0.5 collective-permute-start.24
  39.2 0.7 %collective-permute-done.28.refs_2_ = f32[16,8,128]{2,1,0:T(8,128)S(1)} collective-permute-done((f32[16,8,128]{2,1,0:T(8,128)S(1)}, f32[16,8,128]{2,1,0:T(8,128)S(1)}, u32[]{:S(2)}, u32[]{:S(2)}) %collective-permute-start.28) | collective-permute-done | bytes 65568 | tf_op jit(solution)/shard_map/ppermute | solution.py:451
  39.9 0.7 %collective-permute-start.29 = (f32[16,8,128]{2,1,0:T(8,128)S(1)}, f32[16,8,128]{2,1,0:T(8,128)S(1)}, u32[]{:S(2)}, u32[]{:S(2)}) collective-permute-start(f32[16,8,128]{2,1,0:T(8,128)S(1)} %get-tuple-element.139), channel_id=1, source_target_pairs={{0,2},{1,3},{2,0},{3,1},{4,6},{5,7},{6,4},{7,5},{8,10},{9,11},{10,... | collective-permute-start | bytes 196616 | tf_op jit(solution)/shard_map/ppermute | solution.py:451
  40.6 1.1 %collective-permute-done.9.refs_1_ = f32[32,8,128]{2,1,0:T(8,128)S(1)} collective-permute-done((f32[32,8,128]{2,1,0:T(8,128)S(1)}, f32[32,8,128]{2,1,0:T(8,128)S(1)}, u32[]{:S(2)}, u32[]{:S(2)}) %collective-permute-start.9) | collective-permute-done | bytes 131104 | tf_op jit(solution)/shard_map/ppermute | solution.py:451
  41.7 0.8 %collective-permute-start.25 = (f32[17,8,128]{2,1,0:T(8,128)S(1)}, f32[17,8,128]{2,1,0:T(8,128)S(1)}, u32[]{:S(2)}, u32[]{:S(2)}) collective-permute-start(f32[17,8,128]{2,1,0:T(8,128)S(1)} %get-tuple-element.134), channel_id=1, source_target_pairs={{0,2},{1,3},{2,0},{3,1},{4,6},{5,7},{6,4},{7,5},{8,10},{9,11},{10,... | collective-permute-start | bytes 208904 | tf_op jit(solution)/shard_map/ppermute | solution.py:451
  42.5 1.4 %collective-permute-done.10.refs_2_ = f32[32,8,128]{2,1,0:T(8,128)S(1)} collective-permute-done((f32[32,8,128]{2,1,0:T(8,128)S(1)}, f32[32,8,128]{2,1,0:T(8,128)S(1)}, u32[]{:S(2)}, u32[]{:S(2)}) %collective-permute-start.10) | collective-permute-done | bytes 131104 | tf_op jit(solution)/shard_map/ppermute | solution.py:451
  43.9 1.6 %collective-permute-start.26 = (f32[17,8,128]{2,1,0:T(8,128)S(1)}, f32[17,8,128]{2,1,0:T(8,128)S(1)}, u32[]{:S(2)}, u32[]{:S(2)}) collective-permute-start(f32[17,8,128]{2,1,0:T(8,128)S(1)} %get-tuple-element.135), channel_id=1, source_target_pairs={{0,3},{1,2},{2,1},{3,0},{4,7},{5,6},{6,5},{7,4},{8,11},{9,10},{10,... | collective-permute-start | bytes 208904 | tf_op jit(solution)/shard_map/ppermute | solution.py:451
  45.5 3.4 %collective-permute-done.14.refs_2_ = f32[32,8,128]{2,1,0:T(8,128)S(1)} collective-permute-done((f32[32,8,128]{2,1,0:T(8,128)S(1)}, f32[32,8,128]{2,1,0:T(8,128)S(1)}, u32[]{:S(2)}, u32[]{:S(2)}) %collective-permute-start.14) | collective-permute-done | bytes 131104 | tf_op jit(solution)/shard_map/ppermute | solution.py:451
  48.9 0.4 collective-permute-start.30
  49.4 1.3 %collective-permute-start.11 = (f32[16,8,128]{2,1,0:T(8,128)S(1)}, f32[16,8,128]{2,1,0:T(8,128)S(1)}, u32[]{:S(2)}, u32[]{:S(2)}) collective-permute-start(f32[16,8,128]{2,1,0:T(8,128)S(1)} %get-tuple-element.100), channel_id=1, source_target_pairs={{0,1},{1,0},{2,3},{3,2},{4,5},{5,4},{6,7},{7,6},{8,9},{9,8},{10,11... | collective-permute-start | bytes 196616 | tf_op jit(solution)/shard_map/ppermute | solution.py:451
  50.7 0.0 collective-permute-done.24.refs_2_.refs_6_
  50.7 0.1 collective-permute-start.15
  50.8 0.5 collective-permute-start.16
  51.3 1.3 %collective-permute-start.17 = (f32[16,8,128]{2,1,0:T(8,128)S(1)}, f32[16,8,128]{2,1,0:T(8,128)S(1)}, u32[]{:S(2)}, u32[]{:S(2)}) collective-permute-start(f32[16,8,128]{2,1,0:T(8,128)S(1)} %get-tuple-element.108), channel_id=1, source_target_pairs={{0,3},{1,2},{2,1},{3,0},{4,7},{5,6},{6,5},{7,4},{8,11},{9,10},{10,... | collective-permute-start | bytes 196616 | tf_op jit(solution)/shard_map/ppermute | solution.py:451
  52.6 0.7 collective-permute-done.30.refs_4_
  53.3 0.6 collective-permute-start.32
  53.9 0.0 collective-permute-done.11.refs_2_
  53.9 3.8 %collective-permute-start.27 = (f32[33,8,128]{2,1,0:T(8,128)S(1)}, f32[33,8,128]{2,1,0:T(8,128)S(1)}, u32[]{:S(2)}, u32[]{:S(2)}) collective-permute-start(f32[33,8,128]{2,1,0:T(8,128)S(1)} %get-tuple-element.136), channel_id=1, source_target_pairs={{0,12},{1,13},{2,14},{3,15},{4,8},{5,9},{6,10},{7,11},{8,4},{9,5},... | collective-permute-start | bytes 405512 | tf_op jit(solution)/shard_map/ppermute | solution.py:451
  57.7 0.0 collective-permute-done.16.refs_3_
  57.7 0.2 collective-permute-start.12
  57.9 0.0 collective-permute-done.17.refs_4_
  57.9 0.5 collective-permute-start.13
  58.4 1.0 %shard_map.138 = (f32[128,16]{1,0:T(8,128)S(1)}, f32[128,128]{1,0:T(8,128)S(1)}) custom-call(s32[1]{0:T(128)} %bitcast.refs_0_, f32[128,1024]{1,0:T(8,128)S(1)} %get-tuple-element.115.refs_1_, f32[128,1024]{1,0:T(8,128)S(1)} %get-tuple-element.126.refs_2_, f32[128,1024]{1,0:T(8,128)S(1)} %get-tuple-element.127.refs_3_, ...), custom_call_target="tpu_custom_call" | custom-call | flops 402653184 | bytes 2170880 | tf_op jit(solution)/shard_map/pallas_call | solution.py:242
  59.4 0.4 shard_map.134
  59.9 2.5 %collective-permute-done.12.refs_3_ = f32[16,8,128]{2,1,0:T(8,128)S(1)} collective-permute-done((f32[16,8,128]{2,1,0:T(8,128)S(1)}, f32[16,8,128]{2,1,0:T(8,128)S(1)}, u32[]{:S(2)}, u32[]{:S(2)}) %collective-permute-start.12) | collective-permute-done | bytes 65568 | tf_op jit(solution)/shard_map/ppermute | solution.py:451
  62.3 0.0 collective-permute-done.13.refs_4_
  62.3 0.8 %shard_map.135 = (f32[128,1024]{1,0:T(8,128)S(1)}, f32[128,16]{1,0:T(8,128)S(1)}) custom-call(s32[1]{0:T(128)} %bitcast.refs_0_, f32[16,8,128]{2,1,0:T(8,128)S(1)} %get-tuple-element.99.refs_1_, f32[16,8,128]{2,1,0:T(8,128)S(1)} %collective-permute-done.11.refs_2_, f32[16,8,128]{2,1,0:T(8,128)S(1)} %collective-permute-done.12.refs_3_, ...), custom_call_target="tpu_custom_call" | custom-call | flops 201326592 | bytes 2531328 | tf_op jit(solution)/shard_map/pallas_call | solution.py:242
  63.1 3.3 %collective-permute-done.32.refs_2_.refs_8_ = f32[33,8,128]{2,1,0:T(8,128)S(1)} collective-permute-done((f32[33,8,128]{2,1,0:T(8,128)S(1)}, f32[33,8,128]{2,1,0:T(8,128)S(1)}, u32[]{:S(2)}, u32[]{:S(2)}) %collective-permute-start.32) | collective-permute-done | bytes 135200 | tf_op jit(solution)/shard_map/ppermute | solution.py:451
  66.4 0.4 shard_map.141
  66.9 0.2 collective-permute-done.31.refs_6_
  67.0 1.5 %shard_map.142 = (f32[128,1024]{1,0:T(8,128)}, f32[128,16]{1,0:T(8,128)}, f32[128,128]{1,0:T(8,128)}, f32[128,16]{1,0:T(8,128)}, f32[128,1024]{1,0:T(8,128)}, /*index=5*/f32[1,128]{1,0:T(1,128)}, f32[128,128]{1,0:T(8,128)}) custom-call(s32[1]{0:T(128)} %bitcast.refs_0_, f32[128,1024]{1,0:T(8,128)S(1)} %get-tuple-element.114.refs_1_, ...), custom_call_target="tpu_custom_call" | custom-call | flops 201326592 | bytes 4674560 | tf_op jit(solution)/shard_map/pallas_call | solution.py:242
  (33 shorter events, 0.2 us)
Async XLA Ops:
  0.6 7.3 %copy-start.1 = (f32[128,1024]{1,0:T(8,128)S(1)}, f32[128,1024]{1,0:T(8,128)}, u32[]{:S(2)}) copy-start(f32[128,1024]{1,0:T(8,128)} %refs_3_.1) | copy-start | bytes 1572868
  0.6 7.3 %copy-start.6 = (f32[8,16,16]{2,1,0:T(8,128)S(1)}, f32[8,16,16]{2,1,0:T(8,128)}, u32[]{:S(2)}) copy-start(f32[8,16,16]{2,1,0:T(8,128)} %param.13) | copy-start | bytes 24580
  2.2 14.4 %collective-permute-start = (f32[33,8,128]{2,1,0:T(8,128)S(1)}, f32[33,8,128]{2,1,0:T(8,128)S(1)}, u32[]{:S(2)}, u32[]{:S(2)}) collective-permute-start(f32[33,8,128]{2,1,0:T(8,128)S(1)} %get-tuple-element.84), channel_id=1, source_target_pairs={{0,8},{1,9},{2,10},{3,11},{4,12},{5,13},{6,14},{7,15},{8,0},{9,1},... | collective-permute-start | bytes 405512 | tf_op jit(solution)/shard_map/ppermute | solution.py:451
  6.3 10.3 %collective-permute-start.4 = (f32[33,8,128]{2,1,0:T(8,128)S(1)}, f32[33,8,128]{2,1,0:T(8,128)S(1)}, u32[]{:S(2)}, u32[]{:S(2)}) collective-permute-start(f32[33,8,128]{2,1,0:T(8,128)S(1)} %get-tuple-element.89), channel_id=1, source_target_pairs={{0,12},{1,13},{2,14},{3,15},{4,8},{5,9},{6,10},{7,11},{8,4},{9,5},... | collective-permute-start | bytes 405512 | tf_op jit(solution)/shard_map/ppermute | solution.py:451
  7.7 11.0 %collective-permute-start.5 = (f32[33,8,128]{2,1,0:T(8,128)S(1)}, f32[33,8,128]{2,1,0:T(8,128)S(1)}, u32[]{:S(2)}, u32[]{:S(2)}) collective-permute-start(f32[33,8,128]{2,1,0:T(8,128)S(1)} %get-tuple-element.90), channel_id=1, source_target_pairs={{0,4},{1,5},{2,6},{3,7},{4,0},{5,1},{6,2},{7,3},{8,12},{9,13},{10,... | collective-permute-start | bytes 405512 | tf_op jit(solution)/shard_map/ppermute | solution.py:451
  8.6 10.3 %collective-permute-start.18 = (f32[32,8,128]{2,1,0:T(8,128)S(1)}, f32[32,8,128]{2,1,0:T(8,128)S(1)}, u32[]{:S(2)}, u32[]{:S(2)}) collective-permute-start(f32[32,8,128]{2,1,0:T(8,128)S(1)} %get-tuple-element.117), channel_id=1, source_target_pairs={{0,1},{1,0},{2,3},{3,2},{4,5},{5,4},{6,7},{7,6},{8,9},{9,8},{10,11... | collective-permute-start | bytes 393224 | tf_op jit(solution)/shard_map/ppermute | solution.py:451
  8.6 10.3 %collective-permute-start.19 = (f32[32,8,128]{2,1,0:T(8,128)S(1)}, f32[32,8,128]{2,1,0:T(8,128)S(1)}, u32[]{:S(2)}, u32[]{:S(2)}) collective-permute-start(f32[32,8,128]{2,1,0:T(8,128)S(1)} %get-tuple-element.118), channel_id=1, source_target_pairs={{0,2},{1,3},{2,0},{3,1},{4,6},{5,7},{6,4},{7,5},{8,10},{9,11},{10,... | collective-permute-start | bytes 393224 | tf_op jit(solution)/shard_map/ppermute | solution.py:451
  16.6 5.4 %collective-permute-start.20 = (f32[32,8,128]{2,1,0:T(8,128)S(1)}, f32[32,8,128]{2,1,0:T(8,128)S(1)}, u32[]{:S(2)}, u32[]{:S(2)}) collective-permute-start(f32[32,8,128]{2,1,0:T(8,128)S(1)} %get-tuple-element.119), channel_id=1, source_target_pairs={{0,3},{1,2},{2,1},{3,0},{4,7},{5,6},{6,5},{7,4},{8,11},{9,10},{10,... | collective-permute-start | bytes 393224 | tf_op jit(solution)/shard_map/ppermute | solution.py:451
  16.6 5.7 %collective-permute-start.1 = (f32[16,8,128]{2,1,0:T(8,128)S(1)}, f32[16,8,128]{2,1,0:T(8,128)S(1)}, u32[]{:S(2)}, u32[]{:S(2)}) collective-permute-start(f32[16,8,128]{2,1,0:T(8,128)S(1)} %get-tuple-element.86), channel_id=1, source_target_pairs={{0,1},{1,0},{2,3},{3,2},{4,5},{5,4},{6,7},{7,6},{8,9},{9,8},{10,11... | collective-permute-start | bytes 196616 | tf_op jit(solution)/shard_map/ppermute | solution.py:451
  18.6 9.6 %copy-start = (f32[128,1024]{1,0:T(8,128)S(1)}, f32[128,1024]{1,0:T(8,128)}, u32[]{:S(2)}) copy-start(f32[128,1024]{1,0:T(8,128)} %refs_9_.1) | copy-start | bytes 1572868
  18.6 7.1 %collective-permute-start.2 = (f32[16,8,128]{2,1,0:T(8,128)S(1)}, f32[16,8,128]{2,1,0:T(8,128)S(1)}, u32[]{:S(2)}, u32[]{:S(2)}) collective-permute-start(f32[16,8,128]{2,1,0:T(8,128)S(1)} %get-tuple-element.87), channel_id=1, source_target_pairs={{0,2},{1,3},{2,0},{3,1},{4,6},{5,7},{6,4},{7,5},{8,10},{9,11},{10,... | collective-permute-start | bytes 196616 | tf_op jit(solution)/shard_map/ppermute | solution.py:451
  18.9 9.3 %collective-permute-start.6 = (f32[17,8,128]{2,1,0:T(8,128)S(1)}, f32[17,8,128]{2,1,0:T(8,128)S(1)}, u32[]{:S(2)}, u32[]{:S(2)}) collective-permute-start(f32[17,8,128]{2,1,0:T(8,128)S(1)} %get-tuple-element.92), channel_id=1, source_target_pairs={{0,1},{1,0},{2,3},{3,2},{4,5},{5,4},{6,7},{7,6},{8,9},{9,8},{10,11... | collective-permute-start | bytes 208904 | tf_op jit(solution)/shard_map/ppermute | solution.py:451
  19.0 7.7 %collective-permute-start.3 = (f32[16,8,128]{2,1,0:T(8,128)S(1)}, f32[16,8,128]{2,1,0:T(8,128)S(1)}, u32[]{:S(2)}, u32[]{:S(2)}) collective-permute-start(f32[16,8,128]{2,1,0:T(8,128)S(1)} %get-tuple-element.88), channel_id=1, source_target_pairs={{0,3},{1,2},{2,1},{3,0},{4,7},{5,6},{6,5},{7,4},{8,11},{9,10},{10,... | collective-permute-start | bytes 196616 | tf_op jit(solution)/shard_map/ppermute | solution.py:451
  22.0 6.2 %copy-start.2 = (f32[1,128,128]{2,1,0:T(8,128)S(1)}, f32[1,128,128]{2,1,0:T(8,128)}, u32[]{:S(2)}) copy-start(f32[1,128,128]{2,1,0:T(8,128)} %param.10) | copy-start | bytes 196612
  22.0 6.2 %copy-start.3 = (f32[8,16,16]{2,1,0:T(8,128)S(1)}, f32[8,16,16]{2,1,0:T(8,128)}, u32[]{:S(2)}) copy-start(f32[8,16,16]{2,1,0:T(8,128)} %param.11) | copy-start | bytes 24580
  22.0 14.4 %collective-permute-start.21 = (f32[32,8,128]{2,1,0:T(8,128)S(1)}, f32[32,8,128]{2,1,0:T(8,128)S(1)}, u32[]{:S(2)}, u32[]{:S(2)}) collective-permute-start(f32[32,8,128]{2,1,0:T(8,128)S(1)} %get-tuple-element.121), channel_id=1, source_target_pairs={{0,4},{1,5},{2,6},{3,7},{4,0},{5,1},{6,2},{7,3},{8,12},{9,13},{10,... | collective-permute-start | bytes 393224 | tf_op jit(solution)/shard_map/ppermute | solution.py:451
  22.4 15.6 %collective-permute-start.22 = (f32[32,8,128]{2,1,0:T(8,128)S(1)}, f32[32,8,128]{2,1,0:T(8,128)S(1)}, u32[]{:S(2)}, u32[]{:S(2)}) collective-permute-start(f32[32,8,128]{2,1,0:T(8,128)S(1)} %get-tuple-element.122), channel_id=1, source_target_pairs={{0,8},{1,9},{2,10},{3,11},{4,12},{5,13},{6,14},{7,15},{8,0},{9,1},... | collective-permute-start | bytes 393224 | tf_op jit(solution)/shard_map/ppermute | solution.py:451
  25.7 12.2 %collective-permute-start.23 = (f32[32,8,128]{2,1,0:T(8,128)S(1)}, f32[32,8,128]{2,1,0:T(8,128)S(1)}, u32[]{:S(2)}, u32[]{:S(2)}) collective-permute-start(f32[32,8,128]{2,1,0:T(8,128)S(1)} %get-tuple-element.123), channel_id=1, source_target_pairs={{0,12},{1,13},{2,14},{3,15},{4,8},{5,9},{6,10},{7,11},{8,4},{9,5},... | collective-permute-start | bytes 393224 | tf_op jit(solution)/shard_map/ppermute | solution.py:451
  26.7 4.3 %collective-permute-start.7 = (f32[17,8,128]{2,1,0:T(8,128)S(1)}, f32[17,8,128]{2,1,0:T(8,128)S(1)}, u32[]{:S(2)}, u32[]{:S(2)}) collective-permute-start(f32[17,8,128]{2,1,0:T(8,128)S(1)} %get-tuple-element.93), channel_id=1, source_target_pairs={{0,2},{1,3},{2,0},{3,1},{4,6},{5,7},{6,4},{7,5},{8,10},{9,11},{10,... | collective-permute-start | bytes 208904 | tf_op jit(solution)/shard_map/ppermute | solution.py:451
  28.2 4.3 %collective-permute-start.8 = (f32[17,8,128]{2,1,0:T(8,128)S(1)}, f32[17,8,128]{2,1,0:T(8,128)S(1)}, u32[]{:S(2)}, u32[]{:S(2)}) collective-permute-start(f32[17,8,128]{2,1,0:T(8,128)S(1)} %get-tuple-element.94), channel_id=1, source_target_pairs={{0,3},{1,2},{2,1},{3,0},{4,7},{5,6},{6,5},{7,4},{8,11},{9,10},{10,... | collective-permute-start | bytes 208904 | tf_op jit(solution)/shard_map/ppermute | solution.py:451
  28.2 0.7 copy-start.5
  28.9 3.6 %copy-start.4 = (f32[1,128,128]{2,1,0:T(8,128)S(1)}, f32[1,128,128]{2,1,0:T(8,128)}, u32[]{:S(2)}) copy-start(f32[1,128,128]{2,1,0:T(8,128)} %param.12) | copy-start | bytes 196612
  33.5 8.2 %collective-permute-start.9 = (f32[32,8,128]{2,1,0:T(8,128)S(1)}, f32[32,8,128]{2,1,0:T(8,128)S(1)}, u32[]{:S(2)}, u32[]{:S(2)}) collective-permute-start(f32[32,8,128]{2,1,0:T(8,128)S(1)} %get-tuple-element.97), channel_id=1, source_target_pairs={{0,12},{1,13},{2,14},{3,15},{4,8},{5,9},{6,10},{7,11},{8,4},{9,5},... | collective-permute-start | bytes 393224 | tf_op jit(solution)/shard_map/ppermute | solution.py:451
  36.4 7.5 %collective-permute-start.10 = (f32[32,8,128]{2,1,0:T(8,128)S(1)}, f32[32,8,128]{2,1,0:T(8,128)S(1)}, u32[]{:S(2)}, u32[]{:S(2)}) collective-permute-start(f32[32,8,128]{2,1,0:T(8,128)S(1)} %get-tuple-element.98), channel_id=1, source_target_pairs={{0,4},{1,5},{2,6},{3,7},{4,0},{5,1},{6,2},{7,3},{8,12},{9,13},{10,... | collective-permute-start | bytes 393224 | tf_op jit(solution)/shard_map/ppermute | solution.py:451
  36.4 12.5 %collective-permute-start.14 = (f32[32,8,128]{2,1,0:T(8,128)S(1)}, f32[32,8,128]{2,1,0:T(8,128)S(1)}, u32[]{:S(2)}, u32[]{:S(2)}) collective-permute-start(f32[32,8,128]{2,1,0:T(8,128)S(1)} %get-tuple-element.104), channel_id=1, source_target_pairs={{0,8},{1,9},{2,10},{3,11},{4,12},{5,13},{6,14},{7,15},{8,0},{9,1},... | collective-permute-start | bytes 393224 | tf_op jit(solution)/shard_map/ppermute | solution.py:451
  38.6 1.3 %collective-permute-start.28 = (f32[16,8,128]{2,1,0:T(8,128)S(1)}, f32[16,8,128]{2,1,0:T(8,128)S(1)}, u32[]{:S(2)}, u32[]{:S(2)}) collective-permute-start(f32[16,8,128]{2,1,0:T(8,128)S(1)} %get-tuple-element.138), channel_id=1, source_target_pairs={{0,1},{1,0},{2,3},{3,2},{4,5},{5,4},{6,7},{7,6},{8,9},{9,8},{10,11... | collective-permute-start | bytes 196616 | tf_op jit(solution)/shard_map/ppermute | solution.py:451
  38.7 12.0 %collective-permute-start.24 = (f32[17,8,128]{2,1,0:T(8,128)S(1)}, f32[17,8,128]{2,1,0:T(8,128)S(1)}, u32[]{:S(2)}, u32[]{:S(2)}) collective-permute-start(f32[17,8,128]{2,1,0:T(8,128)S(1)} %get-tuple-element.133), channel_id=1, source_target_pairs={{0,1},{1,0},{2,3},{3,2},{4,5},{5,4},{6,7},{7,6},{8,9},{9,8},{10,11... | collective-permute-start | bytes 208904 | tf_op jit(solution)/shard_map/ppermute | solution.py:451
  39.9 9.4 %collective-permute-start.29 = (f32[16,8,128]{2,1,0:T(8,128)S(1)}, f32[16,8,128]{2,1,0:T(8,128)S(1)}, u32[]{:S(2)}, u32[]{:S(2)}) collective-permute-start(f32[16,8,128]{2,1,0:T(8,128)S(1)} %get-tuple-element.139), channel_id=1, source_target_pairs={{0,2},{1,3},{2,0},{3,1},{4,6},{5,7},{6,4},{7,5},{8,10},{9,11},{10,... | collective-permute-start | bytes 196616 | tf_op jit(solution)/shard_map/ppermute | solution.py:451
  41.7 9.1 %collective-permute-start.25 = (f32[17,8,128]{2,1,0:T(8,128)S(1)}, f32[17,8,128]{2,1,0:T(8,128)S(1)}, u32[]{:S(2)}, u32[]{:S(2)}) collective-permute-start(f32[17,8,128]{2,1,0:T(8,128)S(1)} %get-tuple-element.134), channel_id=1, source_target_pairs={{0,2},{1,3},{2,0},{3,1},{4,6},{5,7},{6,4},{7,5},{8,10},{9,11},{10,... | collective-permute-start | bytes 208904 | tf_op jit(solution)/shard_map/ppermute | solution.py:451
  43.9 7.4 %collective-permute-start.26 = (f32[17,8,128]{2,1,0:T(8,128)S(1)}, f32[17,8,128]{2,1,0:T(8,128)S(1)}, u32[]{:S(2)}, u32[]{:S(2)}) collective-permute-start(f32[17,8,128]{2,1,0:T(8,128)S(1)} %get-tuple-element.135), channel_id=1, source_target_pairs={{0,3},{1,2},{2,1},{3,0},{4,7},{5,6},{6,5},{7,4},{8,11},{9,10},{10,... | collective-permute-start | bytes 208904 | tf_op jit(solution)/shard_map/ppermute | solution.py:451
  48.9 4.3 %collective-permute-start.30 = (f32[16,8,128]{2,1,0:T(8,128)S(1)}, f32[16,8,128]{2,1,0:T(8,128)S(1)}, u32[]{:S(2)}, u32[]{:S(2)}) collective-permute-start(f32[16,8,128]{2,1,0:T(8,128)S(1)} %get-tuple-element.140), channel_id=1, source_target_pairs={{0,3},{1,2},{2,1},{3,0},{4,7},{5,6},{6,5},{7,4},{8,11},{9,10},{10,... | collective-permute-start | bytes 196616 | tf_op jit(solution)/shard_map/ppermute | solution.py:451
  49.4 4.5 %collective-permute-start.11 = (f32[16,8,128]{2,1,0:T(8,128)S(1)}, f32[16,8,128]{2,1,0:T(8,128)S(1)}, u32[]{:S(2)}, u32[]{:S(2)}) collective-permute-start(f32[16,8,128]{2,1,0:T(8,128)S(1)} %get-tuple-element.100), channel_id=1, source_target_pairs={{0,1},{1,0},{2,3},{3,2},{4,5},{5,4},{6,7},{7,6},{8,9},{9,8},{10,11... | collective-permute-start | bytes 196616 | tf_op jit(solution)/shard_map/ppermute | solution.py:451
  50.7 7.0 %collective-permute-start.15 = (f32[16,8,128]{2,1,0:T(8,128)S(1)}, f32[16,8,128]{2,1,0:T(8,128)S(1)}, u32[]{:S(2)}, u32[]{:S(2)}) collective-permute-start(f32[16,8,128]{2,1,0:T(8,128)S(1)} %get-tuple-element.106), channel_id=1, source_target_pairs={{0,1},{1,0},{2,3},{3,2},{4,5},{5,4},{6,7},{7,6},{8,9},{9,8},{10,11... | collective-permute-start | bytes 196616 | tf_op jit(solution)/shard_map/ppermute | solution.py:451
  50.8 6.9 %collective-permute-start.16 = (f32[16,8,128]{2,1,0:T(8,128)S(1)}, f32[16,8,128]{2,1,0:T(8,128)S(1)}, u32[]{:S(2)}, u32[]{:S(2)}) collective-permute-start(f32[16,8,128]{2,1,0:T(8,128)S(1)} %get-tuple-element.107), channel_id=1, source_target_pairs={{0,2},{1,3},{2,0},{3,1},{4,6},{5,7},{6,4},{7,5},{8,10},{9,11},{10,... | collective-permute-start | bytes 196616 | tf_op jit(solution)/shard_map/ppermute | solution.py:451
  51.3 6.6 %collective-permute-start.17 = (f32[16,8,128]{2,1,0:T(8,128)S(1)}, f32[16,8,128]{2,1,0:T(8,128)S(1)}, u32[]{:S(2)}, u32[]{:S(2)}) collective-permute-start(f32[16,8,128]{2,1,0:T(8,128)S(1)} %get-tuple-element.108), channel_id=1, source_target_pairs={{0,3},{1,2},{2,1},{3,0},{4,7},{5,6},{6,5},{7,4},{8,11},{9,10},{10,... | collective-permute-start | bytes 196616 | tf_op jit(solution)/shard_map/ppermute | solution.py:451
  53.3 13.2 %collective-permute-start.32 = (f32[33,8,128]{2,1,0:T(8,128)S(1)}, f32[33,8,128]{2,1,0:T(8,128)S(1)}, u32[]{:S(2)}, u32[]{:S(2)}) collective-permute-start(f32[33,8,128]{2,1,0:T(8,128)S(1)} %get-tuple-element.143), channel_id=1, source_target_pairs={{0,8},{1,9},{2,10},{3,11},{4,12},{5,13},{6,14},{7,15},{8,0},{9,1},... | collective-permute-start | bytes 405512 | tf_op jit(solution)/shard_map/ppermute | solution.py:451
  53.9 13.0 %collective-permute-start.27 = (f32[33,8,128]{2,1,0:T(8,128)S(1)}, f32[33,8,128]{2,1,0:T(8,128)S(1)}, u32[]{:S(2)}, u32[]{:S(2)}) collective-permute-start(f32[33,8,128]{2,1,0:T(8,128)S(1)} %get-tuple-element.136), channel_id=1, source_target_pairs={{0,12},{1,13},{2,14},{3,15},{4,8},{5,9},{6,10},{7,11},{8,4},{9,5},... | collective-permute-start | bytes 405512 | tf_op jit(solution)/shard_map/ppermute | solution.py:451
  57.7 9.4 %collective-permute-start.31 = (f32[33,8,128]{2,1,0:T(8,128)S(1)}, f32[33,8,128]{2,1,0:T(8,128)S(1)}, u32[]{:S(2)}, u32[]{:S(2)}) collective-permute-start(f32[33,8,128]{2,1,0:T(8,128)S(1)} %get-tuple-element.141), channel_id=1, source_target_pairs={{0,4},{1,5},{2,6},{3,7},{4,0},{5,1},{6,2},{7,3},{8,12},{9,13},{10,... | collective-permute-start | bytes 405512 | tf_op jit(solution)/shard_map/ppermute | solution.py:451
  57.7 4.6 %collective-permute-start.12 = (f32[16,8,128]{2,1,0:T(8,128)S(1)}, f32[16,8,128]{2,1,0:T(8,128)S(1)}, u32[]{:S(2)}, u32[]{:S(2)}) collective-permute-start(f32[16,8,128]{2,1,0:T(8,128)S(1)} %get-tuple-element.101), channel_id=1, source_target_pairs={{0,2},{1,3},{2,0},{3,1},{4,6},{5,7},{6,4},{7,5},{8,10},{9,11},{10,... | collective-permute-start | bytes 196616 | tf_op jit(solution)/shard_map/ppermute | solution.py:451
  57.9 4.4 %collective-permute-start.13 = (f32[16,8,128]{2,1,0:T(8,128)S(1)}, f32[16,8,128]{2,1,0:T(8,128)S(1)}, u32[]{:S(2)}, u32[]{:S(2)}) collective-permute-start(f32[16,8,128]{2,1,0:T(8,128)S(1)} %get-tuple-element.102), channel_id=1, source_target_pairs={{0,3},{1,2},{2,1},{3,0},{4,7},{5,6},{6,5},{7,4},{8,11},{9,10},{10,... | collective-permute-start | bytes 196616 | tf_op jit(solution)/shard_map/ppermute | solution.py:451

commit v2 on v1

--- a/solution.py
+++ b/solution.py
@@ -16,6 +16,7 @@
 SUB = 8
 LANE = 128
 KERNEL_VMEM = 16 << 20
+LOADS = 1
 
 
 def gelu_value(values):
@@ -151,12 +152,18 @@
     return keys[: count // 2], keys[count // 2 :]
 
 
+def back_keys(count):
+    places = send_order(count)
+    return [places[0], *places[count // 2 :]], [*places[1 : count // 2], 0]
+
+
 class Plan:
     def __init__(self, count, features, tokens):
         self.count, self.features, self.tokens = count, features, tokens
         self.inner, self.outer = stages(count)
         self.early, self.late = early_keys(self.outer)
         self.far, self.near = range(self.outer // 2, self.outer), range(self.outer // 2)
+        self.sooner, self.later = back_keys(self.outer)
         self.rows = features // count
         self.chunks = tokens // LANE
         self.block_tiles = self.rows // SUB * self.chunks
@@ -199,6 +206,17 @@
     def line_spans(self, keys):
         return [(i, m, k, m) for i, k in enumerate(keys) for m in range(self.inner)]
 
+    def sent_spans(self):
+        return [(k, m, k, m) for k in range(self.outer) for m in range(self.inner)]
+
+    def put_slots(self, values, messages, chunk):
+        for place, (i, slot, _, _) in enumerate(self.sent_spans()):
+            for r in range(self.rows // SUB):
+                start = place * self.rows + r * SUB
+                for c in range(values.shape[1] // LANE):
+                    tile = slot * self.block_tiles + r * self.chunks + chunk + c
+                    messages[i][tile] = values[start : start + SUB, c * LANE : (c + 1) * LANE]
+
     def line_up(self, parts, spans, target):
         for place, (i, slot, _, _) in enumerate(spans):
             for t, r, c in self.tiles():
@@ -233,7 +251,7 @@
     def sums_row(self, tiles):
         return jnp.concatenate([tiles[c // SUB, c % SUB : c % SUB + 1, :] for c in range(self.chunks)], axis=1)
 
-    def call(self, kernel, outs, me, *args, scratch=(), flops=0, loads=False, stores=0, **fixed):
+    def call(self, kernel, outs, me, *args, scratch=(), flops=0, loads=0, stores=0, **fixed):
         outs = tuple(o if isinstance(o, jax.ShapeDtypeStruct) else jax.ShapeDtypeStruct(o, jnp.float32) for o in outs)
         if loads:
             args = [pltpu.with_memory_space_constraint(a, pltpu.HBM) for a in args]
@@ -246,7 +264,7 @@
             + [pl.BlockSpec(memory_space=pltpu.HBM) if loads else vmem] * len(args),
             out_specs=(pl.BlockSpec(memory_space=pl.ANY),) * stores + (vmem,) * (len(outs) - stores),
             scratch_shapes=[pltpu.VMEM(s, jnp.float32) for s in scratch]
-            + ([pltpu.VMEM(a.shape, a.dtype) for a in args] + [pltpu.SemaphoreType.DMA((len(args),))] if loads else [])
+            + ([pltpu.VMEM(a.shape, a.dtype) for a in args] + [pltpu.SemaphoreType.DMA((loads,))] if loads else [])
             + ([pltpu.SemaphoreType.DMA((stores,))] if stores else []),
             cost_estimate=pl.CostEstimate(flops=flops, bytes_accessed=moved, transcendentals=0),
             compiler_params=pltpu.CompilerParams(vmem_limit_bytes=KERNEL_VMEM),
@@ -258,20 +276,27 @@
 
 
 def first_one(plan, n_in, n_out, *refs):
-    me, sources, outs, (held, x, left, gain, arrived) = split_refs(n_in, n_out, refs)
-    z, p = me[0] // plan.inner, me[0] % plan.inner
-    loads = [pltpu.make_async_copy(s, t, arrived.at[i]) for i, (s, t) in enumerate(zip(sources, (x, left, gain)))]
+    me, sources, outs, (turned, x, left, gain, arrived) = split_refs(n_in, n_out, refs)
+    z, p = me[0] // plan.inner, me[0] % plan.inner
+    width = plan.tokens // LOADS
+    spans = [slice(i * width, (i + 1) * width) for i in range(LOADS)]
+    loads = [pltpu.make_async_copy(s, t, arrived.at[i]) for i, (s, t) in enumerate(zip(sources[1:], (left, gain)))]
+    loads += [pltpu.make_async_copy(sources[0].at[:, c], x.at[:, c], arrived.at[2 + i]) for i, c in enumerate(spans)]
     for load in loads:
         load.start()
-    for load in loads:
-        load.wait()
-    values = x[...]
-    held[...] = matmul(left[...].T * gain[...], values)
-    squares = jnp.sum(values * values, axis=0, keepdims=True)
-    for k in range(plan.outer):
-        for m in range(plan.inner):
-            plan.put_block(held, (z ^ k) * plan.inner + (p ^ m), outs[k], m)
-        plan.put_sums(squares, outs[k], plan.inner)
+    loads[0].wait()
+    loads[1].wait()
+    turned[...] = left[...].T * gain[...]
+    weights = plan.gather_rows(turned, plan.sent_spans(), z, p)
+    squares = []
+    for i, c in enumerate(spans):
+        loads[2 + i].wait()
+        values = x[:, c]
+        plan.put_slots(matmul(weights, values), outs, i * width // LANE)
+        squares.append(jnp.sum(values * values, axis=0, keepdims=True))
+    squares = jnp.concatenate(squares, axis=1)
+    for out in outs:
+        plan.put_sums(squares, out, plan.inner)
 
 
 def widen(plan, right):
@@ -300,8 +325,9 @@
     wide_two = widen(plan, right_two[...])
     held[...] = matmul(wide_two, cotangent[...])
     for m in range(plan.inner):
-        for k in range(plan.outer):
-            plan.put_block(held, (z ^ k) * plan.inner + (p ^ m), outs[m], k)
+        for message, keys in ((outs[m], plan.far), (outs[plan.inner + m], plan.near)):
+            for slot, k in enumerate(keys):
+                plan.put_block(held, (z ^ k) * plan.inner + (p ^ m), message, slot)
     outs[-1][...] = wide_two
 
 
@@ -365,10 +391,10 @@
     inner = jnp.sum(dpre * pre[...], axis=0, keepdims=True)
     held[...] = matmul(wide_one[...], dpre)
     for m in range(plan.inner):
-        for message, keys in ((outs[m], plan.far), (outs[plan.inner + m], plan.near)):
+        for message, keys in ((outs[m], plan.sooner), (outs[plan.inner + m], plan.later)):
             for slot, k in enumerate(keys):
                 plan.put_block(held, (z ^ k) * plan.inner + (p ^ m), message, slot)
-        plan.put_sums(inner, outs[m], len(plan.far))
+        plan.put_sums(inner, outs[m], len(plan.sooner))
     outs[-2][...] = back
     outs[-1][...] = dpre
 
@@ -468,13 +494,14 @@
     early, late, far, near = plan.early, plan.late, plan.far, plan.near
 
     sent = call(
-        first_one, [message(inner, True)] * outer, activations, one, gain_row, scratch=[full], flops=cost, loads=True
+        first_one, [message(inner, True)] * outer, activations, one, gain_row, scratch=[square], flops=cost, loads=LOADS + 2
     )
     first = over_outer(line, sent)
     *sent, wide_two = call(
-        back_two, [message(outer, False)] * inner + [square], cotangent, flat_two, scratch=[full], flops=cost
-    )
-    dy2_half = over_inner(sent)
+        back_two, [message(len(far), False)] * inner + [message(len(near), False)] * inner + [square],
+        cotangent, flat_two, scratch=[full], flops=cost,
+    )
+    dy2_far, dy2_near = over_inner(sent[:inner]), over_inner(sent[inner:])
     half, stacked = (features // 2, tokens), jax.ShapeDtypeStruct((features, 2 * features), jnp.bfloat16)
     pair = jax.ShapeDtypeStruct((2 * features, tokens), jnp.bfloat16)
     wide_one, turned_one, gain_kept, scaled_early, scaled_late, wide_early, wide_late, x_pair, cotangent_pair = call(
@@ -483,8 +510,10 @@
     )
     sent = call(regroup, [message(len(early), False)] * inner, *(first[k] for k in early), data=len(early))
     first_early = over_inner(sent)
-    sent = call(regroup, [message(inner, False)] * outer, *dy2_half, data=inner)
-    dy2_parts = over_outer(line, sent)
+    sent = call(regroup, [message(inner, False)] * len(far), *dy2_far, data=inner)
+    dy2_parts = over_outer(far, sent)
+    sent = call(regroup, [message(inner, False)] * len(near), *dy2_near, data=inner)
+    dy2_parts |= over_outer(near, sent)
     sent = call(regroup, [message(len(late), True)] * inner, *(first[k] for k in (*late, *early)), data=len(late))
     first_late = over_inner(sent)
     *sent, y1, pre, act, slope, inverse_root = call(
@@ -493,14 +522,14 @@
     )
     second_half = over_outer(line, sent)
     *sent, dy2, dpre = call(
-        back_one, [message(len(far), True)] * inner + [message(len(near), False)] * inner + [full] * 2,
+        back_one, [message(len(plan.sooner), True)] * inner + [message(len(plan.later), False)] * inner + [full] * 2,
         *(dy2_parts[k] for k in line), two, wide_one, pre, slope, scratch=[full] * 2, flops=2 * cost,
     )
-    dy1_far, dy1_near = over_inner(sent[:inner]), over_inner(sent[inner:])
-    sent = call(regroup, [message(inner, True)] * len(far), *dy1_far, data=inner)
-    dy1_parts = over_outer(far, sent)
-    sent = call(regroup, [message(inner, True)] * len(near), *dy1_near, *dy1_far, data=inner)
-    dy1_parts |= over_outer(near, sent)
+    dy1_sooner, dy1_later = over_inner(sent[:inner]), over_inner(sent[inner:])
+    sent = call(regroup, [message(inner, True)] * len(plan.sooner), *dy1_sooner, data=inner)
+    dy1_parts = over_outer(plan.sooner, sent)
+    sent = call(regroup, [message(inner, True)] * len(plan.later), *dy1_later, *dy1_sooner, data=inner)
+    dy1_parts |= over_outer(plan.later, sent)
     sent = call(regroup, [message(len(early), False)] * inner, *(second_half[k] for k in early), data=len(early))
     second_early = over_inner(sent)
     sent = call(regroup, [message(len(late), False)] * inner, *(second_half[k] for k in late), data=len(late))

time: 68.7 us -> 70.9 us (1.032)
  local copies, waits for them, and re-layouts: 0.65 us -> 2.51 us
  starting transfers between devices: 34.5 us -> 35.6 us
  waiting for transfers between devices: 23.8 us -> 23 us
    unnamed x14 -> x16, local copies, waits for them, and re-layouts: 0.65 us -> 2.51 us
    ppermute x33 -> x36, starting transfers between devices: 34.5 us -> 35.6 us  [across(): lax.ppermute(messages[i], 'blocks', [(s, s ^ i * step) for s in range(cou...]
    ppermute x33 -> x36, waiting for transfers between devices: 23.8 us -> 23 us  [across(): lax.ppermute(messages[i], 'blocks', [(s, s ^ i * step) for s in range(cou...]
    pallas_call x17 -> x18, Pallas kernels: 8.7 us -> 8.63 us  [call(): pl.pallas_call(functools.partial(kernel, self, len(args), len(outs), **fi...]
  transfers between devices with their start and end apart: 33 -> 36, of which waited for: 12 -> 14; matrix products, arithmetic and copies ran while one was open for 0% -> 0% of each run, Pallas kernels for 8% -> 9%
where the time goes in v2:
time: 70.9 us; the launch traced here: 70.6 us
  starting transfers between devices  35.6 us (50%)
  waiting for transfers between devices  23 us (32%)
  Pallas kernels  8.63 us (12%)
  local copies, waits for them, and re-layouts  2.51 us (4%)
  between operations  0.89 us (1%)
    ppermute x36, starting transfers between devices, across(): lax.ppermute(messages[i], 'blocks', [(s, s ^ i * step) for s in range(cou...  35.6 us
    ppermute x36, waiting for transfers between devices, across(): lax.ppermute(messages[i], 'blocks', [(s, s ^ i * step) for s in range(cou...  23 us
    pallas_call x18, Pallas kernels, call(): pl.pallas_call(functools.partial(kernel, self, len(args), len(outs), **fi...  8.63 us
    unnamed x16, local copies, waits for them, and re-layouts  2.51 us
  transfers between devices with their start and end apart: 36, of which 14 were waited for; matrix products, arithmetic and copies ran while one was open for 0% of the time, Pallas kernels for 9%

profile of v2, /device:TPU:0, one launch (start us, length us, event | category | flops | bytes accessed | tf_op | source)
XLA Modules:
  0.0 70.6 jit_solution(14123929970674615717)
XLA Ops:
  0.6 0.0 copy-start.1
  0.6 1.0 %copy-done.1 = f32[128,1024]{1,0:T(8,128)S(1)} copy-done((f32[128,1024]{1,0:T(8,128)S(1)}, f32[128,1024]{1,0:T(8,128)}, u32[]{:S(2)}) %copy-start.1) | copy-done | bytes 524312
  1.7 0.8 %copy-done.7 = f32[8,16,16]{2,1,0:T(8,128)S(1)} copy-done((f32[8,16,16]{2,1,0:T(8,128)S(1)}, f32[8,16,16]{2,1,0:T(8,128)}, u32[]{:S(2)}) %copy-start.7) | copy-done | bytes 8216
  2.5 0.6 shard_map.129
  3.2 0.6 collective-permute-start.18
  3.7 1.4 %shard_map.126 = (f32[33,8,128]{2,1,0:T(8,128)S(1)}, f32[33,8,128]{2,1,0:T(8,128)S(1)}, f32[33,8,128]{2,1,0:T(8,128)S(1)}, f32[33,8,128]{2,1,0:T(8,128)S(1)}) custom-call(s32[1]{0:T(128)} %bitcast.refs_0_, f32[128,1024]{1,0:T(8,128)} %refs_9_.1, f32[128,128]{1,0:T(8,128)} %bitcast.11, f32[1,128]{1,0:T(1,128)} %bitcast.16), custom_call_target="tpu_custom_call" | custom-call | flops 201326592 | bytes 1131008 | tf_op jit(solution)/shard_map/pallas_call | solution.py:260
  5.2 3.7 %collective-permute-start = (f32[33,8,128]{2,1,0:T(8,128)S(1)}, f32[33,8,128]{2,1,0:T(8,128)S(1)}, u32[]{:S(2)}, u32[]{:S(2)}) collective-permute-start(f32[33,8,128]{2,1,0:T(8,128)S(1)} %get-tuple-element.88), channel_id=1, source_target_pairs={{0,8},{1,9},{2,10},{3,11},{4,12},{5,13},{6,14},{7,15},{8,0},{9,1},... | collective-permute-start | bytes 405512 | tf_op jit(solution)/shard_map/ppermute | solution.py:477
  8.9 1.4 %collective-permute-start.4 = (f32[33,8,128]{2,1,0:T(8,128)S(1)}, f32[33,8,128]{2,1,0:T(8,128)S(1)}, u32[]{:S(2)}, u32[]{:S(2)}) collective-permute-start(f32[33,8,128]{2,1,0:T(8,128)S(1)} %get-tuple-element.93), channel_id=1, source_target_pairs={{0,12},{1,13},{2,14},{3,15},{4,8},{5,9},{6,10},{7,11},{8,4},{9,5},... | collective-permute-start | bytes 405512 | tf_op jit(solution)/shard_map/ppermute | solution.py:477
  10.2 0.2 collective-permute-start.5
  10.4 1.5 %collective-permute-start.19 = (f32[16,8,128]{2,1,0:T(8,128)S(1)}, f32[16,8,128]{2,1,0:T(8,128)S(1)}, u32[]{:S(2)}, u32[]{:S(2)}) collective-permute-start(f32[16,8,128]{2,1,0:T(8,128)S(1)} %get-tuple-element.122), channel_id=1, source_target_pairs={{0,2},{1,3},{2,0},{3,1},{4,6},{5,7},{6,4},{7,5},{8,10},{9,11},{10,... | collective-permute-start | bytes 196616 | tf_op jit(solution)/shard_map/ppermute | solution.py:477
  12.0 0.0 collective-permute-done.18.refs_2_
  12.0 0.0 collective-permute-start.20
  12.0 2.7 %collective-permute-done.19.refs_3_ = f32[16,8,128]{2,1,0:T(8,128)S(1)} collective-permute-done((f32[16,8,128]{2,1,0:T(8,128)S(1)}, f32[16,8,128]{2,1,0:T(8,128)S(1)}, u32[]{:S(2)}, u32[]{:S(2)}) %collective-permute-start.19) | collective-permute-done | bytes 65568 | tf_op jit(solution)/shard_map/ppermute | solution.py:477
  14.7 1.5 %collective-permute-done.20.refs_4_ = f32[16,8,128]{2,1,0:T(8,128)S(1)} collective-permute-done((f32[16,8,128]{2,1,0:T(8,128)S(1)}, f32[16,8,128]{2,1,0:T(8,128)S(1)}, u32[]{:S(2)}, u32[]{:S(2)}) %collective-permute-start.20) | collective-permute-done | bytes 65568 | tf_op jit(solution)/shard_map/ppermute | solution.py:477
  16.2 0.7 collective-permute-start.23
  16.9 2.3 %collective-permute-done.refs_2_.refs_4_ = f32[33,8,128]{2,1,0:T(8,128)S(1)} collective-permute-done((f32[33,8,128]{2,1,0:T(8,128)S(1)}, f32[33,8,128]{2,1,0:T(8,128)S(1)}, u32[]{:S(2)}, u32[]{:S(2)}) %collective-permute-start) | collective-permute-done | bytes 135200 | tf_op jit(solution)/shard_map/ppermute | solution.py:477
  19.1 0.6 collective-permute-start.24
  19.8 1.4 %collective-permute-start.1 = (f32[16,8,128]{2,1,0:T(8,128)S(1)}, f32[16,8,128]{2,1,0:T(8,128)S(1)}, u32[]{:S(2)}, u32[]{:S(2)}) collective-permute-start(f32[16,8,128]{2,1,0:T(8,128)S(1)} %get-tuple-element.90), channel_id=1, source_target_pairs={{0,1},{1,0},{2,3},{3,2},{4,5},{5,4},{6,7},{7,6},{8,9},{9,8},{10,11... | collective-permute-start | bytes 196616 | tf_op jit(solution)/shard_map/ppermute | solution.py:477
  21.2 0.0 collective-permute-done.5.refs_2_
  21.2 0.6 collective-permute-start.2
  21.9 0.1 collective-permute-start.6
  22.0 1.5 %collective-permute-start.3 = (f32[16,8,128]{2,1,0:T(8,128)S(1)}, f32[16,8,128]{2,1,0:T(8,128)S(1)}, u32[]{:S(2)}, u32[]{:S(2)}) collective-permute-start(f32[16,8,128]{2,1,0:T(8,128)S(1)} %get-tuple-element.92), channel_id=1, source_target_pairs={{0,3},{1,2},{2,1},{3,0},{4,7},{5,6},{6,5},{7,4},{8,11},{9,10},{10,... | collective-permute-start | bytes 196616 | tf_op jit(solution)/shard_map/ppermute | solution.py:477
  23.5 0.0 collective-permute-done.24.refs_4_
  23.5 1.5 %collective-permute-start.21 = (f32[32,8,128]{2,1,0:T(8,128)S(1)}, f32[32,8,128]{2,1,0:T(8,128)S(1)}, u32[]{:S(2)}, u32[]{:S(2)}) collective-permute-start(f32[32,8,128]{2,1,0:T(8,128)S(1)} %get-tuple-element.125), channel_id=1, source_target_pairs={{0,4},{1,5},{2,6},{3,7},{4,0},{5,1},{6,2},{7,3},{8,12},{9,13},{10,... | collective-permute-start | bytes 393224 | tf_op jit(solution)/shard_map/ppermute | solution.py:477
  25.1 2.3 %collective-permute-start.25 = (f32[32,8,128]{2,1,0:T(8,128)S(1)}, f32[32,8,128]{2,1,0:T(8,128)S(1)}, u32[]{:S(2)}, u32[]{:S(2)}) collective-permute-start(f32[32,8,128]{2,1,0:T(8,128)S(1)} %get-tuple-element.130), channel_id=1, source_target_pairs={{0,8},{1,9},{2,10},{3,11},{4,12},{5,13},{6,14},{7,15},{8,0},{9,1},... | collective-permute-start | bytes 393224 | tf_op jit(solution)/shard_map/ppermute | solution.py:477
  27.4 1.2 %collective-permute-start.26 = (f32[32,8,128]{2,1,0:T(8,128)S(1)}, f32[32,8,128]{2,1,0:T(8,128)S(1)}, u32[]{:S(2)}, u32[]{:S(2)}) collective-permute-start(f32[32,8,128]{2,1,0:T(8,128)S(1)} %get-tuple-element.131), channel_id=1, source_target_pairs={{0,12},{1,13},{2,14},{3,15},{4,8},{5,9},{6,10},{7,11},{8,4},{9,5},... | collective-permute-start | bytes 393224 | tf_op jit(solution)/shard_map/ppermute | solution.py:477
  28.6 1.6 %collective-permute-start.7 = (f32[17,8,128]{2,1,0:T(8,128)S(1)}, f32[17,8,128]{2,1,0:T(8,128)S(1)}, u32[]{:S(2)}, u32[]{:S(2)}) collective-permute-start(f32[17,8,128]{2,1,0:T(8,128)S(1)} %get-tuple-element.97), channel_id=1, source_target_pairs={{0,2},{1,3},{2,0},{3,1},{4,6},{5,7},{6,4},{7,5},{8,10},{9,11},{10,... | collective-permute-start | bytes 208904 | tf_op jit(solution)/shard_map/ppermute | solution.py:477
  30.2 0.0 collective-permute-done.6.refs_6_
  30.2 0.0 collective-permute-start.8
  30.3 0.6 copy-done.6
  30.9 0.5 shard_map.130
  31.4 1.5 %collective-permute-done.7.refs_7_ = f32[17,8,128]{2,1,0:T(8,128)S(1)} collective-permute-done((f32[17,8,128]{2,1,0:T(8,128)S(1)}, f32[17,8,128]{2,1,0:T(8,128)S(1)}, u32[]{:S(2)}, u32[]{:S(2)}) %collective-permute-start.7) | collective-permute-done | bytes 69664 | tf_op jit(solution)/shard_map/ppermute | solution.py:477
  32.9 1.5 %collective-permute-done.8.refs_8_ = f32[17,8,128]{2,1,0:T(8,128)S(1)} collective-permute-done((f32[17,8,128]{2,1,0:T(8,128)S(1)}, f32[17,8,128]{2,1,0:T(8,128)S(1)}, u32[]{:S(2)}, u32[]{:S(2)}) %collective-permute-start.8) | collective-permute-done | bytes 69664 | tf_op jit(solution)/shard_map/ppermute | solution.py:477
  34.4 1.0 %shard_map.131 = (f32[32,8,128]{2,1,0:T(8,128)S(1)}, f32[32,8,128]{2,1,0:T(8,128)S(1)}, f32[32,8,128]{2,1,0:T(8,128)S(1)}, f32[32,8,128]{2,1,0:T(8,128)S(1)}, f3...) custom-call(s32[1]{0:T(128)} %bitcast.refs_0_, ...), custom_call_target="tpu_custom_call" | custom-call | flops 402653184 | bytes 3297280 | tf_op jit(solution)/shard_map/pallas_call | solution.py:260
  35.4 2.7 %collective-permute-start.9 = (f32[32,8,128]{2,1,0:T(8,128)S(1)}, f32[32,8,128]{2,1,0:T(8,128)S(1)}, u32[]{:S(2)}, u32[]{:S(2)}) collective-permute-start(f32[32,8,128]{2,1,0:T(8,128)S(1)} %get-tuple-element.101), channel_id=1, source_target_pairs={{0,12},{1,13},{2,14},{3,15},{4,8},{5,9},{6,10},{7,11},{8,4},{9,5},... | collective-permute-start | bytes 393224 | tf_op jit(solution)/shard_map/ppermute | solution.py:477
  38.1 1.8 %collective-permute-start.14 = (f32[32,8,128]{2,1,0:T(8,128)S(1)}, f32[32,8,128]{2,1,0:T(8,128)S(1)}, u32[]{:S(2)}, u32[]{:S(2)}) collective-permute-start(f32[32,8,128]{2,1,0:T(8,128)S(1)} %get-tuple-element.108), channel_id=1, source_target_pairs={{0,8},{1,9},{2,10},{3,11},{4,12},{5,13},{6,14},{7,15},{8,0},{9,1},... | collective-permute-start | bytes 393224 | tf_op jit(solution)/shard_map/ppermute | solution.py:477
  39.8 0.7 shard_map.138
  40.5 0.1 collective-permute-start.27
  40.6 0.5 collective-permute-start.30
  41.1 0.7 %collective-permute-done.27.refs_2_ = f32[16,8,128]{2,1,0:T(8,128)S(1)} collective-permute-done((f32[16,8,128]{2,1,0:T(8,128)S(1)}, f32[16,8,128]{2,1,0:T(8,128)S(1)}, u32[]{:S(2)}, u32[]{:S(2)}) %collective-permute-start.27) | collective-permute-done | bytes 65568 | tf_op jit(solution)/shard_map/ppermute | solution.py:477
  41.9 0.7 %collective-permute-start.28 = (f32[16,8,128]{2,1,0:T(8,128)S(1)}, f32[16,8,128]{2,1,0:T(8,128)S(1)}, u32[]{:S(2)}, u32[]{:S(2)}) collective-permute-start(f32[16,8,128]{2,1,0:T(8,128)S(1)} %get-tuple-element.142), channel_id=1, source_target_pairs={{0,2},{1,3},{2,0},{3,1},{4,6},{5,7},{6,4},{7,5},{8,10},{9,11},{10,... | collective-permute-start | bytes 196616 | tf_op jit(solution)/shard_map/ppermute | solution.py:477
  42.6 1.1 %collective-permute-done.9.refs_1_ = f32[32,8,128]{2,1,0:T(8,128)S(1)} collective-permute-done((f32[32,8,128]{2,1,0:T(8,128)S(1)}, f32[32,8,128]{2,1,0:T(8,128)S(1)}, u32[]{:S(2)}, u32[]{:S(2)}) %collective-permute-start.9) | collective-permute-done | bytes 131104 | tf_op jit(solution)/shard_map/ppermute | solution.py:477
  43.6 0.8 %collective-permute-start.31 = (f32[17,8,128]{2,1,0:T(8,128)S(1)}, f32[17,8,128]{2,1,0:T(8,128)S(1)}, u32[]{:S(2)}, u32[]{:S(2)}) collective-permute-start(f32[17,8,128]{2,1,0:T(8,128)S(1)} %get-tuple-element.146), channel_id=1, source_target_pairs={{0,2},{1,3},{2,0},{3,1},{4,6},{5,7},{6,4},{7,5},{8,10},{9,11},{10,... | collective-permute-start | bytes 208904 | tf_op jit(solution)/shard_map/ppermute | solution.py:477
  44.4 1.1 %collective-permute-done.10.refs_2_ = f32[32,8,128]{2,1,0:T(8,128)S(1)} collective-permute-done((f32[32,8,128]{2,1,0:T(8,128)S(1)}, f32[32,8,128]{2,1,0:T(8,128)S(1)}, u32[]{:S(2)}, u32[]{:S(2)}) %collective-permute-start.10) | collective-permute-done | bytes 131104 | tf_op jit(solution)/shard_map/ppermute | solution.py:477
  45.4 1.3 %collective-permute-start.32 = (f32[17,8,128]{2,1,0:T(8,128)S(1)}, f32[17,8,128]{2,1,0:T(8,128)S(1)}, u32[]{:S(2)}, u32[]{:S(2)}) collective-permute-start(f32[17,8,128]{2,1,0:T(8,128)S(1)} %get-tuple-element.147), channel_id=1, source_target_pairs={{0,3},{1,2},{2,1},{3,0},{4,7},{5,6},{6,5},{7,4},{8,11},{9,10},{10,... | collective-permute-start | bytes 208904 | tf_op jit(solution)/shard_map/ppermute | solution.py:477
  46.8 4.2 %collective-permute-done.14.refs_2_ = f32[32,8,128]{2,1,0:T(8,128)S(1)} collective-permute-done((f32[32,8,128]{2,1,0:T(8,128)S(1)}, f32[32,8,128]{2,1,0:T(8,128)S(1)}, u32[]{:S(2)}, u32[]{:S(2)}) %collective-permute-start.14) | collective-permute-done | bytes 131104 | tf_op jit(solution)/shard_map/ppermute | solution.py:477
  51.0 0.6 collective-permute-start.29
  51.6 1.1 %collective-permute-start.11 = (f32[16,8,128]{2,1,0:T(8,128)S(1)}, f32[16,8,128]{2,1,0:T(8,128)S(1)}, u32[]{:S(2)}, u32[]{:S(2)}) collective-permute-start(f32[16,8,128]{2,1,0:T(8,128)S(1)} %get-tuple-element.104), channel_id=1, source_target_pairs={{0,1},{1,0},{2,3},{3,2},{4,5},{5,4},{6,7},{7,6},{8,9},{9,8},{10,11... | collective-permute-start | bytes 196616 | tf_op jit(solution)/shard_map/ppermute | solution.py:477
  52.7 0.1 collective-permute-start.15
  52.8 0.5 collective-permute-start.16
  53.3 1.3 %collective-permute-start.17 = (f32[16,8,128]{2,1,0:T(8,128)S(1)}, f32[16,8,128]{2,1,0:T(8,128)S(1)}, u32[]{:S(2)}, u32[]{:S(2)}) collective-permute-start(f32[16,8,128]{2,1,0:T(8,128)S(1)} %get-tuple-element.112), channel_id=1, source_target_pairs={{0,3},{1,2},{2,1},{3,0},{4,7},{5,6},{6,5},{7,4},{8,11},{9,10},{10,... | collective-permute-start | bytes 196616 | tf_op jit(solution)/shard_map/ppermute | solution.py:477
  54.6 0.7 collective-permute-done.29.refs_4_
  55.3 3.4 %collective-permute-start.35 = (f32[33,8,128]{2,1,0:T(8,128)S(1)}, f32[33,8,128]{2,1,0:T(8,128)S(1)}, u32[]{:S(2)}, u32[]{:S(2)}) collective-permute-start(f32[33,8,128]{2,1,0:T(8,128)S(1)} %get-tuple-element.151), channel_id=1, source_target_pairs={{0,8},{1,9},{2,10},{3,11},{4,12},{5,13},{6,14},{7,15},{8,0},{9,1},... | collective-permute-start | bytes 405512 | tf_op jit(solution)/shard_map/ppermute | solution.py:477
  58.7 0.9 %collective-permute-start.33 = (f32[33,8,128]{2,1,0:T(8,128)S(1)}, f32[33,8,128]{2,1,0:T(8,128)S(1)}, u32[]{:S(2)}, u32[]{:S(2)}) collective-permute-start(f32[33,8,128]{2,1,0:T(8,128)S(1)} %get-tuple-element.148), channel_id=1, source_target_pairs={{0,12},{1,13},{2,14},{3,15},{4,8},{5,9},{6,10},{7,11},{8,4},{9,5},... | collective-permute-start | bytes 405512 | tf_op jit(solution)/shard_map/ppermute | solution.py:477
  59.6 1.0 %collective-permute-start.12 = (f32[16,8,128]{2,1,0:T(8,128)S(1)}, f32[16,8,128]{2,1,0:T(8,128)S(1)}, u32[]{:S(2)}, u32[]{:S(2)}) collective-permute-start(f32[16,8,128]{2,1,0:T(8,128)S(1)} %get-tuple-element.105), channel_id=1, source_target_pairs={{0,2},{1,3},{2,0},{3,1},{4,6},{5,7},{6,4},{7,5},{8,10},{9,11},{10,... | collective-permute-start | bytes 196616 | tf_op jit(solution)/shard_map/ppermute | solution.py:477
  60.6 1.0 %shard_map.139 = (f32[128,16]{1,0:T(8,128)S(1)}, f32[128,128]{1,0:T(8,128)S(1)}) custom-call(s32[1]{0:T(128)} %bitcast.refs_0_, f32[128,1024]{1,0:T(8,128)S(1)} %get-tuple-element.119.refs_1_, f32[128,1024]{1,0:T(8,128)S(1)} %get-tuple-element.134.refs_2_, f32[128,1024]{1,0:T(8,128)S(1)} %get-tuple-element.135.refs_3_, ...), custom_call_target="tpu_custom_call" | custom-call | flops 402653184 | bytes 2170880 | tf_op jit(solution)/shard_map/pallas_call | solution.py:260
  61.7 0.4 shard_map.134
  62.1 2.2 %collective-permute-done.12.refs_3_ = f32[16,8,128]{2,1,0:T(8,128)S(1)} collective-permute-done((f32[16,8,128]{2,1,0:T(8,128)S(1)}, f32[16,8,128]{2,1,0:T(8,128)S(1)}, u32[]{:S(2)}, u32[]{:S(2)}) %collective-permute-start.12) | collective-permute-done | bytes 65568 | tf_op jit(solution)/shard_map/ppermute | solution.py:477
  64.3 0.7 %collective-permute-done.13.refs_4_ = f32[16,8,128]{2,1,0:T(8,128)S(1)} collective-permute-done((f32[16,8,128]{2,1,0:T(8,128)S(1)}, f32[16,8,128]{2,1,0:T(8,128)S(1)}, u32[]{:S(2)}, u32[]{:S(2)}) %collective-permute-start.13) | collective-permute-done | bytes 65568 | tf_op jit(solution)/shard_map/ppermute | solution.py:477
  65.0 0.8 %shard_map.135 = (f32[128,1024]{1,0:T(8,128)S(1)}, f32[128,16]{1,0:T(8,128)S(1)}) custom-call(s32[1]{0:T(128)} %bitcast.refs_0_, f32[16,8,128]{2,1,0:T(8,128)S(1)} %get-tuple-element.103.refs_1_, f32[16,8,128]{2,1,0:T(8,128)S(1)} %collective-permute-done.11.refs_2_, f32[16,8,128]{2,1,0:T(8,128)S(1)} %collective-permute-done.12.refs_3_, ...), custom_call_target="tpu_custom_call" | custom-call | flops 201326592 | bytes 2531328 | tf_op jit(solution)/shard_map/pallas_call | solution.py:260
  65.8 2.5 %collective-permute-done.35.refs_2_.refs_8_ = f32[33,8,128]{2,1,0:T(8,128)S(1)} collective-permute-done((f32[33,8,128]{2,1,0:T(8,128)S(1)}, f32[33,8,128]{2,1,0:T(8,128)S(1)}, u32[]{:S(2)}, u32[]{:S(2)}) %collective-permute-start.35) | collective-permute-done | bytes 135200 | tf_op jit(solution)/shard_map/ppermute | solution.py:477
  68.3 0.4 shard_map.142
  68.7 0.4 collective-permute-done.34.refs_6_
  69.1 1.5 %shard_map.143 = (f32[128,1024]{1,0:T(8,128)}, f32[128,16]{1,0:T(8,128)}, f32[128,128]{1,0:T(8,128)}, f32[128,16]{1,0:T(8,128)}, f32[128,1024]{1,0:T(8,128)}, /*index=5*/f32[1,128]{1,0:T(1,128)}, f32[128,128]{1,0:T(8,128)}) custom-call(s32[1]{0:T(128)} %bitcast.refs_0_, f32[128,1024]{1,0:T(8,128)S(1)} %get-tuple-element.118.refs_1_, ...), custom_call_target="tpu_custom_call" | custom-call | flops 201326592 | bytes 4674560 | tf_op jit(solution)/shard_map/pallas_call | solution.py:260
  (42 shorter events, 0.2 us)
Async XLA Ops:
  0.6 1.0 %copy-start.1 = (f32[128,1024]{1,0:T(8,128)S(1)}, f32[128,1024]{1,0:T(8,128)}, u32[]{:S(2)}) copy-start(f32[128,1024]{1,0:T(8,128)} %refs_3_.1) | copy-start | bytes 1572868
  1.7 0.8 %copy-start.7 = (f32[8,16,16]{2,1,0:T(8,128)S(1)}, f32[8,16,16]{2,1,0:T(8,128)}, u32[]{:S(2)}) copy-start(f32[8,16,16]{2,1,0:T(8,128)} %param.13) | copy-start | bytes 24580
  3.2 8.8 %collective-permute-start.18 = (f32[16,8,128]{2,1,0:T(8,128)S(1)}, f32[16,8,128]{2,1,0:T(8,128)S(1)}, u32[]{:S(2)}, u32[]{:S(2)}) collective-permute-start(f32[16,8,128]{2,1,0:T(8,128)S(1)} %get-tuple-element.121), channel_id=1, source_target_pairs={{0,1},{1,0},{2,3},{3,2},{4,5},{5,4},{6,7},{7,6},{8,9},{9,8},{10,11... | collective-permute-start | bytes 196616 | tf_op jit(solution)/shard_map/ppermute | solution.py:477
  5.2 13.9 %collective-permute-start = (f32[33,8,128]{2,1,0:T(8,128)S(1)}, f32[33,8,128]{2,1,0:T(8,128)S(1)}, u32[]{:S(2)}, u32[]{:S(2)}) collective-permute-start(f32[33,8,128]{2,1,0:T(8,128)S(1)} %get-tuple-element.88), channel_id=1, source_target_pairs={{0,8},{1,9},{2,10},{3,11},{4,12},{5,13},{6,14},{7,15},{8,0},{9,1},... | collective-permute-start | bytes 405512 | tf_op jit(solution)/shard_map/ppermute | solution.py:477
  8.9 10.9 %collective-permute-start.4 = (f32[33,8,128]{2,1,0:T(8,128)S(1)}, f32[33,8,128]{2,1,0:T(8,128)S(1)}, u32[]{:S(2)}, u32[]{:S(2)}) collective-permute-start(f32[33,8,128]{2,1,0:T(8,128)S(1)} %get-tuple-element.93), channel_id=1, source_target_pairs={{0,12},{1,13},{2,14},{3,15},{4,8},{5,9},{6,10},{7,11},{8,4},{9,5},... | collective-permute-start | bytes 405512 | tf_op jit(solution)/shard_map/ppermute | solution.py:477
  10.2 11.0 %collective-permute-start.5 = (f32[33,8,128]{2,1,0:T(8,128)S(1)}, f32[33,8,128]{2,1,0:T(8,128)S(1)}, u32[]{:S(2)}, u32[]{:S(2)}) collective-permute-start(f32[33,8,128]{2,1,0:T(8,128)S(1)} %get-tuple-element.94), channel_id=1, source_target_pairs={{0,4},{1,5},{2,6},{3,7},{4,0},{5,1},{6,2},{7,3},{8,12},{9,13},{10,... | collective-permute-start | bytes 405512 | tf_op jit(solution)/shard_map/ppermute | solution.py:477
  10.4 4.3 %collective-permute-start.19 = (f32[16,8,128]{2,1,0:T(8,128)S(1)}, f32[16,8,128]{2,1,0:T(8,128)S(1)}, u32[]{:S(2)}, u32[]{:S(2)}) collective-permute-start(f32[16,8,128]{2,1,0:T(8,128)S(1)} %get-tuple-element.122), channel_id=1, source_target_pairs={{0,2},{1,3},{2,0},{3,1},{4,6},{5,7},{6,4},{7,5},{8,10},{9,11},{10,... | collective-permute-start | bytes 196616 | tf_op jit(solution)/shard_map/ppermute | solution.py:477
  12.0 4.2 %collective-permute-start.20 = (f32[16,8,128]{2,1,0:T(8,128)S(1)}, f32[16,8,128]{2,1,0:T(8,128)S(1)}, u32[]{:S(2)}, u32[]{:S(2)}) collective-permute-start(f32[16,8,128]{2,1,0:T(8,128)S(1)} %get-tuple-element.123), channel_id=1, source_target_pairs={{0,3},{1,2},{2,1},{3,0},{4,7},{5,6},{6,5},{7,4},{8,11},{9,10},{10,... | collective-permute-start | bytes 196616 | tf_op jit(solution)/shard_map/ppermute | solution.py:477
  14.7 7.2 %collective-permute-start.22 = (f32[16,8,128]{2,1,0:T(8,128)S(1)}, f32[16,8,128]{2,1,0:T(8,128)S(1)}, u32[]{:S(2)}, u32[]{:S(2)}) collective-permute-start(f32[16,8,128]{2,1,0:T(8,128)S(1)} %get-tuple-element.127), channel_id=1, source_target_pairs={{0,1},{1,0},{2,3},{3,2},{4,5},{5,4},{6,7},{7,6},{8,9},{9,8},{10,11... | collective-permute-start | bytes 196616 | tf_op jit(solution)/shard_map/ppermute | solution.py:477
  16.2 5.8 %collective-permute-start.23 = (f32[16,8,128]{2,1,0:T(8,128)S(1)}, f32[16,8,128]{2,1,0:T(8,128)S(1)}, u32[]{:S(2)}, u32[]{:S(2)}) collective-permute-start(f32[16,8,128]{2,1,0:T(8,128)S(1)} %get-tuple-element.128), channel_id=1, source_target_pairs={{0,2},{1,3},{2,0},{3,1},{4,6},{5,7},{6,4},{7,5},{8,10},{9,11},{10,... | collective-permute-start | bytes 196616 | tf_op jit(solution)/shard_map/ppermute | solution.py:477
  19.1 4.4 %collective-permute-start.24 = (f32[16,8,128]{2,1,0:T(8,128)S(1)}, f32[16,8,128]{2,1,0:T(8,128)S(1)}, u32[]{:S(2)}, u32[]{:S(2)}) collective-permute-start(f32[16,8,128]{2,1,0:T(8,128)S(1)} %get-tuple-element.129), channel_id=1, source_target_pairs={{0,3},{1,2},{2,1},{3,0},{4,7},{5,6},{6,5},{7,4},{8,11},{9,10},{10,... | collective-permute-start | bytes 196616 | tf_op jit(solution)/shard_map/ppermute | solution.py:477
  19.7 10.5 %copy-start.3 = (f32[1,128,128]{2,1,0:T(8,128)S(1)}, f32[1,128,128]{2,1,0:T(8,128)}, u32[]{:S(2)}) copy-start(f32[1,128,128]{2,1,0:T(8,128)} %param.10) | copy-start | bytes 196612
  19.7 10.5 %copy-start.4 = (f32[8,16,16]{2,1,0:T(8,128)S(1)}, f32[8,16,16]{2,1,0:T(8,128)}, u32[]{:S(2)}) copy-start(f32[8,16,16]{2,1,0:T(8,128)} %param.11) | copy-start | bytes 24580
  19.8 5.3 %collective-permute-start.1 = (f32[16,8,128]{2,1,0:T(8,128)S(1)}, f32[16,8,128]{2,1,0:T(8,128)S(1)}, u32[]{:S(2)}, u32[]{:S(2)}) collective-permute-start(f32[16,8,128]{2,1,0:T(8,128)S(1)} %get-tuple-element.90), channel_id=1, source_target_pairs={{0,1},{1,0},{2,3},{3,2},{4,5},{5,4},{6,7},{7,6},{8,9},{9,8},{10,11... | collective-permute-start | bytes 196616 | tf_op jit(solution)/shard_map/ppermute | solution.py:477
  21.2 9.0 %copy-start = (f32[128,1024]{1,0:T(8,128)S(1)}, f32[128,1024]{1,0:T(8,128)}, u32[]{:S(2)}) copy-start(f32[128,1024]{1,0:T(8,128)} %refs_9_.1) | copy-start | bytes 1572868
  21.2 9.0 %copy-start.2 = (f32[128,1024]{1,0:T(8,128)S(1)}, f32[128,1024]{1,0:T(8,128)}, u32[]{:S(2)}) copy-start(f32[128,1024]{1,0:T(8,128)} %refs_3_.1) | copy-start | bytes 1572868
  21.2 6.2 %collective-permute-start.2 = (f32[16,8,128]{2,1,0:T(8,128)S(1)}, f32[16,8,128]{2,1,0:T(8,128)S(1)}, u32[]{:S(2)}, u32[]{:S(2)}) collective-permute-start(f32[16,8,128]{2,1,0:T(8,128)S(1)} %get-tuple-element.91), channel_id=1, source_target_pairs={{0,2},{1,3},{2,0},{3,1},{4,6},{5,7},{6,4},{7,5},{8,10},{9,11},{10,... | collective-permute-start | bytes 196616 | tf_op jit(solution)/shard_map/ppermute | solution.py:477
  21.9 8.3 %collective-permute-start.6 = (f32[17,8,128]{2,1,0:T(8,128)S(1)}, f32[17,8,128]{2,1,0:T(8,128)S(1)}, u32[]{:S(2)}, u32[]{:S(2)}) collective-permute-start(f32[17,8,128]{2,1,0:T(8,128)S(1)} %get-tuple-element.96), channel_id=1, source_target_pairs={{0,1},{1,0},{2,3},{3,2},{4,5},{5,4},{6,7},{7,6},{8,9},{9,8},{10,11... | collective-permute-start | bytes 208904 | tf_op jit(solution)/shard_map/ppermute | solution.py:477
  22.0 6.6 %collective-permute-start.3 = (f32[16,8,128]{2,1,0:T(8,128)S(1)}, f32[16,8,128]{2,1,0:T(8,128)S(1)}, u32[]{:S(2)}, u32[]{:S(2)}) collective-permute-start(f32[16,8,128]{2,1,0:T(8,128)S(1)} %get-tuple-element.92), channel_id=1, source_target_pairs={{0,3},{1,2},{2,1},{3,0},{4,7},{5,6},{6,5},{7,4},{8,11},{9,10},{10,... | collective-permute-start | bytes 196616 | tf_op jit(solution)/shard_map/ppermute | solution.py:477
  23.5 14.6 %collective-permute-start.21 = (f32[32,8,128]{2,1,0:T(8,128)S(1)}, f32[32,8,128]{2,1,0:T(8,128)S(1)}, u32[]{:S(2)}, u32[]{:S(2)}) collective-permute-start(f32[32,8,128]{2,1,0:T(8,128)S(1)} %get-tuple-element.125), channel_id=1, source_target_pairs={{0,4},{1,5},{2,6},{3,7},{4,0},{5,1},{6,2},{7,3},{8,12},{9,13},{10,... | collective-permute-start | bytes 393224 | tf_op jit(solution)/shard_map/ppermute | solution.py:477
  25.1 14.8 %collective-permute-start.25 = (f32[32,8,128]{2,1,0:T(8,128)S(1)}, f32[32,8,128]{2,1,0:T(8,128)S(1)}, u32[]{:S(2)}, u32[]{:S(2)}) collective-permute-start(f32[32,8,128]{2,1,0:T(8,128)S(1)} %get-tuple-element.130), channel_id=1, source_target_pairs={{0,8},{1,9},{2,10},{3,11},{4,12},{5,13},{6,14},{7,15},{8,0},{9,1},... | collective-permute-start | bytes 393224 | tf_op jit(solution)/shard_map/ppermute | solution.py:477
  27.4 12.5 %collective-permute-start.26 = (f32[32,8,128]{2,1,0:T(8,128)S(1)}, f32[32,8,128]{2,1,0:T(8,128)S(1)}, u32[]{:S(2)}, u32[]{:S(2)}) collective-permute-start(f32[32,8,128]{2,1,0:T(8,128)S(1)} %get-tuple-element.131), channel_id=1, source_target_pairs={{0,12},{1,13},{2,14},{3,15},{4,8},{5,9},{6,10},{7,11},{8,4},{9,5},... | collective-permute-start | bytes 393224 | tf_op jit(solution)/shard_map/ppermute | solution.py:477
  28.6 4.3 %collective-permute-start.7 = (f32[17,8,128]{2,1,0:T(8,128)S(1)}, f32[17,8,128]{2,1,0:T(8,128)S(1)}, u32[]{:S(2)}, u32[]{:S(2)}) collective-permute-start(f32[17,8,128]{2,1,0:T(8,128)S(1)} %get-tuple-element.97), channel_id=1, source_target_pairs={{0,2},{1,3},{2,0},{3,1},{4,6},{5,7},{6,4},{7,5},{8,10},{9,11},{10,... | collective-permute-start | bytes 208904 | tf_op jit(solution)/shard_map/ppermute | solution.py:477
  30.2 4.2 %collective-permute-start.8 = (f32[17,8,128]{2,1,0:T(8,128)S(1)}, f32[17,8,128]{2,1,0:T(8,128)S(1)}, u32[]{:S(2)}, u32[]{:S(2)}) collective-permute-start(f32[17,8,128]{2,1,0:T(8,128)S(1)} %get-tuple-element.98), channel_id=1, source_target_pairs={{0,3},{1,2},{2,1},{3,0},{4,7},{5,6},{6,5},{7,4},{8,11},{9,10},{10,... | collective-permute-start | bytes 208904 | tf_op jit(solution)/shard_map/ppermute | solution.py:477
  30.2 0.7 copy-start.6
  30.9 3.5 %copy-start.5 = (f32[1,128,128]{2,1,0:T(8,128)S(1)}, f32[1,128,128]{2,1,0:T(8,128)}, u32[]{:S(2)}) copy-start(f32[1,128,128]{2,1,0:T(8,128)} %param.12) | copy-start | bytes 196612
  35.4 8.2 %collective-permute-start.9 = (f32[32,8,128]{2,1,0:T(8,128)S(1)}, f32[32,8,128]{2,1,0:T(8,128)S(1)}, u32[]{:S(2)}, u32[]{:S(2)}) collective-permute-start(f32[32,8,128]{2,1,0:T(8,128)S(1)} %get-tuple-element.101), channel_id=1, source_target_pairs={{0,12},{1,13},{2,14},{3,15},{4,8},{5,9},{6,10},{7,11},{8,4},{9,5},... | collective-permute-start | bytes 393224 | tf_op jit(solution)/shard_map/ppermute | solution.py:477
  38.1 7.4 %collective-permute-start.10 = (f32[32,8,128]{2,1,0:T(8,128)S(1)}, f32[32,8,128]{2,1,0:T(8,128)S(1)}, u32[]{:S(2)}, u32[]{:S(2)}) collective-permute-start(f32[32,8,128]{2,1,0:T(8,128)S(1)} %get-tuple-element.102), channel_id=1, source_target_pairs={{0,4},{1,5},{2,6},{3,7},{4,0},{5,1},{6,2},{7,3},{8,12},{9,13},{10,... | collective-permute-start | bytes 393224 | tf_op jit(solution)/shard_map/ppermute | solution.py:477
  38.1 12.9 %collective-permute-start.14 = (f32[32,8,128]{2,1,0:T(8,128)S(1)}, f32[32,8,128]{2,1,0:T(8,128)S(1)}, u32[]{:S(2)}, u32[]{:S(2)}) collective-permute-start(f32[32,8,128]{2,1,0:T(8,128)S(1)} %get-tuple-element.108), channel_id=1, source_target_pairs={{0,8},{1,9},{2,10},{3,11},{4,12},{5,13},{6,14},{7,15},{8,0},{9,1},... | collective-permute-start | bytes 393224 | tf_op jit(solution)/shard_map/ppermute | solution.py:477
  40.5 1.3 %collective-permute-start.27 = (f32[16,8,128]{2,1,0:T(8,128)S(1)}, f32[16,8,128]{2,1,0:T(8,128)S(1)}, u32[]{:S(2)}, u32[]{:S(2)}) collective-permute-start(f32[16,8,128]{2,1,0:T(8,128)S(1)} %get-tuple-element.141), channel_id=1, source_target_pairs={{0,1},{1,0},{2,3},{3,2},{4,5},{5,4},{6,7},{7,6},{8,9},{9,8},{10,11... | collective-permute-start | bytes 196616 | tf_op jit(solution)/shard_map/ppermute | solution.py:477
  40.6 12.1 %collective-permute-start.30 = (f32[17,8,128]{2,1,0:T(8,128)S(1)}, f32[17,8,128]{2,1,0:T(8,128)S(1)}, u32[]{:S(2)}, u32[]{:S(2)}) collective-permute-start(f32[17,8,128]{2,1,0:T(8,128)S(1)} %get-tuple-element.145), channel_id=1, source_target_pairs={{0,1},{1,0},{2,3},{3,2},{4,5},{5,4},{6,7},{7,6},{8,9},{9,8},{10,11... | collective-permute-start | bytes 208904 | tf_op jit(solution)/shard_map/ppermute | solution.py:477
  41.9 9.7 %collective-permute-start.28 = (f32[16,8,128]{2,1,0:T(8,128)S(1)}, f32[16,8,128]{2,1,0:T(8,128)S(1)}, u32[]{:S(2)}, u32[]{:S(2)}) collective-permute-start(f32[16,8,128]{2,1,0:T(8,128)S(1)} %get-tuple-element.142), channel_id=1, source_target_pairs={{0,2},{1,3},{2,0},{3,1},{4,6},{5,7},{6,4},{7,5},{8,10},{9,11},{10,... | collective-permute-start | bytes 196616 | tf_op jit(solution)/shard_map/ppermute | solution.py:477
  43.6 9.2 %collective-permute-start.31 = (f32[17,8,128]{2,1,0:T(8,128)S(1)}, f32[17,8,128]{2,1,0:T(8,128)S(1)}, u32[]{:S(2)}, u32[]{:S(2)}) collective-permute-start(f32[17,8,128]{2,1,0:T(8,128)S(1)} %get-tuple-element.146), channel_id=1, source_target_pairs={{0,2},{1,3},{2,0},{3,1},{4,6},{5,7},{6,4},{7,5},{8,10},{9,11},{10,... | collective-permute-start | bytes 208904 | tf_op jit(solution)/shard_map/ppermute | solution.py:477
  45.4 7.9 %collective-permute-start.32 = (f32[17,8,128]{2,1,0:T(8,128)S(1)}, f32[17,8,128]{2,1,0:T(8,128)S(1)}, u32[]{:S(2)}, u32[]{:S(2)}) collective-permute-start(f32[17,8,128]{2,1,0:T(8,128)S(1)} %get-tuple-element.147), channel_id=1, source_target_pairs={{0,3},{1,2},{2,1},{3,0},{4,7},{5,6},{6,5},{7,4},{8,11},{9,10},{10,... | collective-permute-start | bytes 208904 | tf_op jit(solution)/shard_map/ppermute | solution.py:477
  51.0 4.3 %collective-permute-start.29 = (f32[16,8,128]{2,1,0:T(8,128)S(1)}, f32[16,8,128]{2,1,0:T(8,128)S(1)}, u32[]{:S(2)}, u32[]{:S(2)}) collective-permute-start(f32[16,8,128]{2,1,0:T(8,128)S(1)} %get-tuple-element.143), channel_id=1, source_target_pairs={{0,3},{1,2},{2,1},{3,0},{4,7},{5,6},{6,5},{7,4},{8,11},{9,10},{10,... | collective-permute-start | bytes 196616 | tf_op jit(solution)/shard_map/ppermute | solution.py:477
  51.6 7.1 %collective-permute-start.11 = (f32[16,8,128]{2,1,0:T(8,128)S(1)}, f32[16,8,128]{2,1,0:T(8,128)S(1)}, u32[]{:S(2)}, u32[]{:S(2)}) collective-permute-start(f32[16,8,128]{2,1,0:T(8,128)S(1)} %get-tuple-element.104), channel_id=1, source_target_pairs={{0,1},{1,0},{2,3},{3,2},{4,5},{5,4},{6,7},{7,6},{8,9},{9,8},{10,11... | collective-permute-start | bytes 196616 | tf_op jit(solution)/shard_map/ppermute | solution.py:477
  52.7 6.9 %collective-permute-start.15 = (f32[16,8,128]{2,1,0:T(8,128)S(1)}, f32[16,8,128]{2,1,0:T(8,128)S(1)}, u32[]{:S(2)}, u32[]{:S(2)}) collective-permute-start(f32[16,8,128]{2,1,0:T(8,128)S(1)} %get-tuple-element.110), channel_id=1, source_target_pairs={{0,1},{1,0},{2,3},{3,2},{4,5},{5,4},{6,7},{7,6},{8,9},{9,8},{10,11... | collective-permute-start | bytes 196616 | tf_op jit(solution)/shard_map/ppermute | solution.py:477
  52.8 6.8 %collective-permute-start.16 = (f32[16,8,128]{2,1,0:T(8,128)S(1)}, f32[16,8,128]{2,1,0:T(8,128)S(1)}, u32[]{:S(2)}, u32[]{:S(2)}) collective-permute-start(f32[16,8,128]{2,1,0:T(8,128)S(1)} %get-tuple-element.111), channel_id=1, source_target_pairs={{0,2},{1,3},{2,0},{3,1},{4,6},{5,7},{6,4},{7,5},{8,10},{9,11},{10,... | collective-permute-start | bytes 196616 | tf_op jit(solution)/shard_map/ppermute | solution.py:477
  53.3 7.3 %collective-permute-start.17 = (f32[16,8,128]{2,1,0:T(8,128)S(1)}, f32[16,8,128]{2,1,0:T(8,128)S(1)}, u32[]{:S(2)}, u32[]{:S(2)}) collective-permute-start(f32[16,8,128]{2,1,0:T(8,128)S(1)} %get-tuple-element.112), channel_id=1, source_target_pairs={{0,3},{1,2},{2,1},{3,0},{4,7},{5,6},{6,5},{7,4},{8,11},{9,10},{10,... | collective-permute-start | bytes 196616 | tf_op jit(solution)/shard_map/ppermute | solution.py:477
  55.3 13.0 %collective-permute-start.35 = (f32[33,8,128]{2,1,0:T(8,128)S(1)}, f32[33,8,128]{2,1,0:T(8,128)S(1)}, u32[]{:S(2)}, u32[]{:S(2)}) collective-permute-start(f32[33,8,128]{2,1,0:T(8,128)S(1)} %get-tuple-element.151), channel_id=1, source_target_pairs={{0,8},{1,9},{2,10},{3,11},{4,12},{5,13},{6,14},{7,15},{8,0},{9,1},... | collective-permute-start | bytes 405512 | tf_op jit(solution)/shard_map/ppermute | solution.py:477
  58.7 10.0 %collective-permute-start.33 = (f32[33,8,128]{2,1,0:T(8,128)S(1)}, f32[33,8,128]{2,1,0:T(8,128)S(1)}, u32[]{:S(2)}, u32[]{:S(2)}) collective-permute-start(f32[33,8,128]{2,1,0:T(8,128)S(1)} %get-tuple-element.148), channel_id=1, source_target_pairs={{0,12},{1,13},{2,14},{3,15},{4,8},{5,9},{6,10},{7,11},{8,4},{9,5},... | collective-permute-start | bytes 405512 | tf_op jit(solution)/shard_map/ppermute | solution.py:477
  59.6 9.5 %collective-permute-start.34 = (f32[33,8,128]{2,1,0:T(8,128)S(1)}, f32[33,8,128]{2,1,0:T(8,128)S(1)}, u32[]{:S(2)}, u32[]{:S(2)}) collective-permute-start(f32[33,8,128]{2,1,0:T(8,128)S(1)} %get-tuple-element.149), channel_id=1, source_target_pairs={{0,4},{1,5},{2,6},{3,7},{4,0},{5,1},{6,2},{7,3},{8,12},{9,13},{10,... | collective-permute-start | bytes 405512 | tf_op jit(solution)/shard_map/ppermute | solution.py:477
  59.6 4.7 %collective-permute-start.12 = (f32[16,8,128]{2,1,0:T(8,128)S(1)}, f32[16,8,128]{2,1,0:T(8,128)S(1)}, u32[]{:S(2)}, u32[]{:S(2)}) collective-permute-start(f32[16,8,128]{2,1,0:T(8,128)S(1)} %get-tuple-element.105), channel_id=1, source_target_pairs={{0,2},{1,3},{2,0},{3,1},{4,6},{5,7},{6,4},{7,5},{8,10},{9,11},{10,... | collective-permute-start | bytes 196616 | tf_op jit(solution)/shard_map/ppermute | solution.py:477
  60.6 4.4 %collective-permute-start.13 = (f32[16,8,128]{2,1,0:T(8,128)S(1)}, f32[16,8,128]{2,1,0:T(8,128)S(1)}, u32[]{:S(2)}, u32[]{:S(2)}) collective-permute-start(f32[16,8,128]{2,1,0:T(8,128)S(1)} %get-tuple-element.106), channel_id=1, source_target_pairs={{0,3},{1,2},{2,1},{3,0},{4,7},{5,6},{6,5},{7,4},{8,11},{9,10},{10,... | collective-permute-start | bytes 196616 | tf_op jit(solution)/shard_map/ppermute | solution.py:477

commit v3 on v2

--- a/solution.py
+++ b/solution.py
@@ -164,6 +164,8 @@
         self.early, self.late = early_keys(self.outer)
         self.far, self.near = range(self.outer // 2, self.outer), range(self.outer // 2)
         self.sooner, self.later = back_keys(self.outer)
+        self.last = self.later[:1]
+        self.soon = [k for k in range(self.outer) if k not in self.last]
         self.rows = features // count
         self.chunks = tokens // LANE
         self.block_tiles = self.rows // SUB * self.chunks
@@ -339,8 +341,8 @@
     turned[...] = left[...].T
     gain_kept[...] = gain[...]
     table[...] = left[...].T * gain[...]
-    scaled_early[...] = stacked_left(plan.gather_rows(table, plan.line_spans(plan.early), z, p))
-    scaled_late[...] = stacked_left(plan.gather_rows(table, plan.line_spans(plan.late), z, p))
+    scaled_early[...] = stacked_left(plan.gather_rows(table, plan.line_spans(plan.soon), z, p))
+    scaled_late[...] = stacked_left(plan.gather_rows(table, plan.line_spans(plan.last), z, p))
     wide_early[...] = stacked_left(plan.gather_rows(wide_two, plan.plane_spans(plan.early), z, p))
     wide_late[...] = stacked_left(plan.gather_rows(wide_two, plan.plane_spans(plan.late), z, p))
     x_pair[...] = pair_of(x[...])
@@ -429,8 +431,8 @@
 
 def early_input(plan, n_in, n_out, *refs):
     _, ins, (partial, product), (dy1,) = split_refs(n_in, n_out, refs)
-    parts, (cotangent, scaled, x_pair, inverse_root) = ins[: len(plan.early)], ins[len(plan.early) :]
-    plan.line_up(parts, plan.line_spans(plan.early), dy1)
+    parts, (cotangent, scaled, x_pair, inverse_root) = ins[: len(plan.soon)], ins[len(plan.soon) :]
+    plan.line_up(parts, plan.line_spans(plan.soon), dy1)
     back = dy1[...] * inverse_root[...]
     partial[...] = cotangent[...] + matmul_stacked(scaled[...], back)
     product[...] = matmul_nt_pair(back, x_pair[...])
@@ -447,12 +449,12 @@
     input_gradient, gain_gradient, grad_left_one = made
     root = inverse_root[...]
     inner = plan.sums_row(plan.add_sums(parts)) / plan.width
-    spans = plan.line_spans(plan.late)
-    plan.line_up(parts[: len(plan.late)], spans, dy1)
+    spans = plan.line_spans(plan.last)
+    plan.line_up(parts[: len(plan.last)], spans, dy1)
     back = dy1[...] * root
     input_gradient[...] = partial[...] + matmul_stacked(scaled[...], back) - x[...] * (root * root * inner)
     stores[len(ready)].start()
-    plan.scatter_rows(product[...], plan.line_spans(plan.early), whole, z, p)
+    plan.scatter_rows(product[...], plan.line_spans(plan.soon), whole, z, p)
     plan.scatter_rows(matmul_nt_pair(back, x_pair[...]), spans, whole, z, p)
     total = whole[...]
     gain_gradient[...] = jnp.sum(turned[...] * total, axis=0, keepdims=True) * plan.factor
@@ -502,10 +504,13 @@
         cotangent, flat_two, scratch=[full], flops=cost,
     )
     dy2_far, dy2_near = over_inner(sent[:inner]), over_inner(sent[inner:])
-    half, stacked = (features // 2, tokens), jax.ShapeDtypeStruct((features, 2 * features), jnp.bfloat16)
+    half, soon = (features // 2, tokens), features // outer * len(plan.soon)
+    stacked_half, stacked_soon, stacked_last = (
+        jax.ShapeDtypeStruct((features, 4 * rows), jnp.bfloat16) for rows in (features // 2, soon, features - soon)
+    )
     pair = jax.ShapeDtypeStruct((2 * features, tokens), jnp.bfloat16)
     wide_one, turned_one, gain_kept, scaled_early, scaled_late, wide_early, wide_late, x_pair, cotangent_pair = call(
-        prepare, [square] * 2 + [(1, features)] + [stacked] * 4 + [pair] * 2,
+        prepare, [square] * 2 + [(1, features)] + [stacked_soon, stacked_last] + [stacked_half] * 2 + [pair] * 2,
         flat_one, one, gain_row, wide_two, activations, cotangent, scratch=[square], flops=cost // 8,
     )
     sent = call(regroup, [message(len(early), False)] * inner, *(first[k] for k in early), data=len(early))
@@ -540,8 +545,8 @@
         scratch=[half], flops=cost,
     )
     partial_input, product_one = call(
-        early_input, [full, (features // 2, features)], *(dy1_parts[k] for k in early), cotangent, scaled_early,
-        x_pair, inverse_root, scratch=[half], flops=cost,
+        early_input, [full, (soon, features)], *(dy1_parts[k] for k in plan.soon), cotangent, scaled_early,
+        x_pair, inverse_root, scratch=[(soon, tokens)], flops=cost,
     )
     output, grad_right_two = call(
         finish_output, [full, (features, count)], *second_late, partial_output, product_two, wide_late,
@@ -550,8 +555,8 @@
     ready, made = [full, (features, count), square, (features, count)], [full, (1, features), square]
     output, grad_right_one, grad_left_two, grad_right_two, input_gradient, gain_gradient, grad_left_one = call(
         finish_input, ready + made, output, grad_right_one, grad_left_two, grad_right_two,
-        *(dy1_parts[k] for k in (*late, *early)), activations, x_pair, gain_kept, turned_one, scaled_late, inverse_root,
-        partial_input, product_one, scratch=[half, square, *made], flops=cost, stores=len(ready + made),
+        *(dy1_parts[k] for k in (*plan.last, *plan.soon)), activations, x_pair, gain_kept, turned_one, scaled_late, inverse_root,
+        partial_input, product_one, scratch=[(features - soon, tokens), square, *made], flops=cost, stores=len(ready + made),
     )
     return (
         output,

time: 70.9 us -> 72.2 us (1.018)
  starting transfers between devices: 35.6 us -> 36.8 us
    ppermute x36, starting transfers between devices: 35.6 us -> 36.8 us  [across(): lax.ppermute(messages[i], 'blocks', [(s, s ^ i * step) for s in range(cou...]
  transfers between devices with their start and end apart: 36 -> 36, of which waited for: 14 -> 11; matrix products, arithmetic and copies ran while one was open for 0% -> 0% of each run, Pallas kernels for 9% -> 9%
where the time goes in v3:
time: 72.2 us; the launch traced here: 72 us
  starting transfers between devices  36.8 us (51%)
  waiting for transfers between devices  23.2 us (32%)
  Pallas kernels  8.57 us (12%)
  local copies, waits for them, and re-layouts  2.51 us (3%)
  between operations  0.91 us (1%)
    ppermute x36, starting transfers between devices, across(): lax.ppermute(messages[i], 'blocks', [(s, s ^ i * step) for s in range(cou...  36.8 us
    ppermute x36, waiting for transfers between devices, across(): lax.ppermute(messages[i], 'blocks', [(s, s ^ i * step) for s in range(cou...  23.2 us
    pallas_call x18, Pallas kernels, call(): pl.pallas_call(functools.partial(kernel, self, len(args), len(outs), **fi...  8.57 us
    unnamed x16, local copies, waits for them, and re-layouts  2.51 us
  transfers between devices with their start and end apart: 36, of which 11 were waited for; matrix products, arithmetic and copies ran while one was open for 0% of the time, Pallas kernels for 9%

profile of v3, /device:TPU:0, one launch (start us, length us, event | category | flops | bytes accessed | tf_op | source)
XLA Modules:
  0.0 72.0 jit_solution(15686484651829966173)
XLA Ops:
  0.6 0.0 copy-start.1
  0.6 1.0 %copy-done.1 = f32[128,1024]{1,0:T(8,128)S(1)} copy-done((f32[128,1024]{1,0:T(8,128)S(1)}, f32[128,1024]{1,0:T(8,128)}, u32[]{:S(2)}) %copy-start.1) | copy-done | bytes 524312
  1.7 0.8 %copy-done.7 = f32[8,16,16]{2,1,0:T(8,128)S(1)} copy-done((f32[8,16,16]{2,1,0:T(8,128)S(1)}, f32[8,16,16]{2,1,0:T(8,128)}, u32[]{:S(2)}) %copy-start.7) | copy-done | bytes 8216
  2.5 0.6 shard_map.129
  3.2 0.6 collective-permute-start.18
  3.7 1.4 %shard_map.126 = (f32[33,8,128]{2,1,0:T(8,128)S(1)}, f32[33,8,128]{2,1,0:T(8,128)S(1)}, f32[33,8,128]{2,1,0:T(8,128)S(1)}, f32[33,8,128]{2,1,0:T(8,128)S(1)}) custom-call(s32[1]{0:T(128)} %bitcast.refs_0_, f32[128,1024]{1,0:T(8,128)} %refs_9_.1, f32[128,128]{1,0:T(8,128)} %bitcast.11, f32[1,128]{1,0:T(1,128)} %bitcast.16), custom_call_target="tpu_custom_call" | custom-call | flops 201326592 | bytes 1131008 | tf_op jit(solution)/shard_map/pallas_call | solution.py:262
  5.2 3.7 %collective-permute-start = (f32[33,8,128]{2,1,0:T(8,128)S(1)}, f32[33,8,128]{2,1,0:T(8,128)S(1)}, u32[]{:S(2)}, u32[]{:S(2)}) collective-permute-start(f32[33,8,128]{2,1,0:T(8,128)S(1)} %get-tuple-element.88), channel_id=1, source_target_pairs={{0,8},{1,9},{2,10},{3,11},{4,12},{5,13},{6,14},{7,15},{8,0},{9,1},... | collective-permute-start | bytes 405512 | tf_op jit(solution)/shard_map/ppermute | solution.py:479
  8.9 1.4 %collective-permute-start.4 = (f32[33,8,128]{2,1,0:T(8,128)S(1)}, f32[33,8,128]{2,1,0:T(8,128)S(1)}, u32[]{:S(2)}, u32[]{:S(2)}) collective-permute-start(f32[33,8,128]{2,1,0:T(8,128)S(1)} %get-tuple-element.93), channel_id=1, source_target_pairs={{0,12},{1,13},{2,14},{3,15},{4,8},{5,9},{6,10},{7,11},{8,4},{9,5},... | collective-permute-start | bytes 405512 | tf_op jit(solution)/shard_map/ppermute | solution.py:479
  10.2 0.2 collective-permute-start.5
  10.4 1.5 %collective-permute-start.19 = (f32[16,8,128]{2,1,0:T(8,128)S(1)}, f32[16,8,128]{2,1,0:T(8,128)S(1)}, u32[]{:S(2)}, u32[]{:S(2)}) collective-permute-start(f32[16,8,128]{2,1,0:T(8,128)S(1)} %get-tuple-element.122), channel_id=1, source_target_pairs={{0,2},{1,3},{2,0},{3,1},{4,6},{5,7},{6,4},{7,5},{8,10},{9,11},{10,... | collective-permute-start | bytes 196616 | tf_op jit(solution)/shard_map/ppermute | solution.py:479
  12.0 0.0 collective-permute-done.18.refs_2_
  12.0 0.0 collective-permute-start.20
  12.0 2.7 %collective-permute-done.19.refs_3_ = f32[16,8,128]{2,1,0:T(8,128)S(1)} collective-permute-done((f32[16,8,128]{2,1,0:T(8,128)S(1)}, f32[16,8,128]{2,1,0:T(8,128)S(1)}, u32[]{:S(2)}, u32[]{:S(2)}) %collective-permute-start.19) | collective-permute-done | bytes 65568 | tf_op jit(solution)/shard_map/ppermute | solution.py:479
  14.7 1.5 %collective-permute-done.20.refs_4_ = f32[16,8,128]{2,1,0:T(8,128)S(1)} collective-permute-done((f32[16,8,128]{2,1,0:T(8,128)S(1)}, f32[16,8,128]{2,1,0:T(8,128)S(1)}, u32[]{:S(2)}, u32[]{:S(2)}) %collective-permute-start.20) | collective-permute-done | bytes 65568 | tf_op jit(solution)/shard_map/ppermute | solution.py:479
  16.2 0.7 collective-permute-start.23
  16.9 2.3 %collective-permute-done.refs_2_.refs_4_ = f32[33,8,128]{2,1,0:T(8,128)S(1)} collective-permute-done((f32[33,8,128]{2,1,0:T(8,128)S(1)}, f32[33,8,128]{2,1,0:T(8,128)S(1)}, u32[]{:S(2)}, u32[]{:S(2)}) %collective-permute-start) | collective-permute-done | bytes 135200 | tf_op jit(solution)/shard_map/ppermute | solution.py:479
  19.1 0.6 collective-permute-start.24
  19.8 1.4 %collective-permute-start.1 = (f32[16,8,128]{2,1,0:T(8,128)S(1)}, f32[16,8,128]{2,1,0:T(8,128)S(1)}, u32[]{:S(2)}, u32[]{:S(2)}) collective-permute-start(f32[16,8,128]{2,1,0:T(8,128)S(1)} %get-tuple-element.90), channel_id=1, source_target_pairs={{0,1},{1,0},{2,3},{3,2},{4,5},{5,4},{6,7},{7,6},{8,9},{9,8},{10,11... | collective-permute-start | bytes 196616 | tf_op jit(solution)/shard_map/ppermute | solution.py:479
  21.2 0.0 collective-permute-done.5.refs_2_
  21.2 0.6 collective-permute-start.2
  21.9 0.1 collective-permute-start.6
  22.0 1.5 %collective-permute-start.3 = (f32[16,8,128]{2,1,0:T(8,128)S(1)}, f32[16,8,128]{2,1,0:T(8,128)S(1)}, u32[]{:S(2)}, u32[]{:S(2)}) collective-permute-start(f32[16,8,128]{2,1,0:T(8,128)S(1)} %get-tuple-element.92), channel_id=1, source_target_pairs={{0,3},{1,2},{2,1},{3,0},{4,7},{5,6},{6,5},{7,4},{8,11},{9,10},{10,... | collective-permute-start | bytes 196616 | tf_op jit(solution)/shard_map/ppermute | solution.py:479
  23.5 0.0 collective-permute-done.24.refs_4_
  23.5 1.5 %collective-permute-start.21 = (f32[32,8,128]{2,1,0:T(8,128)S(1)}, f32[32,8,128]{2,1,0:T(8,128)S(1)}, u32[]{:S(2)}, u32[]{:S(2)}) collective-permute-start(f32[32,8,128]{2,1,0:T(8,128)S(1)} %get-tuple-element.125), channel_id=1, source_target_pairs={{0,4},{1,5},{2,6},{3,7},{4,0},{5,1},{6,2},{7,3},{8,12},{9,13},{10,... | collective-permute-start | bytes 393224 | tf_op jit(solution)/shard_map/ppermute | solution.py:479
  25.0 0.0 collective-permute-done.1.refs_2_
  25.1 2.3 %collective-permute-start.25 = (f32[32,8,128]{2,1,0:T(8,128)S(1)}, f32[32,8,128]{2,1,0:T(8,128)S(1)}, u32[]{:S(2)}, u32[]{:S(2)}) collective-permute-start(f32[32,8,128]{2,1,0:T(8,128)S(1)} %get-tuple-element.130), channel_id=1, source_target_pairs={{0,8},{1,9},{2,10},{3,11},{4,12},{5,13},{6,14},{7,15},{8,0},{9,1},... | collective-permute-start | bytes 393224 | tf_op jit(solution)/shard_map/ppermute | solution.py:479
  27.4 0.0 collective-permute-done.2.refs_3_
  27.4 1.2 %collective-permute-start.26 = (f32[32,8,128]{2,1,0:T(8,128)S(1)}, f32[32,8,128]{2,1,0:T(8,128)S(1)}, u32[]{:S(2)}, u32[]{:S(2)}) collective-permute-start(f32[32,8,128]{2,1,0:T(8,128)S(1)} %get-tuple-element.131), channel_id=1, source_target_pairs={{0,12},{1,13},{2,14},{3,15},{4,8},{5,9},{6,10},{7,11},{8,4},{9,5},... | collective-permute-start | bytes 393224 | tf_op jit(solution)/shard_map/ppermute | solution.py:479
  28.6 0.0 collective-permute-done.3.refs_4_
  28.6 1.6 %collective-permute-start.7 = (f32[17,8,128]{2,1,0:T(8,128)S(1)}, f32[17,8,128]{2,1,0:T(8,128)S(1)}, u32[]{:S(2)}, u32[]{:S(2)}) collective-permute-start(f32[17,8,128]{2,1,0:T(8,128)S(1)} %get-tuple-element.97), channel_id=1, source_target_pairs={{0,2},{1,3},{2,0},{3,1},{4,6},{5,7},{6,4},{7,5},{8,10},{9,11},{10,... | collective-permute-start | bytes 208904 | tf_op jit(solution)/shard_map/ppermute | solution.py:479
  30.2 0.0 collective-permute-done.6.refs_6_
  30.2 0.0 collective-permute-start.8
  30.3 0.6 copy-done.6
  30.9 0.5 shard_map.130
  31.4 1.5 %collective-permute-done.7.refs_7_ = f32[17,8,128]{2,1,0:T(8,128)S(1)} collective-permute-done((f32[17,8,128]{2,1,0:T(8,128)S(1)}, f32[17,8,128]{2,1,0:T(8,128)S(1)}, u32[]{:S(2)}, u32[]{:S(2)}) %collective-permute-start.7) | collective-permute-done | bytes 69664 | tf_op jit(solution)/shard_map/ppermute | solution.py:479
  32.9 1.5 %collective-permute-done.8.refs_8_ = f32[17,8,128]{2,1,0:T(8,128)S(1)} collective-permute-done((f32[17,8,128]{2,1,0:T(8,128)S(1)}, f32[17,8,128]{2,1,0:T(8,128)S(1)}, u32[]{:S(2)}, u32[]{:S(2)}) %collective-permute-start.8) | collective-permute-done | bytes 69664 | tf_op jit(solution)/shard_map/ppermute | solution.py:479
  34.4 1.0 %shard_map.131 = (f32[32,8,128]{2,1,0:T(8,128)S(1)}, f32[32,8,128]{2,1,0:T(8,128)S(1)}, f32[32,8,128]{2,1,0:T(8,128)S(1)}, f32[32,8,128]{2,1,0:T(8,128)S(1)}, f3...) custom-call(s32[1]{0:T(128)} %bitcast.refs_0_, ...), custom_call_target="tpu_custom_call" | custom-call | flops 402653184 | bytes 3297280 | tf_op jit(solution)/shard_map/pallas_call | solution.py:262
  35.4 2.7 %collective-permute-start.9 = (f32[32,8,128]{2,1,0:T(8,128)S(1)}, f32[32,8,128]{2,1,0:T(8,128)S(1)}, u32[]{:S(2)}, u32[]{:S(2)}) collective-permute-start(f32[32,8,128]{2,1,0:T(8,128)S(1)} %get-tuple-element.101), channel_id=1, source_target_pairs={{0,12},{1,13},{2,14},{3,15},{4,8},{5,9},{6,10},{7,11},{8,4},{9,5},... | collective-permute-start | bytes 393224 | tf_op jit(solution)/shard_map/ppermute | solution.py:479
  38.1 1.8 %collective-permute-start.14 = (f32[32,8,128]{2,1,0:T(8,128)S(1)}, f32[32,8,128]{2,1,0:T(8,128)S(1)}, u32[]{:S(2)}, u32[]{:S(2)}) collective-permute-start(f32[32,8,128]{2,1,0:T(8,128)S(1)} %get-tuple-element.108), channel_id=1, source_target_pairs={{0,8},{1,9},{2,10},{3,11},{4,12},{5,13},{6,14},{7,15},{8,0},{9,1},... | collective-permute-start | bytes 393224 | tf_op jit(solution)/shard_map/ppermute | solution.py:479
  39.9 0.7 shard_map.138
  40.5 0.1 collective-permute-start.27
  40.6 0.8 %collective-permute-start.28 = (f32[16,8,128]{2,1,0:T(8,128)S(1)}, f32[16,8,128]{2,1,0:T(8,128)S(1)}, u32[]{:S(2)}, u32[]{:S(2)}) collective-permute-start(f32[16,8,128]{2,1,0:T(8,128)S(1)} %get-tuple-element.142), channel_id=1, source_target_pairs={{0,2},{1,3},{2,0},{3,1},{4,6},{5,7},{6,4},{7,5},{8,10},{9,11},{10,... | collective-permute-start | bytes 196616 | tf_op jit(solution)/shard_map/ppermute | solution.py:479
  41.4 0.5 collective-permute-done.27.refs_2_
  41.9 0.2 collective-permute-start.30
  42.0 1.6 %collective-permute-done.9.refs_1_ = f32[32,8,128]{2,1,0:T(8,128)S(1)} collective-permute-done((f32[32,8,128]{2,1,0:T(8,128)S(1)}, f32[32,8,128]{2,1,0:T(8,128)S(1)}, u32[]{:S(2)}, u32[]{:S(2)}) %collective-permute-start.9) | collective-permute-done | bytes 131104 | tf_op jit(solution)/shard_map/ppermute | solution.py:479
  43.6 0.8 %collective-permute-start.31 = (f32[17,8,128]{2,1,0:T(8,128)S(1)}, f32[17,8,128]{2,1,0:T(8,128)S(1)}, u32[]{:S(2)}, u32[]{:S(2)}) collective-permute-start(f32[17,8,128]{2,1,0:T(8,128)S(1)} %get-tuple-element.146), channel_id=1, source_target_pairs={{0,2},{1,3},{2,0},{3,1},{4,6},{5,7},{6,4},{7,5},{8,10},{9,11},{10,... | collective-permute-start | bytes 208904 | tf_op jit(solution)/shard_map/ppermute | solution.py:479
  44.4 1.1 %collective-permute-done.10.refs_2_ = f32[32,8,128]{2,1,0:T(8,128)S(1)} collective-permute-done((f32[32,8,128]{2,1,0:T(8,128)S(1)}, f32[32,8,128]{2,1,0:T(8,128)S(1)}, u32[]{:S(2)}, u32[]{:S(2)}) %collective-permute-start.10) | collective-permute-done | bytes 131104 | tf_op jit(solution)/shard_map/ppermute | solution.py:479
  45.5 1.3 %collective-permute-start.32 = (f32[17,8,128]{2,1,0:T(8,128)S(1)}, f32[17,8,128]{2,1,0:T(8,128)S(1)}, u32[]{:S(2)}, u32[]{:S(2)}) collective-permute-start(f32[17,8,128]{2,1,0:T(8,128)S(1)} %get-tuple-element.147), channel_id=1, source_target_pairs={{0,3},{1,2},{2,1},{3,0},{4,7},{5,6},{6,5},{7,4},{8,11},{9,10},{10,... | collective-permute-start | bytes 208904 | tf_op jit(solution)/shard_map/ppermute | solution.py:479
  46.8 0.5 collective-permute-start.29
  47.3 3.7 %collective-permute-done.14.refs_2_ = f32[32,8,128]{2,1,0:T(8,128)S(1)} collective-permute-done((f32[32,8,128]{2,1,0:T(8,128)S(1)}, f32[32,8,128]{2,1,0:T(8,128)S(1)}, u32[]{:S(2)}, u32[]{:S(2)}) %collective-permute-start.14) | collective-permute-done | bytes 131104 | tf_op jit(solution)/shard_map/ppermute | solution.py:479
  51.0 0.6 collective-permute-start.15
  51.6 1.5 %collective-permute-start.16 = (f32[16,8,128]{2,1,0:T(8,128)S(1)}, f32[16,8,128]{2,1,0:T(8,128)S(1)}, u32[]{:S(2)}, u32[]{:S(2)}) collective-permute-start(f32[16,8,128]{2,1,0:T(8,128)S(1)} %get-tuple-element.111), channel_id=1, source_target_pairs={{0,2},{1,3},{2,0},{3,1},{4,6},{5,7},{6,4},{7,5},{8,10},{9,11},{10,... | collective-permute-start | bytes 196616 | tf_op jit(solution)/shard_map/ppermute | solution.py:479
  53.2 3.9 %collective-permute-start.34 = (f32[33,8,128]{2,1,0:T(8,128)S(1)}, f32[33,8,128]{2,1,0:T(8,128)S(1)}, u32[]{:S(2)}, u32[]{:S(2)}) collective-permute-start(f32[33,8,128]{2,1,0:T(8,128)S(1)} %get-tuple-element.150), channel_id=1, source_target_pairs={{0,4},{1,5},{2,6},{3,7},{4,0},{5,1},{6,2},{7,3},{8,12},{9,13},{10,... | collective-permute-start | bytes 405512 | tf_op jit(solution)/shard_map/ppermute | solution.py:479
  57.1 1.7 %collective-permute-start.35 = (f32[33,8,128]{2,1,0:T(8,128)S(1)}, f32[33,8,128]{2,1,0:T(8,128)S(1)}, u32[]{:S(2)}, u32[]{:S(2)}) collective-permute-start(f32[33,8,128]{2,1,0:T(8,128)S(1)} %get-tuple-element.151), channel_id=1, source_target_pairs={{0,8},{1,9},{2,10},{3,11},{4,12},{5,13},{6,14},{7,15},{8,0},{9,1},... | collective-permute-start | bytes 405512 | tf_op jit(solution)/shard_map/ppermute | solution.py:479
  58.8 1.4 %collective-permute-start.33 = (f32[33,8,128]{2,1,0:T(8,128)S(1)}, f32[33,8,128]{2,1,0:T(8,128)S(1)}, u32[]{:S(2)}, u32[]{:S(2)}) collective-permute-start(f32[33,8,128]{2,1,0:T(8,128)S(1)} %get-tuple-element.148), channel_id=1, source_target_pairs={{0,12},{1,13},{2,14},{3,15},{4,8},{5,9},{6,10},{7,11},{8,4},{9,5},... | collective-permute-start | bytes 405512 | tf_op jit(solution)/shard_map/ppermute | solution.py:479
  60.2 0.2 collective-permute-start.12
  60.4 0.5 collective-permute-start.13
  60.9 1.0 %shard_map.139 = (f32[128,16]{1,0:T(8,128)S(1)}, f32[128,128]{1,0:T(8,128)S(1)}) custom-call(s32[1]{0:T(128)} %bitcast.refs_0_, f32[128,1024]{1,0:T(8,128)S(1)} %get-tuple-element.119.refs_1_, f32[128,1024]{1,0:T(8,128)S(1)} %get-tuple-element.134.refs_2_, f32[128,1024]{1,0:T(8,128)S(1)} %get-tuple-element.135.refs_3_, ...), custom_call_target="tpu_custom_call" | custom-call | flops 402653184 | bytes 2170880 | tf_op jit(solution)/shard_map/pallas_call | solution.py:262
  62.0 0.4 shard_map.134
  62.4 2.4 %collective-permute-done.12.refs_3_ = f32[16,8,128]{2,1,0:T(8,128)S(1)} collective-permute-done((f32[16,8,128]{2,1,0:T(8,128)S(1)}, f32[16,8,128]{2,1,0:T(8,128)S(1)}, u32[]{:S(2)}, u32[]{:S(2)}) %collective-permute-start.12) | collective-permute-done | bytes 65568 | tf_op jit(solution)/shard_map/ppermute | solution.py:479
  64.8 0.8 %shard_map.135 = (f32[128,1024]{1,0:T(8,128)S(1)}, f32[128,16]{1,0:T(8,128)S(1)}) custom-call(s32[1]{0:T(128)} %bitcast.refs_0_, f32[16,8,128]{2,1,0:T(8,128)S(1)} %get-tuple-element.103.refs_1_, f32[16,8,128]{2,1,0:T(8,128)S(1)} %collective-permute-done.11.refs_2_, f32[16,8,128]{2,1,0:T(8,128)S(1)} %collective-permute-done.12.refs_3_, ...), custom_call_target="tpu_custom_call" | custom-call | flops 201326592 | bytes 2531328 | tf_op jit(solution)/shard_map/pallas_call | solution.py:262
  65.6 4.4 %collective-permute-done.35.refs_3_.refs_8_ = f32[33,8,128]{2,1,0:T(8,128)S(1)} collective-permute-done((f32[33,8,128]{2,1,0:T(8,128)S(1)}, f32[33,8,128]{2,1,0:T(8,128)S(1)}, u32[]{:S(2)}, u32[]{:S(2)}) %collective-permute-start.35) | collective-permute-done | bytes 135200 | tf_op jit(solution)/shard_map/ppermute | solution.py:479
  70.1 0.5 shard_map.142
  70.6 1.4 %shard_map.143 = (f32[128,1024]{1,0:T(8,128)}, f32[128,16]{1,0:T(8,128)}, f32[128,128]{1,0:T(8,128)}, f32[128,16]{1,0:T(8,128)}, f32[128,1024]{1,0:T(8,128)}, /*index=5*/f32[1,128]{1,0:T(1,128)}, f32[128,128]{1,0:T(8,128)}) custom-call(s32[1]{0:T(128)} %bitcast.refs_0_, f32[128,1024]{1,0:T(8,128)S(1)} %get-tuple-element.118.refs_1_, ...), custom_call_target="tpu_custom_call" | custom-call | flops 201326592 | bytes 4625408 | tf_op jit(solution)/shard_map/pallas_call | solution.py:262
  (42 shorter events, 0.2 us)
Async XLA Ops:
  0.6 1.0 %copy-start.1 = (f32[128,1024]{1,0:T(8,128)S(1)}, f32[128,1024]{1,0:T(8,128)}, u32[]{:S(2)}) copy-start(f32[128,1024]{1,0:T(8,128)} %refs_4_.1) | copy-start | bytes 1572868
  1.7 0.8 %copy-start.7 = (f32[8,16,16]{2,1,0:T(8,128)S(1)}, f32[8,16,16]{2,1,0:T(8,128)}, u32[]{:S(2)}) copy-start(f32[8,16,16]{2,1,0:T(8,128)} %param.13) | copy-start | bytes 24580
  3.2 8.8 %collective-permute-start.18 = (f32[16,8,128]{2,1,0:T(8,128)S(1)}, f32[16,8,128]{2,1,0:T(8,128)S(1)}, u32[]{:S(2)}, u32[]{:S(2)}) collective-permute-start(f32[16,8,128]{2,1,0:T(8,128)S(1)} %get-tuple-element.121), channel_id=1, source_target_pairs={{0,1},{1,0},{2,3},{3,2},{4,5},{5,4},{6,7},{7,6},{8,9},{9,8},{10,11... | collective-permute-start | bytes 196616 | tf_op jit(solution)/shard_map/ppermute | solution.py:479
  5.2 13.9 %collective-permute-start = (f32[33,8,128]{2,1,0:T(8,128)S(1)}, f32[33,8,128]{2,1,0:T(8,128)S(1)}, u32[]{:S(2)}, u32[]{:S(2)}) collective-permute-start(f32[33,8,128]{2,1,0:T(8,128)S(1)} %get-tuple-element.88), channel_id=1, source_target_pairs={{0,8},{1,9},{2,10},{3,11},{4,12},{5,13},{6,14},{7,15},{8,0},{9,1},... | collective-permute-start | bytes 405512 | tf_op jit(solution)/shard_map/ppermute | solution.py:479
  8.9 10.9 %collective-permute-start.4 = (f32[33,8,128]{2,1,0:T(8,128)S(1)}, f32[33,8,128]{2,1,0:T(8,128)S(1)}, u32[]{:S(2)}, u32[]{:S(2)}) collective-permute-start(f32[33,8,128]{2,1,0:T(8,128)S(1)} %get-tuple-element.93), channel_id=1, source_target_pairs={{0,12},{1,13},{2,14},{3,15},{4,8},{5,9},{6,10},{7,11},{8,4},{9,5},... | collective-permute-start | bytes 405512 | tf_op jit(solution)/shard_map/ppermute | solution.py:479
  10.2 11.0 %collective-permute-start.5 = (f32[33,8,128]{2,1,0:T(8,128)S(1)}, f32[33,8,128]{2,1,0:T(8,128)S(1)}, u32[]{:S(2)}, u32[]{:S(2)}) collective-permute-start(f32[33,8,128]{2,1,0:T(8,128)S(1)} %get-tuple-element.94), channel_id=1, source_target_pairs={{0,4},{1,5},{2,6},{3,7},{4,0},{5,1},{6,2},{7,3},{8,12},{9,13},{10,... | collective-permute-start | bytes 405512 | tf_op jit(solution)/shard_map/ppermute | solution.py:479
  10.4 4.3 %collective-permute-start.19 = (f32[16,8,128]{2,1,0:T(8,128)S(1)}, f32[16,8,128]{2,1,0:T(8,128)S(1)}, u32[]{:S(2)}, u32[]{:S(2)}) collective-permute-start(f32[16,8,128]{2,1,0:T(8,128)S(1)} %get-tuple-element.122), channel_id=1, source_target_pairs={{0,2},{1,3},{2,0},{3,1},{4,6},{5,7},{6,4},{7,5},{8,10},{9,11},{10,... | collective-permute-start | bytes 196616 | tf_op jit(solution)/shard_map/ppermute | solution.py:479
  12.0 4.2 %collective-permute-start.20 = (f32[16,8,128]{2,1,0:T(8,128)S(1)}, f32[16,8,128]{2,1,0:T(8,128)S(1)}, u32[]{:S(2)}, u32[]{:S(2)}) collective-permute-start(f32[16,8,128]{2,1,0:T(8,128)S(1)} %get-tuple-element.123), channel_id=1, source_target_pairs={{0,3},{1,2},{2,1},{3,0},{4,7},{5,6},{6,5},{7,4},{8,11},{9,10},{10,... | collective-permute-start | bytes 196616 | tf_op jit(solution)/shard_map/ppermute | solution.py:479
  14.7 7.2 %collective-permute-start.22 = (f32[16,8,128]{2,1,0:T(8,128)S(1)}, f32[16,8,128]{2,1,0:T(8,128)S(1)}, u32[]{:S(2)}, u32[]{:S(2)}) collective-permute-start(f32[16,8,128]{2,1,0:T(8,128)S(1)} %get-tuple-element.127), channel_id=1, source_target_pairs={{0,1},{1,0},{2,3},{3,2},{4,5},{5,4},{6,7},{7,6},{8,9},{9,8},{10,11... | collective-permute-start | bytes 196616 | tf_op jit(solution)/shard_map/ppermute | solution.py:479
  16.2 5.8 %collective-permute-start.23 = (f32[16,8,128]{2,1,0:T(8,128)S(1)}, f32[16,8,128]{2,1,0:T(8,128)S(1)}, u32[]{:S(2)}, u32[]{:S(2)}) collective-permute-start(f32[16,8,128]{2,1,0:T(8,128)S(1)} %get-tuple-element.128), channel_id=1, source_target_pairs={{0,2},{1,3},{2,0},{3,1},{4,6},{5,7},{6,4},{7,5},{8,10},{9,11},{10,... | collective-permute-start | bytes 196616 | tf_op jit(solution)/shard_map/ppermute | solution.py:479
  19.1 4.4 %collective-permute-start.24 = (f32[16,8,128]{2,1,0:T(8,128)S(1)}, f32[16,8,128]{2,1,0:T(8,128)S(1)}, u32[]{:S(2)}, u32[]{:S(2)}) collective-permute-start(f32[16,8,128]{2,1,0:T(8,128)S(1)} %get-tuple-element.129), channel_id=1, source_target_pairs={{0,3},{1,2},{2,1},{3,0},{4,7},{5,6},{6,5},{7,4},{8,11},{9,10},{10,... | collective-permute-start | bytes 196616 | tf_op jit(solution)/shard_map/ppermute | solution.py:479
  19.7 10.5 %copy-start.3 = (f32[1,128,128]{2,1,0:T(8,128)S(1)}, f32[1,128,128]{2,1,0:T(8,128)}, u32[]{:S(2)}) copy-start(f32[1,128,128]{2,1,0:T(8,128)} %param.10) | copy-start | bytes 196612
  19.7 10.5 %copy-start.4 = (f32[8,16,16]{2,1,0:T(8,128)S(1)}, f32[8,16,16]{2,1,0:T(8,128)}, u32[]{:S(2)}) copy-start(f32[8,16,16]{2,1,0:T(8,128)} %param.11) | copy-start | bytes 24580
  19.8 5.3 %collective-permute-start.1 = (f32[16,8,128]{2,1,0:T(8,128)S(1)}, f32[16,8,128]{2,1,0:T(8,128)S(1)}, u32[]{:S(2)}, u32[]{:S(2)}) collective-permute-start(f32[16,8,128]{2,1,0:T(8,128)S(1)} %get-tuple-element.90), channel_id=1, source_target_pairs={{0,1},{1,0},{2,3},{3,2},{4,5},{5,4},{6,7},{7,6},{8,9},{9,8},{10,11... | collective-permute-start | bytes 196616 | tf_op jit(solution)/shard_map/ppermute | solution.py:479
  21.2 9.0 %copy-start = (f32[128,1024]{1,0:T(8,128)S(1)}, f32[128,1024]{1,0:T(8,128)}, u32[]{:S(2)}) copy-start(f32[128,1024]{1,0:T(8,128)} %refs_9_.1) | copy-start | bytes 1572868
  21.2 9.0 %copy-start.2 = (f32[128,1024]{1,0:T(8,128)S(1)}, f32[128,1024]{1,0:T(8,128)}, u32[]{:S(2)}) copy-start(f32[128,1024]{1,0:T(8,128)} %refs_4_.1) | copy-start | bytes 1572868
  21.2 6.2 %collective-permute-start.2 = (f32[16,8,128]{2,1,0:T(8,128)S(1)}, f32[16,8,128]{2,1,0:T(8,128)S(1)}, u32[]{:S(2)}, u32[]{:S(2)}) collective-permute-start(f32[16,8,128]{2,1,0:T(8,128)S(1)} %get-tuple-element.91), channel_id=1, source_target_pairs={{0,2},{1,3},{2,0},{3,1},{4,6},{5,7},{6,4},{7,5},{8,10},{9,11},{10,... | collective-permute-start | bytes 196616 | tf_op jit(solution)/shard_map/ppermute | solution.py:479
  21.9 8.3 %collective-permute-start.6 = (f32[17,8,128]{2,1,0:T(8,128)S(1)}, f32[17,8,128]{2,1,0:T(8,128)S(1)}, u32[]{:S(2)}, u32[]{:S(2)}) collective-permute-start(f32[17,8,128]{2,1,0:T(8,128)S(1)} %get-tuple-element.96), channel_id=1, source_target_pairs={{0,1},{1,0},{2,3},{3,2},{4,5},{5,4},{6,7},{7,6},{8,9},{9,8},{10,11... | collective-permute-start | bytes 208904 | tf_op jit(solution)/shard_map/ppermute | solution.py:479
  22.0 6.6 %collective-permute-start.3 = (f32[16,8,128]{2,1,0:T(8,128)S(1)}, f32[16,8,128]{2,1,0:T(8,128)S(1)}, u32[]{:S(2)}, u32[]{:S(2)}) collective-permute-start(f32[16,8,128]{2,1,0:T(8,128)S(1)} %get-tuple-element.92), channel_id=1, source_target_pairs={{0,3},{1,2},{2,1},{3,0},{4,7},{5,6},{6,5},{7,4},{8,11},{9,10},{10,... | collective-permute-start | bytes 196616 | tf_op jit(solution)/shard_map/ppermute | solution.py:479
  23.5 14.6 %collective-permute-start.21 = (f32[32,8,128]{2,1,0:T(8,128)S(1)}, f32[32,8,128]{2,1,0:T(8,128)S(1)}, u32[]{:S(2)}, u32[]{:S(2)}) collective-permute-start(f32[32,8,128]{2,1,0:T(8,128)S(1)} %get-tuple-element.125), channel_id=1, source_target_pairs={{0,4},{1,5},{2,6},{3,7},{4,0},{5,1},{6,2},{7,3},{8,12},{9,13},{10,... | collective-permute-start | bytes 393224 | tf_op jit(solution)/shard_map/ppermute | solution.py:479
  25.1 14.8 %collective-permute-start.25 = (f32[32,8,128]{2,1,0:T(8,128)S(1)}, f32[32,8,128]{2,1,0:T(8,128)S(1)}, u32[]{:S(2)}, u32[]{:S(2)}) collective-permute-start(f32[32,8,128]{2,1,0:T(8,128)S(1)} %get-tuple-element.130), channel_id=1, source_target_pairs={{0,8},{1,9},{2,10},{3,11},{4,12},{5,13},{6,14},{7,15},{8,0},{9,1},... | collective-permute-start | bytes 393224 | tf_op jit(solution)/shard_map/ppermute | solution.py:479
  27.4 12.5 %collective-permute-start.26 = (f32[32,8,128]{2,1,0:T(8,128)S(1)}, f32[32,8,128]{2,1,0:T(8,128)S(1)}, u32[]{:S(2)}, u32[]{:S(2)}) collective-permute-start(f32[32,8,128]{2,1,0:T(8,128)S(1)} %get-tuple-element.131), channel_id=1, source_target_pairs={{0,12},{1,13},{2,14},{3,15},{4,8},{5,9},{6,10},{7,11},{8,4},{9,5},... | collective-permute-start | bytes 393224 | tf_op jit(solution)/shard_map/ppermute | solution.py:479
  28.6 4.3 %collective-permute-start.7 = (f32[17,8,128]{2,1,0:T(8,128)S(1)}, f32[17,8,128]{2,1,0:T(8,128)S(1)}, u32[]{:S(2)}, u32[]{:S(2)}) collective-permute-start(f32[17,8,128]{2,1,0:T(8,128)S(1)} %get-tuple-element.97), channel_id=1, source_target_pairs={{0,2},{1,3},{2,0},{3,1},{4,6},{5,7},{6,4},{7,5},{8,10},{9,11},{10,... | collective-permute-start | bytes 208904 | tf_op jit(solution)/shard_map/ppermute | solution.py:479
  30.2 4.2 %collective-permute-start.8 = (f32[17,8,128]{2,1,0:T(8,128)S(1)}, f32[17,8,128]{2,1,0:T(8,128)S(1)}, u32[]{:S(2)}, u32[]{:S(2)}) collective-permute-start(f32[17,8,128]{2,1,0:T(8,128)S(1)} %get-tuple-element.98), channel_id=1, source_target_pairs={{0,3},{1,2},{2,1},{3,0},{4,7},{5,6},{6,5},{7,4},{8,11},{9,10},{10,... | collective-permute-start | bytes 208904 | tf_op jit(solution)/shard_map/ppermute | solution.py:479
  30.2 0.7 copy-start.6
  30.9 3.5 %copy-start.5 = (f32[1,128,128]{2,1,0:T(8,128)S(1)}, f32[1,128,128]{2,1,0:T(8,128)}, u32[]{:S(2)}) copy-start(f32[1,128,128]{2,1,0:T(8,128)} %param.12) | copy-start | bytes 196612
  35.4 8.2 %collective-permute-start.9 = (f32[32,8,128]{2,1,0:T(8,128)S(1)}, f32[32,8,128]{2,1,0:T(8,128)S(1)}, u32[]{:S(2)}, u32[]{:S(2)}) collective-permute-start(f32[32,8,128]{2,1,0:T(8,128)S(1)} %get-tuple-element.101), channel_id=1, source_target_pairs={{0,12},{1,13},{2,14},{3,15},{4,8},{5,9},{6,10},{7,11},{8,4},{9,5},... | collective-permute-start | bytes 393224 | tf_op jit(solution)/shard_map/ppermute | solution.py:479
  38.1 7.4 %collective-permute-start.10 = (f32[32,8,128]{2,1,0:T(8,128)S(1)}, f32[32,8,128]{2,1,0:T(8,128)S(1)}, u32[]{:S(2)}, u32[]{:S(2)}) collective-permute-start(f32[32,8,128]{2,1,0:T(8,128)S(1)} %get-tuple-element.102), channel_id=1, source_target_pairs={{0,4},{1,5},{2,6},{3,7},{4,0},{5,1},{6,2},{7,3},{8,12},{9,13},{10,... | collective-permute-start | bytes 393224 | tf_op jit(solution)/shard_map/ppermute | solution.py:479
  38.1 12.9 %collective-permute-start.14 = (f32[32,8,128]{2,1,0:T(8,128)S(1)}, f32[32,8,128]{2,1,0:T(8,128)S(1)}, u32[]{:S(2)}, u32[]{:S(2)}) collective-permute-start(f32[32,8,128]{2,1,0:T(8,128)S(1)} %get-tuple-element.108), channel_id=1, source_target_pairs={{0,8},{1,9},{2,10},{3,11},{4,12},{5,13},{6,14},{7,15},{8,0},{9,1},... | collective-permute-start | bytes 393224 | tf_op jit(solution)/shard_map/ppermute | solution.py:479
  40.5 1.3 %collective-permute-start.27 = (f32[16,8,128]{2,1,0:T(8,128)S(1)}, f32[16,8,128]{2,1,0:T(8,128)S(1)}, u32[]{:S(2)}, u32[]{:S(2)}) collective-permute-start(f32[16,8,128]{2,1,0:T(8,128)S(1)} %get-tuple-element.141), channel_id=1, source_target_pairs={{0,1},{1,0},{2,3},{3,2},{4,5},{5,4},{6,7},{7,6},{8,9},{9,8},{10,11... | collective-permute-start | bytes 196616 | tf_op jit(solution)/shard_map/ppermute | solution.py:479
  40.6 6.2 %collective-permute-start.28 = (f32[16,8,128]{2,1,0:T(8,128)S(1)}, f32[16,8,128]{2,1,0:T(8,128)S(1)}, u32[]{:S(2)}, u32[]{:S(2)}) collective-permute-start(f32[16,8,128]{2,1,0:T(8,128)S(1)} %get-tuple-element.142), channel_id=1, source_target_pairs={{0,2},{1,3},{2,0},{3,1},{4,6},{5,7},{6,4},{7,5},{8,10},{9,11},{10,... | collective-permute-start | bytes 196616 | tf_op jit(solution)/shard_map/ppermute | solution.py:479
  41.9 9.2 %collective-permute-start.30 = (f32[17,8,128]{2,1,0:T(8,128)S(1)}, f32[17,8,128]{2,1,0:T(8,128)S(1)}, u32[]{:S(2)}, u32[]{:S(2)}) collective-permute-start(f32[17,8,128]{2,1,0:T(8,128)S(1)} %get-tuple-element.145), channel_id=1, source_target_pairs={{0,1},{1,0},{2,3},{3,2},{4,5},{5,4},{6,7},{7,6},{8,9},{9,8},{10,11... | collective-permute-start | bytes 208904 | tf_op jit(solution)/shard_map/ppermute | solution.py:479
  43.6 8.0 %collective-permute-start.31 = (f32[17,8,128]{2,1,0:T(8,128)S(1)}, f32[17,8,128]{2,1,0:T(8,128)S(1)}, u32[]{:S(2)}, u32[]{:S(2)}) collective-permute-start(f32[17,8,128]{2,1,0:T(8,128)S(1)} %get-tuple-element.146), channel_id=1, source_target_pairs={{0,2},{1,3},{2,0},{3,1},{4,6},{5,7},{6,4},{7,5},{8,10},{9,11},{10,... | collective-permute-start | bytes 208904 | tf_op jit(solution)/shard_map/ppermute | solution.py:479
  45.5 7.7 %collective-permute-start.32 = (f32[17,8,128]{2,1,0:T(8,128)S(1)}, f32[17,8,128]{2,1,0:T(8,128)S(1)}, u32[]{:S(2)}, u32[]{:S(2)}) collective-permute-start(f32[17,8,128]{2,1,0:T(8,128)S(1)} %get-tuple-element.147), channel_id=1, source_target_pairs={{0,3},{1,2},{2,1},{3,0},{4,7},{5,6},{6,5},{7,4},{8,11},{9,10},{10,... | collective-permute-start | bytes 208904 | tf_op jit(solution)/shard_map/ppermute | solution.py:479
  46.8 6.3 %collective-permute-start.29 = (f32[16,8,128]{2,1,0:T(8,128)S(1)}, f32[16,8,128]{2,1,0:T(8,128)S(1)}, u32[]{:S(2)}, u32[]{:S(2)}) collective-permute-start(f32[16,8,128]{2,1,0:T(8,128)S(1)} %get-tuple-element.143), channel_id=1, source_target_pairs={{0,3},{1,2},{2,1},{3,0},{4,7},{5,6},{6,5},{7,4},{8,11},{9,10},{10,... | collective-permute-start | bytes 196616 | tf_op jit(solution)/shard_map/ppermute | solution.py:479
  51.0 6.1 %collective-permute-start.11 = (f32[16,8,128]{2,1,0:T(8,128)S(1)}, f32[16,8,128]{2,1,0:T(8,128)S(1)}, u32[]{:S(2)}, u32[]{:S(2)}) collective-permute-start(f32[16,8,128]{2,1,0:T(8,128)S(1)} %get-tuple-element.104), channel_id=1, source_target_pairs={{0,1},{1,0},{2,3},{3,2},{4,5},{5,4},{6,7},{7,6},{8,9},{9,8},{10,11... | collective-permute-start | bytes 196616 | tf_op jit(solution)/shard_map/ppermute | solution.py:479
  51.0 7.8 %collective-permute-start.15 = (f32[16,8,128]{2,1,0:T(8,128)S(1)}, f32[16,8,128]{2,1,0:T(8,128)S(1)}, u32[]{:S(2)}, u32[]{:S(2)}) collective-permute-start(f32[16,8,128]{2,1,0:T(8,128)S(1)} %get-tuple-element.110), channel_id=1, source_target_pairs={{0,1},{1,0},{2,3},{3,2},{4,5},{5,4},{6,7},{7,6},{8,9},{9,8},{10,11... | collective-permute-start | bytes 196616 | tf_op jit(solution)/shard_map/ppermute | solution.py:479
  51.6 8.7 %collective-permute-start.16 = (f32[16,8,128]{2,1,0:T(8,128)S(1)}, f32[16,8,128]{2,1,0:T(8,128)S(1)}, u32[]{:S(2)}, u32[]{:S(2)}) collective-permute-start(f32[16,8,128]{2,1,0:T(8,128)S(1)} %get-tuple-element.111), channel_id=1, source_target_pairs={{0,2},{1,3},{2,0},{3,1},{4,6},{5,7},{6,4},{7,5},{8,10},{9,11},{10,... | collective-permute-start | bytes 196616 | tf_op jit(solution)/shard_map/ppermute | solution.py:479
  53.1 7.3 %collective-permute-start.17 = (f32[16,8,128]{2,1,0:T(8,128)S(1)}, f32[16,8,128]{2,1,0:T(8,128)S(1)}, u32[]{:S(2)}, u32[]{:S(2)}) collective-permute-start(f32[16,8,128]{2,1,0:T(8,128)S(1)} %get-tuple-element.112), channel_id=1, source_target_pairs={{0,3},{1,2},{2,1},{3,0},{4,7},{5,6},{6,5},{7,4},{8,11},{9,10},{10,... | collective-permute-start | bytes 196616 | tf_op jit(solution)/shard_map/ppermute | solution.py:479
  53.2 12.5 %collective-permute-start.34 = (f32[33,8,128]{2,1,0:T(8,128)S(1)}, f32[33,8,128]{2,1,0:T(8,128)S(1)}, u32[]{:S(2)}, u32[]{:S(2)}) collective-permute-start(f32[33,8,128]{2,1,0:T(8,128)S(1)} %get-tuple-element.150), channel_id=1, source_target_pairs={{0,4},{1,5},{2,6},{3,7},{4,0},{5,1},{6,2},{7,3},{8,12},{9,13},{10,... | collective-permute-start | bytes 405512 | tf_op jit(solution)/shard_map/ppermute | solution.py:479
  57.1 13.0 %collective-permute-start.35 = (f32[33,8,128]{2,1,0:T(8,128)S(1)}, f32[33,8,128]{2,1,0:T(8,128)S(1)}, u32[]{:S(2)}, u32[]{:S(2)}) collective-permute-start(f32[33,8,128]{2,1,0:T(8,128)S(1)} %get-tuple-element.151), channel_id=1, source_target_pairs={{0,8},{1,9},{2,10},{3,11},{4,12},{5,13},{6,14},{7,15},{8,0},{9,1},... | collective-permute-start | bytes 405512 | tf_op jit(solution)/shard_map/ppermute | solution.py:479
  58.8 11.8 %collective-permute-start.33 = (f32[33,8,128]{2,1,0:T(8,128)S(1)}, f32[33,8,128]{2,1,0:T(8,128)S(1)}, u32[]{:S(2)}, u32[]{:S(2)}) collective-permute-start(f32[33,8,128]{2,1,0:T(8,128)S(1)} %get-tuple-element.148), channel_id=1, source_target_pairs={{0,12},{1,13},{2,14},{3,15},{4,8},{5,9},{6,10},{7,11},{8,4},{9,5},... | collective-permute-start | bytes 405512 | tf_op jit(solution)/shard_map/ppermute | solution.py:479
  60.2 4.6 %collective-permute-start.12 = (f32[16,8,128]{2,1,0:T(8,128)S(1)}, f32[16,8,128]{2,1,0:T(8,128)S(1)}, u32[]{:S(2)}, u32[]{:S(2)}) collective-permute-start(f32[16,8,128]{2,1,0:T(8,128)S(1)} %get-tuple-element.105), channel_id=1, source_target_pairs={{0,2},{1,3},{2,0},{3,1},{4,6},{5,7},{6,4},{7,5},{8,10},{9,11},{10,... | collective-permute-start | bytes 196616 | tf_op jit(solution)/shard_map/ppermute | solution.py:479
  60.4 4.4 %collective-permute-start.13 = (f32[16,8,128]{2,1,0:T(8,128)S(1)}, f32[16,8,128]{2,1,0:T(8,128)S(1)}, u32[]{:S(2)}, u32[]{:S(2)}) collective-permute-start(f32[16,8,128]{2,1,0:T(8,128)S(1)} %get-tuple-element.106), channel_id=1, source_target_pairs={{0,3},{1,2},{2,1},{3,0},{4,7},{5,6},{6,5},{7,4},{8,11},{9,10},{10,... | collective-permute-start | bytes 196616 | tf_op jit(solution)/shard_map/ppermute | solution.py:479
